TPU v7x, 32 devices: a whole 2x2x4 slice. The times are simulated.
32 devices in a mesh: query: 4 (over y, x), cand: 2 (over core), tensor: 4 (over z).
Axes of the slice: x: 2, y: 2, z: 4, core: 2. Of those that a mesh axis runs over, the one named last changes fastest.
Arguments:
- cand_states: bfloat16 [8192, 2048], P(('query', 'cand'), 'tensor'), parts along dimension 0, may hold values from -6 to 6
- prefix_states: bfloat16 [256, 2048], P(('query', 'cand'), 'tensor'), parts along dimension 0, may hold values from -6 to 6
- norm_gain: float32 [2048], replicated, may hold values from 0.5 to 1.5
- w_query: bfloat16 [2048, 1024], P(None, 'tensor'), may hold values from -1 to 1
- w_key: bfloat16 [2048, 256], P(None, 'tensor'), may hold values from -1 to 1
- w_value: bfloat16 [2048, 256], P(None, 'tensor'), may hold values from -0.125 to 0.125
- w_out: bfloat16 [1024, 2048], P('tensor'), may hold values from -1.5 to 1.5
- cand_lengths: int32 [64], P(('query', 'cand')), parts along dimension 0, may hold values from 32 to 128, as said below
Outputs:
- attn_out: bfloat16 [8192, 2048], P(('query', 'cand', 'tensor')), parts along dimension 0
There are 4 independent parts, one for each index of `query`. A program takes and returns all parts, laid end to end along the dimension named above; an argument that names none is the same for every part. Nothing has to cross between parts.
Inputs may be any that keep to these rules, and one draw needn't show every extreme that they name: `cand_lengths`: some candidate has all 128 slots live.
All inputs are finite; a program needn't handle non-finite values.
Results may differ from a plain program's by a relative error of at most 0.013.
Values may be sent and summed in bfloat16 or wider, within the bound.
No kernel may reach another device: no remote copies, remote signals or barrier semaphores. Data moves between devices by JAX's collectives and lax.ppermute only.
A program may use at most 64 MiB of HBM per device.

v0:
```python
import functools

import jax
import jax.numpy as jnp
from jax import lax
from jax.experimental import pallas as pl
from jax.experimental.pallas import tpu as pltpu
from jax.sharding import PartitionSpec as P


epsilon = 1e-06
theta_base = 10000.0
PLANE = ("query", "cand")


def shift(k):
    n = lax.axis_size("tensor")
    return lambda v: lax.ppermute(v, "tensor", [(i, (i + k) % n) for i in range(n)])


def other_core(v):
    n = lax.axis_size("cand")
    return lax.ppermute(v, "cand", [(i, i ^ 1) for i in range(n)])


def plane_xor(masks):
    nq, nc = lax.axis_size("query"), lax.axis_size("cand")
    pairs = [(q * nc + c, (q ^ masks[c % 2]) * nc + c) for q in range(nq) for c in range(nc)]
    return lambda v: lax.ppermute(v, PLANE, pairs)


def spread(whole, piece):
    bits = lax.axis_size("query").bit_length() - 1
    held = [(piece, (0, 0))]
    for step in range(bits):
        flip = (1 << step, 1 << ((step + 1) % bits))
        held = held + [
            (
                plane_xor(flip)(v),
                (masks[0] ^ flip[0], masks[1] ^ flip[1]),
            )
            for v, masks in held
        ]
    held[0] = (whole, held[0][1])
    crossed = [(other_core(v), (masks[1], masks[0]), 1) for v, masks in held]
    return [(v, masks, 0) for v, masks in held] + crossed


def nearest(n):
    hops = [1] + [n - 1] * (n > 2) + list(range(2, n - 1))
    return [tuple((t - k) % n for t in range(n)) for k in hops]


def pick_kernel(choice, count, *refs):
    in_refs, o_refs = refs[:count], refs[count:]
    me = lax.axis_index("tensor")
    for i, ref in enumerate(in_refs):
        wanted = functools.reduce(
            jnp.logical_or, [me == t for t, which in enumerate(choice) if which == i]
        )

        @pl.when(wanted)
        def _(ref=ref):
            for o in o_refs:
                o[...] = ref[: o.shape[0], :]


def pick(by_place, heights, whole=None):
    distinct = []
    for v in by_place:
        if not any(v is d for d in distinct):
            distinct.append(v)
    choice = [next(i for i, d in enumerate(distinct) if d is v) for v in by_place]
    width = distinct[0].shape[1]
    made = pl.pallas_call(
        functools.partial(pick_kernel, choice, len(distinct)),
        out_shape=[jax.ShapeDtypeStruct((h, width), distinct[0].dtype) for h in heights],
        in_specs=[pl.BlockSpec(memory_space=pltpu.VMEM)] * len(distinct),
        out_specs=[pl.BlockSpec(memory_space=pltpu.VMEM)] * len(heights),
        compiler_params=pltpu.CompilerParams(vmem_limit_bytes=4 * 2**20),
    )(*distinct)
    return made if whole is None else [whole] + list(made)


def along_line(piece, height):
    n = lax.axis_size("tensor")
    came = {1: shift(1)(piece)}
    if n > 2:
        came[n - 1] = shift(n - 1)(piece)
    for k in range(2, n - 1):
        came[k] = shift(1)(came[k - 1])
    hops = [1] + [n - 1] * (n > 2) + list(range(2, n - 1))
    return [pick([came[k]] * n, (height,), came[k]) for k in hops]


def prefix_blocks(row, parity, prefix_rows, prefix_len, width, size):
    if 2 * prefix_rows == prefix_len:
        return [
            (row + i * prefix_rows, prefix_rows, parity * prefix_rows, i * size)
            for i in range(width // size)
        ]
    return [(row, prefix_len, 0, parity * size)]


def cut_kernel(dims, q_ref, out_ref, k_ref, v_ref, p_ref, o_ref, sems):
    prefix_rows, prefix_len, width = dims
    size, head = o_ref.shape[1], out_ref.shape[0]
    share = k_ref.shape[0]
    parity = lax.rem(lax.axis_index("cand"), 2)
    part = (lax.axis_index("query") * 2 + parity) * size
    at = pl.ds(pl.multiple_of(part, size), size)
    copies = []

    def copy(src, row, count):
        copies.append(
            pltpu.make_async_copy(src, o_ref.at[pl.ds(row, count), :], sems.at[len(copies)])
        )

    half, half_head = size // 2, head // 2
    for i in range(2):
        copy(q_ref.at[pl.ds(pl.multiple_of(part + i * half, half), half), :], i * half, half)
        copy(out_ref.at[pl.ds(i * half_head, half_head), at], size + i * half_head, half_head)
    copy(k_ref.at[:, at], size + head, share)
    copy(v_ref.at[:, at], size + head + share, share)
    blocks = prefix_blocks(size + head + 2 * share, parity, prefix_rows, prefix_len, width, size)
    for row, count, start, lane in blocks:
        if 2 * prefix_rows == prefix_len:
            start = 0
        lanes = pl.ds(pl.multiple_of(lane, size), size)
        copy(p_ref.at[pl.ds(start, count), lanes], row, count)
    for c in copies:
        c.start()
    for c in copies:
        c.wait()


def rotary_tables(count, half, head_size):
    frequency = theta_base ** (-jnp.arange(half, dtype=jnp.float32) * 2.0 / head_size)
    angles = jnp.arange(count, dtype=jnp.float32)[:, None] * frequency[None, :]
    return jnp.cos(angles), jnp.sin(angles)


def kernel(dims, rounds, plan, *refs):
    n, rows, cand_len, prefix_rows, prefix_len, depth, head, _ = dims
    n_pieces = len(plan)
    n_in = 11 + (n - 1) + (n - 1) * n_pieces
    cand_ref, gain_ref, cos_ref, sin_ref, len_ref = refs[:5]
    prefix_refs = refs[5:7]
    own_q, own_out, own_k, own_v = refs[7:11]
    x_refs = refs[11 : 11 + n - 1]
    piece_refs = refs[11 + n - 1 : n_in]
    o_ref = refs[n_in]
    x_own, w_query, w_out, w_kv, p_raw, normed, kv_scr, q_scr, heads, sems = refs[n_in + 1 :]
    me = lax.axis_index("tensor")
    q_at = lax.axis_index("query")
    parity = lax.rem(lax.axis_index("cand"), 2)
    width = depth // n
    half = head // 2
    share = own_k.shape[0]
    size = w_query.shape[1]
    chunks = width // size

    def rows_of(start, size):
        return pl.ds(pl.multiple_of(start, size), size)

    def table(places):
        value = places[0]
        for t in range(1, n):
            value = jnp.where(me == t, places[t], value)
        return value

    moves = [
        (cand_ref.at[rows_of(me * rows, rows), :], x_own),
        (own_k, w_kv.at[pl.ds(0, share), :]),
        (own_v, w_kv.at[pl.ds(share, share), :]),
        (own_q, w_query),
        (own_out, w_out),
    ]
    copies = [pltpu.make_async_copy(src, dst, sems.at[i]) for i, (src, dst) in enumerate(moves)]
    for c in copies:
        c.start()

    sources = [me] + [table(places) for places in rounds]
    pieces = [piece_refs[r * n_pieces : (r + 1) * n_pieces] for r in range(n - 1)]
    parts = []
    for masks, crossed in plan:
        mask = jnp.where(parity == 0, masks[0], masks[1])
        parts.append(lax.bitwise_xor(q_at, mask) * 2 + (parity if not crossed else 1 - parity))

    fixed = size + head + 2 * share
    prefix_in = [prefix_refs] + [(p[0], p[n_pieces // 2]) for p in pieces]
    for source, both in zip(sources, prefix_in):
        for ref, side in zip(both, (parity, 1 - parity)):
            for at, count, start, lane in prefix_blocks(
                fixed, side, prefix_rows, prefix_len, width, size
            ):
                to = rows_of(start, count) if 2 * prefix_rows == prefix_len else pl.ds(start, count)
                p_raw[source * chunks + lane // size, to, :] = ref[pl.ds(at, count), :]

    block = 32

    def normalise(parts_in, to_rows):
        values = [v.astype(jnp.float32) for _, v in parts_in]
        square = sum(jnp.sum(v * v, axis=-1, keepdims=True) for v in values) / depth
        scale = lax.rsqrt(square + epsilon)
        for (chunk, _), v in zip(parts_in, values):
            normed[chunk, to_rows, :] = (v * scale * gain_ref[chunk]).astype(jnp.bfloat16)

    @pl.loop(0, prefix_len // block)
    def _(i):
        at = rows_of(i * block, block)
        to = pl.ds(pl.multiple_of(rows + i * block, block), block)
        normalise([(c, p_raw[c, at, :]) for c in range(n * chunks)], to)

    copies[0].wait()
    x_all = [x_own] + list(x_refs)
    x_from = [me] + [lax.rem(me - k + n, n) for k in range(1, n)]

    @pl.loop(0, rows // block)
    def _(i):
        at = rows_of(i * block, block)
        normalise(
            [
                (source * chunks + h, ref[at, pl.ds(h * size, size)])
                for source, ref in zip(x_from, x_all)
                for h in range(chunks)
            ],
            at,
        )

    cos, sin = cos_ref[...], sin_ref[...]
    cand_cos = jnp.concatenate([cos[prefix_len:]] * (rows // cand_len), axis=0)
    cand_sin = jnp.concatenate([sin[prefix_len:]] * (rows // cand_len), axis=0)
    all_cos = jnp.concatenate([cand_cos, cos[:prefix_len]], axis=0)
    all_sin = jnp.concatenate([cand_sin, sin[:prefix_len]], axis=0)
    trans = (((1,), (1,)), ((), ()))

    copies[1].wait()
    copies[2].wait()
    made = None
    for i, part in enumerate(parts):
        weights = jnp.concatenate(
            [w_kv[:, rows_of(part * size, size)]]
            + [p[i][pl.ds(size + head, 2 * share), :] for p in pieces],
            axis=0,
        )
        term = lax.dot_general(normed[part], weights, trans, preferred_element_type=jnp.float32)
        made = term if made is None else made + term
    for k, source in enumerate(sources):
        kv_scr[source] = made[:, k * 2 * share : (k + 1) * 2 * share].astype(jnp.bfloat16)
    shares = [kv_scr[s] for s in range(n)]
    low = jnp.concatenate([p[:, :share] for p in shares[: n // 2]], axis=1).astype(jnp.float32)
    up = jnp.concatenate([p[:, :share] for p in shares[n // 2 :]], axis=1).astype(jnp.float32)
    keys = jnp.concatenate(
        [low * all_cos - up * all_sin, up * all_cos + low * all_sin], axis=1
    ).astype(jnp.bfloat16)
    values = jnp.concatenate([p[:, share:] for p in shares], axis=1)
    prefix_keys, prefix_values = keys[rows:], values[rows:]

    scale = head ** (-0.5)
    for k in range(n - 1, -1, -1):
        if k == 0:
            copies[3].wait()
        made = None
        for i, part in enumerate(parts):
            if k == 0:
                weights = w_query[rows_of(part * size, size), :]
            else:
                weights = pieces[k - 1][i][pl.ds(0, size), :]
            term = jnp.dot(
                normed[part, pl.ds(0, rows), :], weights, preferred_element_type=jnp.float32
            )
            made = term if made is None else made + term
        lower, upper = made[:, :half], made[:, half:]
        q_scr[k, :, :half] = ((lower * cand_cos - upper * cand_sin) * scale).astype(jnp.bfloat16)
        q_scr[k, :, half:] = ((upper * cand_cos + lower * cand_sin) * scale).astype(jnp.bfloat16)

    tall = (n, cand_len, cand_len + prefix_len)
    slot = lax.broadcasted_iota(jnp.int32, tall, 1).reshape(n * cand_len, tall[2])
    other = lax.broadcasted_iota(jnp.int32, tall, 2).reshape(n * cand_len, tall[2])
    seen = (slot >= other) | (other >= cand_len)
    for j in range(rows // cand_len):
        own = slice(j * cand_len, (j + 1) * cand_len)
        live = slot[:, :1] < len_ref[me * (rows // cand_len) + j]
        keys_j = jnp.concatenate([keys[own], prefix_keys], axis=0)
        values_j = jnp.concatenate([values[own], prefix_values], axis=0)
        queries = jnp.concatenate([q_scr[k, own, :] for k in range(n)], axis=0)
        scores = lax.dot_general(queries, keys_j, trans, preferred_element_type=jnp.float32)
        scores = jnp.where(seen, scores, -jnp.inf)
        weights = jnp.exp(scores - scores.max(-1, keepdims=True))
        divisor = weights.sum(-1, keepdims=True)
        mix = jnp.dot(weights.astype(jnp.bfloat16), values_j, preferred_element_type=jnp.float32)
        mix = jnp.where(live, mix / divisor, 0.0).astype(jnp.bfloat16)
        for k in range(n):
            heads[k, own, :] = mix[k * cand_len : (k + 1) * cand_len]

    copies[4].wait()
    for i, part in enumerate(parts):
        spot = rows_of(part * size, size)
        total = None
        for k in range(n):
            weights = w_out[:, spot] if k == 0 else pieces[k - 1][i][pl.ds(size, head), :]
            term = jnp.dot(heads[k], weights, preferred_element_type=jnp.float32)
            term = term.astype(jnp.bfloat16).astype(jnp.float32)
            total = term if total is None else total + term
        o_ref[:, spot] = total.astype(jnp.bfloat16)


def body(cand_states, prefix_states, norm_gain, w_query, w_key, w_value, w_out, cand_lengths):
    n = lax.axis_size("tensor")
    nq, nc = lax.axis_size("query"), lax.axis_size("cand")
    me = lax.axis_index("tensor")
    depth, head = w_query.shape
    share = w_key.shape[1]
    out_cols = w_out.shape[1]
    size = depth // (2 * nq)
    cand_len = cand_states.shape[0] // cand_lengths.shape[0]
    rows = cand_states.shape[0] // n
    prefix_len = prefix_states.shape[0] * nc
    half = head // 2
    any_spec = pl.BlockSpec(memory_space=pl.ANY)
    hbm = pl.BlockSpec(memory_space=pltpu.HBM)
    vmem = pl.BlockSpec(memory_space=pltpu.VMEM)
    smem = pl.BlockSpec(memory_space=pltpu.SMEM)

    key_t, value_t = w_key.T, w_value.T
    prefix_rows = prefix_states.shape[0]
    near = prefix_states
    if 2 * prefix_rows != prefix_len:
        near = lax.all_gather(prefix_states, "cand", axis=0, tiled=True)
    height = size + head + 2 * share
    tail = prefix_rows * (cand_states.shape[1] // size) if near is prefix_states else prefix_len
    piece = pl.pallas_call(
        functools.partial(cut_kernel, (prefix_rows, prefix_len, cand_states.shape[1])),
        name="cut",
        out_shape=jax.ShapeDtypeStruct((height + tail, size), jnp.bfloat16),
        in_specs=[any_spec] * 5,
        out_specs=vmem,
        scratch_shapes=[pltpu.SemaphoreType.DMA((8,))],
        compiler_params=pltpu.CompilerParams(vmem_limit_bytes=60 * 2**20),
    )(w_query, w_out, key_t, value_t, near)
    moved = along_line(piece, height)
    xs = [
        shift(k)(lax.dynamic_slice_in_dim(cand_states, (me + k) % n * rows, rows, 0))
        for k in range(1, n)
    ]
    across = other_core(piece)
    spreads = [spread(whole, v) for whole, v in moved]
    plan = tuple((masks, crossed) for _, masks, crossed in spreads[0])
    pieces = [v for s in spreads for v, _, _ in s]
    cos, sin = rotary_tables(prefix_len + cand_len, half, head)

    dims = (n, rows, cand_len, prefix_rows, prefix_len, depth, head, out_cols)
    return pl.pallas_call(
        functools.partial(kernel, dims, nearest(n), plan),
        name="main",
        out_shape=jax.ShapeDtypeStruct((rows, out_cols), jnp.bfloat16),
        in_specs=[hbm, vmem, vmem, vmem, smem]
        + [vmem] * 2
        + [hbm] * 4
        + [vmem] * (len(xs) + len(pieces)),
        out_specs=vmem,
        scratch_shapes=[
            pltpu.VMEM((rows, depth // n), jnp.bfloat16),
            pltpu.VMEM((depth, head), jnp.bfloat16),
            pltpu.VMEM((head, out_cols), jnp.bfloat16),
            pltpu.VMEM((2 * share, depth), jnp.bfloat16),
            pltpu.VMEM((depth // size, prefix_len, size), jnp.bfloat16),
            pltpu.VMEM((depth // size, rows + prefix_len, size), jnp.bfloat16),
            pltpu.VMEM((n, rows + prefix_len, 2 * share), jnp.bfloat16),
            pltpu.VMEM((n, rows, head), jnp.bfloat16),
            pltpu.VMEM((n, rows, head), jnp.bfloat16),
            pltpu.SemaphoreType.DMA((5,)),
        ],
        compiler_params=pltpu.CompilerParams(vmem_limit_bytes=32 * 2**20),
    )(
        cand_states, norm_gain.reshape(depth // size, 1, size), cos, sin, cand_lengths,
        piece, across, w_query, w_out, key_t, value_t, *xs, *pieces,
    )


def solution(mesh):
    in_specs = (
        P(("query", "cand"), "tensor"),
        P(("query", "cand"), "tensor"),
        P(),
        P(None, "tensor"),
        P(None, "tensor"),
        P(None, "tensor"),
        P("tensor", None),
        P(("query", "cand")),
    )
    out_specs = P(("query", "cand", "tensor"), None)

    return jax.shard_map(body, mesh=mesh, in_specs=in_specs, out_specs=out_specs, check_vma=False)
```

profile of v0, /device:TPU:0, one launch (start us, length us, event | category | flops | bytes accessed | tf_op | source)
XLA Modules:
  0.0 91.7 jit_solution(530470902423324519)
XLA Ops:
  0.0 1.8 %cut.1.refs_5_ = bf16[704,256]{1,0:T(8,128)(2,1)} custom-call(bf16[2048,256]{1,0:T(8,128)(2,1)} %refs_7_.1, bf16[256,2048]{1,0:T(8,128)(2,1)} %refs_8_.1, bf16[64,2048]{1,0:T(8,128)(2,1)} %bitcast.3, bf16[64,2048]{1,0:T(8,128)(2,1)} %bitcast.5, bf16[32,512]{1,0:T(8,128)(2,1)} %p_ref.1), custom_call_target="tpu_custom_call" | custom-call | tf_op jit(solution)/shard_map/cut/pallas_call | solution.py:333
  1.8 5.1 %collective-permute-start.12 = (bf16[704,256]{1,0:T(8,128)(2,1)}, bf16[704,256]{1,0:T(8,128)(2,1)S(1)}, u32[]{:S(2)}, u32[]{:S(2)}) collective-permute-start(bf16[704,256]{1,0:T(8,128)(2,1)} %cut.1.refs_5_), channel_id=1, source_target_pairs={{0,3},{1,0},{2,1},{3,2},{4,7},{5,4},{6,5},{7,6},{8,11},{9,8},{10,9... | collective-permute-start | bytes 1081352 | tf_op jit(solution)/shard_map/ppermute | solution.py:18
  7.0 0.0 collective-permute-start.4
  7.0 0.0 copy-start.5
  7.0 0.1 constant_dynamic-slice_fusion
  7.1 0.0 copy-start
  7.1 0.0 copy-start.1
  7.1 3.9 %collective-permute-start.3 = (bf16[256,512]{1,0:T(8,128)(2,1)S(1)}, bf16[256,512]{1,0:T(8,128)(2,1)S(1)}, u32[]{:S(2)}, u32[]{:S(2)}) collective-permute-start(bf16[256,512]{1,0:T(8,128)(2,1)S(1)} %get-tuple-element.5), channel_id=1, source_target_pairs={{0,3},{1,0},{2,1},{3,2},{4,7},{5,4},{6,5},{7,6},{8,11},{9,8},{10,9... | collective-permute-start | bytes 786440 | tf_op jit(solution)/shard_map/ppermute | solution.py:18
  11.0 0.0 collective-permute-start
  11.0 5.1 %collective-permute-done.12.refs_0_.refs_22_ = bf16[704,256]{1,0:T(8,128)(2,1)S(1)} collective-permute-done((bf16[704,256]{1,0:T(8,128)(2,1)}, bf16[704,256]{1,0:T(8,128)(2,1)S(1)}, u32[]{:S(2)}, u32[]{:S(2)}) %collective-permute-start.12) | collective-permute-done | bytes 360480 | tf_op jit(solution)/shard_map/ppermute | solution.py:18
  16.1 1.6 %collective-permute-start.14 = (bf16[640,256]{1,0:T(8,128)(2,1)S(1)}, bf16[640,256]{1,0:T(8,128)(2,1)S(1)}, u32[]{:S(2)}, u32[]{:S(2)}) collective-permute-start(bf16[640,256]{1,0:T(8,128)(2,1)S(1)} %shard_map.83), channel_id=1, source_target_pairs={{0,16},{4,12},{8,24},{12,4},{16,0},{20,28},{24,8},{28,20},{1,17},{... | collective-permute-start | bytes 983048 | tf_op jit(solution)/shard_map/ppermute | solution.py:29
  17.7 1.5 %collective-permute-start.13 = (bf16[640,256]{1,0:T(8,128)(2,1)S(1)}, bf16[640,256]{1,0:T(8,128)(2,1)S(1)}, u32[]{:S(2)}, u32[]{:S(2)}) collective-permute-start(bf16[640,256]{1,0:T(8,128)(2,1)S(1)} %shard_map.83), channel_id=1, source_target_pairs={{0,8},{4,20},{8,0},{12,28},{16,24},{20,4},{24,16},{28,12},{1,9},{5... | collective-permute-start | bytes 983048 | tf_op jit(solution)/shard_map/ppermute | solution.py:29
  19.2 9.0 %collective-permute-done.3.refs_13_ = bf16[256,512]{1,0:T(8,128)(2,1)S(1)} collective-permute-done((bf16[256,512]{1,0:T(8,128)(2,1)S(1)}, bf16[256,512]{1,0:T(8,128)(2,1)S(1)}, u32[]{:S(2)}, u32[]{:S(2)}) %collective-permute-start.3) | collective-permute-done | bytes 262176 | tf_op jit(solution)/shard_map/ppermute | solution.py:18
  28.2 1.5 %collective-permute-start.2 = (bf16[256,512]{1,0:T(8,128)(2,1)S(1)}, bf16[256,512]{1,0:T(8,128)(2,1)S(1)}, u32[]{:S(2)}, u32[]{:S(2)}) collective-permute-start(bf16[256,512]{1,0:T(8,128)(2,1)S(1)} %get-tuple-element.6), channel_id=1, source_target_pairs={{0,2},{1,3},{2,0},{3,1},{4,6},{5,7},{6,4},{7,5},{8,10},{9,11},{10,... | collective-permute-start | bytes 786440 | tf_op jit(solution)/shard_map/ppermute | solution.py:18
  29.7 0.0 collective-permute-done.4.refs_0_.refs_14_
  29.7 3.4 %collective-permute-start.1 = (bf16[256,512]{1,0:T(8,128)(2,1)S(1)}, bf16[256,512]{1,0:T(8,128)(2,1)S(1)}, u32[]{:S(2)}, u32[]{:S(2)}) collective-permute-start(bf16[256,512]{1,0:T(8,128)(2,1)S(1)} %get-tuple-element.7), channel_id=1, source_target_pairs={{0,1},{1,2},{2,3},{3,0},{4,5},{5,6},{6,7},{7,4},{8,9},{9,10},{10,1... | collective-permute-start | bytes 786440 | tf_op jit(solution)/shard_map/ppermute | solution.py:18
  33.1 14.5 %collective-permute-done.2.refs_12_ = bf16[256,512]{1,0:T(8,128)(2,1)S(1)} collective-permute-done((bf16[256,512]{1,0:T(8,128)(2,1)S(1)}, bf16[256,512]{1,0:T(8,128)(2,1)S(1)}, u32[]{:S(2)}, u32[]{:S(2)}) %collective-permute-start.2) | collective-permute-done | bytes 262176 | tf_op jit(solution)/shard_map/ppermute | solution.py:18
  47.6 0.0 collective-permute-start.20
  47.6 0.0 collective-permute-done.refs_6_
  47.6 1.6 %collective-permute-start.6 = (bf16[640,256]{1,0:T(8,128)(2,1)S(1)}, bf16[640,256]{1,0:T(8,128)(2,1)S(1)}, u32[]{:S(2)}, u32[]{:S(2)}) collective-permute-start(bf16[640,256]{1,0:T(8,128)(2,1)S(1)} %shard_map.82), channel_id=1, source_target_pairs={{0,16},{4,12},{8,24},{12,4},{16,0},{20,28},{24,8},{28,20},{1,17},{... | collective-permute-start | bytes 983048 | tf_op jit(solution)/shard_map/ppermute | solution.py:29
  49.2 0.2 collective-permute-start.8
  49.4 1.4 %collective-permute-start.5 = (bf16[640,256]{1,0:T(8,128)(2,1)S(1)}, bf16[640,256]{1,0:T(8,128)(2,1)S(1)}, u32[]{:S(2)}, u32[]{:S(2)}) collective-permute-start(bf16[640,256]{1,0:T(8,128)(2,1)S(1)} %shard_map.82), channel_id=1, source_target_pairs={{0,8},{4,20},{8,0},{12,28},{16,24},{20,4},{24,16},{28,12},{1,9},{5... | collective-permute-start | bytes 983048 | tf_op jit(solution)/shard_map/ppermute | solution.py:29
  50.8 6.4 %collective-permute-done.6.refs_16_ = bf16[640,256]{1,0:T(8,128)(2,1)S(1)} collective-permute-done((bf16[640,256]{1,0:T(8,128)(2,1)S(1)}, bf16[640,256]{1,0:T(8,128)(2,1)S(1)}, u32[]{:S(2)}, u32[]{:S(2)}) %collective-permute-start.6) | collective-permute-done | bytes 327712 | tf_op jit(solution)/shard_map/ppermute | solution.py:29
  57.2 0.0 collective-permute-start.18
  57.2 0.6 collective-permute-done.5.refs_15_
  57.8 0.6 collective-permute-start.17
  58.4 1.5 %collective-permute-start.15 = (bf16[640,256]{1,0:T(8,128)(2,1)S(1)}, bf16[640,256]{1,0:T(8,128)(2,1)S(1)}, u32[]{:S(2)}, u32[]{:S(2)}) collective-permute-start(bf16[640,256]{1,0:T(8,128)(2,1)S(1)} %collective-permute-done.13.refs_23_), channel_id=1, source_target_pairs={{0,16},{4,12},{8,24},{12,4},{16,0},{20,28},{24,8},{28,20},{1,17},{... | collective-permute-start | bytes 983048 | tf_op jit(solution)/shard_map/ppermute | solution.py:29
  59.9 0.3 collective-permute-done.20.refs_0_.refs_30_
  60.2 0.0 collective-permute-start.10
  60.3 0.0 collective-permute-done.8.refs_18_
  60.3 1.6 %collective-permute-start.21 = (bf16[640,256]{1,0:T(8,128)(2,1)S(1)}, bf16[640,256]{1,0:T(8,128)(2,1)S(1)}, u32[]{:S(2)}, u32[]{:S(2)}) collective-permute-start(bf16[640,256]{1,0:T(8,128)(2,1)S(1)} %shard_map.84), channel_id=1, source_target_pairs={{0,8},{4,20},{8,0},{12,28},{16,24},{20,4},{24,16},{28,12},{1,9},{5... | collective-permute-start | bytes 983048 | tf_op jit(solution)/shard_map/ppermute | solution.py:29
  61.9 0.0 collective-permute-done.18.refs_28_
  61.9 0.2 collective-permute-start.24
  62.1 0.3 collective-permute-start.9
  62.4 5.1 %collective-permute-done.15.refs_25_ = bf16[640,256]{1,0:T(8,128)(2,1)S(1)} collective-permute-done((bf16[640,256]{1,0:T(8,128)(2,1)S(1)}, bf16[640,256]{1,0:T(8,128)(2,1)S(1)}, u32[]{:S(2)}, u32[]{:S(2)}) %collective-permute-start.15) | collective-permute-done | bytes 327712 | tf_op jit(solution)/shard_map/ppermute | solution.py:29
  67.5 1.5 %collective-permute-start.7 = (bf16[640,256]{1,0:T(8,128)(2,1)S(1)}, bf16[640,256]{1,0:T(8,128)(2,1)S(1)}, u32[]{:S(2)}, u32[]{:S(2)}) collective-permute-start(bf16[640,256]{1,0:T(8,128)(2,1)S(1)} %collective-permute-done.5.refs_15_), channel_id=1, source_target_pairs={{0,16},{4,12},{8,24},{12,4},{16,0},{20,28},{24,8},{28,20},{1,17},{... | collective-permute-start | bytes 983048 | tf_op jit(solution)/shard_map/ppermute | solution.py:29
  69.0 0.0 collective-permute-done.10.refs_20_
  69.0 0.5 collective-permute-start.22
  69.6 1.5 %collective-permute-start.23 = (bf16[640,256]{1,0:T(8,128)(2,1)S(1)}, bf16[640,256]{1,0:T(8,128)(2,1)S(1)}, u32[]{:S(2)}, u32[]{:S(2)}) collective-permute-start(bf16[640,256]{1,0:T(8,128)(2,1)S(1)} %collective-permute-done.21.refs_31_), channel_id=1, source_target_pairs={{0,16},{4,12},{8,24},{12,4},{16,0},{20,28},{24,8},{28,20},{1,17},{... | collective-permute-start | bytes 983048 | tf_op jit(solution)/shard_map/ppermute | solution.py:29
  71.1 3.5 %collective-permute-done.7.refs_17_ = bf16[640,256]{1,0:T(8,128)(2,1)S(1)} collective-permute-done((bf16[640,256]{1,0:T(8,128)(2,1)S(1)}, bf16[640,256]{1,0:T(8,128)(2,1)S(1)}, u32[]{:S(2)}, u32[]{:S(2)}) %collective-permute-start.7) | collective-permute-done | bytes 327712 | tf_op jit(solution)/shard_map/ppermute | solution.py:29
  74.6 3.5 %collective-permute-done.22.refs_32_ = bf16[640,256]{1,0:T(8,128)(2,1)S(1)} collective-permute-done((bf16[640,256]{1,0:T(8,128)(2,1)S(1)}, bf16[640,256]{1,0:T(8,128)(2,1)S(1)}, u32[]{:S(2)}, u32[]{:S(2)}) %collective-permute-start.22) | collective-permute-done | bytes 327712 | tf_op jit(solution)/shard_map/ppermute | solution.py:29
  78.1 0.5 collective-permute-start.26
  78.6 3.0 %collective-permute-done.23.refs_33_ = bf16[640,256]{1,0:T(8,128)(2,1)S(1)} collective-permute-done((bf16[640,256]{1,0:T(8,128)(2,1)S(1)}, bf16[640,256]{1,0:T(8,128)(2,1)S(1)}, u32[]{:S(2)}, u32[]{:S(2)}) %collective-permute-start.23) | collective-permute-done | bytes 327712 | tf_op jit(solution)/shard_map/ppermute | solution.py:29
  81.6 0.0 copy-start.6
  81.6 0.4 fusion
  82.1 1.2 %collective-permute-done.27.refs_37_ = bf16[640,256]{1,0:T(8,128)(2,1)S(1)} collective-permute-done((bf16[640,256]{1,0:T(8,128)(2,1)S(1)}, bf16[640,256]{1,0:T(8,128)(2,1)S(1)}, u32[]{:S(2)}, u32[]{:S(2)}) %collective-permute-start.27) | collective-permute-done | bytes 327712 | tf_op jit(solution)/shard_map/ppermute | solution.py:23
  83.3 0.6 copy-done.7
  83.9 7.8 %main.1 = bf16[256,2048]{1,0:T(8,128)(2,1)} custom-call(bf16[1024,512]{1,0:T(8,128)(2,1)S(1)} %copy-done.2, f32[8,1,256]{2,1,0:T(1,128)S(1)} %bitcast.7, f32[192,128]{1,0:T(8,128)S(1)} %get-tuple-element.9.refs_2_, f32[192,128]{1,0:T(8,128)S(1)} %get-tuple-element.8.refs_3_, s32[8]{0:T(128)S(1)} %copy-done.7, bf16[704,256]{1,0:T(8,128)(2,1)S(1)} %copy-done.3, ...), custom_call_target="tpu_custom_call" | custom-call | tf_op jit(solution)/shard_map/main/pallas_call | solution.py:354
  (32 shorter events, 0.1 us)
Async XLA Ops:
  0.0 7.0 %copy-start.2 = (bf16[1024,512]{1,0:T(8,128)(2,1)S(1)}, bf16[1024,512]{1,0:T(8,128)(2,1)}, u32[]{:S(2)}) copy-start(bf16[1024,512]{1,0:T(8,128)(2,1)} %refs_0_.1) | copy-start | bytes 3145732
  1.8 14.2 %collective-permute-start.12 = (bf16[704,256]{1,0:T(8,128)(2,1)}, bf16[704,256]{1,0:T(8,128)(2,1)S(1)}, u32[]{:S(2)}, u32[]{:S(2)}) collective-permute-start(bf16[704,256]{1,0:T(8,128)(2,1)} %cut.1.refs_5_), channel_id=1, source_target_pairs={{0,3},{1,0},{2,1},{3,2},{4,7},{5,4},{6,5},{7,6},{8,11},{9,8},{10,9... | collective-permute-start | bytes 1081352 | tf_op jit(solution)/shard_map/ppermute | solution.py:18
  7.0 22.7 %collective-permute-start.4 = (bf16[704,256]{1,0:T(8,128)(2,1)}, bf16[704,256]{1,0:T(8,128)(2,1)S(1)}, u32[]{:S(2)}, u32[]{:S(2)}) collective-permute-start(bf16[704,256]{1,0:T(8,128)(2,1)} %cut.1.refs_5_), channel_id=1, source_target_pairs={{0,1},{1,2},{2,3},{3,0},{4,5},{5,6},{6,7},{7,4},{8,9},{9,10},{10,1... | collective-permute-start | bytes 1081352 | tf_op jit(solution)/shard_map/ppermute | solution.py:18
  7.0 4.0 %copy-start.3 = (bf16[704,256]{1,0:T(8,128)(2,1)S(1)}, bf16[704,256]{1,0:T(8,128)(2,1)}, u32[]{:S(2)}) copy-start(bf16[704,256]{1,0:T(8,128)(2,1)} %cut.1.refs_5_) | copy-start | bytes 1081348
  7.0 76.3 %copy-start.4 = (bf16[2048,64]{0,1:T(8,128)(2,1)S(1)}, bf16[2048,64]{0,1:T(8,128)(2,1)}, u32[]{:S(2)}) copy-start(bf16[2048,64]{0,1:T(8,128)(2,1)} %param.12) | copy-start | bytes 786436
  7.0 76.3 %copy-start.5 = (bf16[2048,64]{0,1:T(8,128)(2,1)S(1)}, bf16[2048,64]{0,1:T(8,128)(2,1)}, u32[]{:S(2)}) copy-start(bf16[2048,64]{0,1:T(8,128)(2,1)} %param.13) | copy-start | bytes 786436
  7.1 76.2 %copy-start = (bf16[2048,256]{1,0:T(8,128)(2,1)S(1)}, bf16[2048,256]{1,0:T(8,128)(2,1)}, u32[]{:S(2)}) copy-start(bf16[2048,256]{1,0:T(8,128)(2,1)} %refs_7_.1) | copy-start | bytes 3145732
  7.1 76.2 %copy-start.1 = (bf16[256,2048]{1,0:T(8,128)(2,1)S(1)}, bf16[256,2048]{1,0:T(8,128)(2,1)}, u32[]{:S(2)}) copy-start(bf16[256,2048]{1,0:T(8,128)(2,1)} %refs_8_.1) | copy-start | bytes 3145732
  7.1 21.1 %collective-permute-start.3 = (bf16[256,512]{1,0:T(8,128)(2,1)S(1)}, bf16[256,512]{1,0:T(8,128)(2,1)S(1)}, u32[]{:S(2)}, u32[]{:S(2)}) collective-permute-start(bf16[256,512]{1,0:T(8,128)(2,1)S(1)} %get-tuple-element.5), channel_id=1, source_target_pairs={{0,3},{1,0},{2,1},{3,2},{4,7},{5,4},{6,5},{7,6},{8,11},{9,8},{10,9... | collective-permute-start | bytes 786440 | tf_op jit(solution)/shard_map/ppermute | solution.py:18
  11.0 36.7 %collective-permute-start = (bf16[704,256]{1,0:T(8,128)(2,1)S(1)}, bf16[704,256]{1,0:T(8,128)(2,1)S(1)}, u32[]{:S(2)}, u32[]{:S(2)}) collective-permute-start(bf16[704,256]{1,0:T(8,128)(2,1)S(1)} %copy-done.3), channel_id=1, source_target_pairs={{0,4},{4,0},{1,5},{5,1},{2,6},{6,2},{3,7},{7,3},{8,12},{12,8},{9,1... | collective-permute-start | bytes 1081352 | tf_op jit(solution)/shard_map/ppermute | solution.py:23
  16.1 33.1 %collective-permute-start.14 = (bf16[640,256]{1,0:T(8,128)(2,1)S(1)}, bf16[640,256]{1,0:T(8,128)(2,1)S(1)}, u32[]{:S(2)}, u32[]{:S(2)}) collective-permute-start(bf16[640,256]{1,0:T(8,128)(2,1)S(1)} %shard_map.83), channel_id=1, source_target_pairs={{0,16},{4,12},{8,24},{12,4},{16,0},{20,28},{24,8},{28,20},{1,17},{... | collective-permute-start | bytes 983048 | tf_op jit(solution)/shard_map/ppermute | solution.py:29
  17.7 31.7 %collective-permute-start.13 = (bf16[640,256]{1,0:T(8,128)(2,1)S(1)}, bf16[640,256]{1,0:T(8,128)(2,1)S(1)}, u32[]{:S(2)}, u32[]{:S(2)}) collective-permute-start(bf16[640,256]{1,0:T(8,128)(2,1)S(1)} %shard_map.83), channel_id=1, source_target_pairs={{0,8},{4,20},{8,0},{12,28},{16,24},{20,4},{24,16},{28,12},{1,9},{5... | collective-permute-start | bytes 983048 | tf_op jit(solution)/shard_map/ppermute | solution.py:29
  28.2 19.4 %collective-permute-start.2 = (bf16[256,512]{1,0:T(8,128)(2,1)S(1)}, bf16[256,512]{1,0:T(8,128)(2,1)S(1)}, u32[]{:S(2)}, u32[]{:S(2)}) collective-permute-start(bf16[256,512]{1,0:T(8,128)(2,1)S(1)} %get-tuple-element.6), channel_id=1, source_target_pairs={{0,2},{1,3},{2,0},{3,1},{4,6},{5,7},{6,4},{7,5},{8,10},{9,11},{10,... | collective-permute-start | bytes 786440 | tf_op jit(solution)/shard_map/ppermute | solution.py:18
  29.7 17.9 %collective-permute-start.1 = (bf16[256,512]{1,0:T(8,128)(2,1)S(1)}, bf16[256,512]{1,0:T(8,128)(2,1)S(1)}, u32[]{:S(2)}, u32[]{:S(2)}) collective-permute-start(bf16[256,512]{1,0:T(8,128)(2,1)S(1)} %get-tuple-element.7), channel_id=1, source_target_pairs={{0,1},{1,2},{2,3},{3,0},{4,5},{5,6},{6,7},{7,4},{8,9},{9,10},{10,1... | collective-permute-start | bytes 786440 | tf_op jit(solution)/shard_map/ppermute | solution.py:18
  47.6 10.8 %collective-permute-start.16 = (bf16[704,256]{1,0:T(8,128)(2,1)S(1)}, bf16[704,256]{1,0:T(8,128)(2,1)S(1)}, u32[]{:S(2)}, u32[]{:S(2)}) collective-permute-start(bf16[704,256]{1,0:T(8,128)(2,1)S(1)} %collective-permute-done.12.refs_0_.refs_22_), channel_id=1, source_target_pairs={{0,4},{4,0},{1,5},{5,1},{2,6},{6,2},{3,7},{7,3},{8,12},{12,8},{9,1... | collective-permute-start | bytes 1081352 | tf_op jit(solution)/shard_map/ppermute | solution.py:23
  47.6 12.6 %collective-permute-start.20 = (bf16[704,256]{1,0:T(8,128)(2,1)S(1)}, bf16[704,256]{1,0:T(8,128)(2,1)S(1)}, u32[]{:S(2)}, u32[]{:S(2)}) collective-permute-start(bf16[704,256]{1,0:T(8,128)(2,1)S(1)} %collective-permute-done.4.refs_0_.refs_14_), channel_id=1, source_target_pairs={{0,1},{1,2},{2,3},{3,0},{4,5},{5,6},{6,7},{7,4},{8,9},{9,10},{10,1... | collective-permute-start | bytes 1081352 | tf_op jit(solution)/shard_map/ppermute | solution.py:18
  47.6 9.6 %collective-permute-start.6 = (bf16[640,256]{1,0:T(8,128)(2,1)S(1)}, bf16[640,256]{1,0:T(8,128)(2,1)S(1)}, u32[]{:S(2)}, u32[]{:S(2)}) collective-permute-start(bf16[640,256]{1,0:T(8,128)(2,1)S(1)} %shard_map.82), channel_id=1, source_target_pairs={{0,16},{4,12},{8,24},{12,4},{16,0},{20,28},{24,8},{28,20},{1,17},{... | collective-permute-start | bytes 983048 | tf_op jit(solution)/shard_map/ppermute | solution.py:29
  49.2 11.0 %collective-permute-start.8 = (bf16[704,256]{1,0:T(8,128)(2,1)S(1)}, bf16[704,256]{1,0:T(8,128)(2,1)S(1)}, u32[]{:S(2)}, u32[]{:S(2)}) collective-permute-start(bf16[704,256]{1,0:T(8,128)(2,1)S(1)} %collective-permute-done.4.refs_0_.refs_14_), channel_id=1, source_target_pairs={{0,4},{4,0},{1,5},{5,1},{2,6},{6,2},{3,7},{7,3},{8,12},{12,8},{9,1... | collective-permute-start | bytes 1081352 | tf_op jit(solution)/shard_map/ppermute | solution.py:23
  49.4 8.4 %collective-permute-start.5 = (bf16[640,256]{1,0:T(8,128)(2,1)S(1)}, bf16[640,256]{1,0:T(8,128)(2,1)S(1)}, u32[]{:S(2)}, u32[]{:S(2)}) collective-permute-start(bf16[640,256]{1,0:T(8,128)(2,1)S(1)} %shard_map.82), channel_id=1, source_target_pairs={{0,8},{4,20},{8,0},{12,28},{16,24},{20,4},{24,16},{28,12},{1,9},{5... | collective-permute-start | bytes 983048 | tf_op jit(solution)/shard_map/ppermute | solution.py:29
  57.2 4.7 %collective-permute-start.18 = (bf16[640,256]{1,0:T(8,128)(2,1)S(1)}, bf16[640,256]{1,0:T(8,128)(2,1)S(1)}, u32[]{:S(2)}, u32[]{:S(2)}) collective-permute-start(bf16[640,256]{1,0:T(8,128)(2,1)S(1)} %collective-permute-done.14.refs_24_), channel_id=1, source_target_pairs={{0,4},{4,0},{1,5},{5,1},{2,6},{6,2},{3,7},{7,3},{8,12},{12,8},{9,1... | collective-permute-start | bytes 983048 | tf_op jit(solution)/shard_map/ppermute | solution.py:23
  57.8 4.3 %collective-permute-start.17 = (bf16[640,256]{1,0:T(8,128)(2,1)S(1)}, bf16[640,256]{1,0:T(8,128)(2,1)S(1)}, u32[]{:S(2)}, u32[]{:S(2)}) collective-permute-start(bf16[640,256]{1,0:T(8,128)(2,1)S(1)} %collective-permute-done.13.refs_23_), channel_id=1, source_target_pairs={{0,4},{4,0},{1,5},{5,1},{2,6},{6,2},{3,7},{7,3},{8,12},{12,8},{9,1... | collective-permute-start | bytes 983048 | tf_op jit(solution)/shard_map/ppermute | solution.py:23
  58.4 9.1 %collective-permute-start.15 = (bf16[640,256]{1,0:T(8,128)(2,1)S(1)}, bf16[640,256]{1,0:T(8,128)(2,1)S(1)}, u32[]{:S(2)}, u32[]{:S(2)}) collective-permute-start(bf16[640,256]{1,0:T(8,128)(2,1)S(1)} %collective-permute-done.13.refs_23_), channel_id=1, source_target_pairs={{0,16},{4,12},{8,24},{12,4},{16,0},{20,28},{24,8},{28,20},{1,17},{... | collective-permute-start | bytes 983048 | tf_op jit(solution)/shard_map/ppermute | solution.py:29
  60.2 8.8 %collective-permute-start.10 = (bf16[640,256]{1,0:T(8,128)(2,1)S(1)}, bf16[640,256]{1,0:T(8,128)(2,1)S(1)}, u32[]{:S(2)}, u32[]{:S(2)}) collective-permute-start(bf16[640,256]{1,0:T(8,128)(2,1)S(1)} %collective-permute-done.6.refs_16_), channel_id=1, source_target_pairs={{0,4},{4,0},{1,5},{5,1},{2,6},{6,2},{3,7},{7,3},{8,12},{12,8},{9,1... | collective-permute-start | bytes 983048 | tf_op jit(solution)/shard_map/ppermute | solution.py:23
  60.3 9.3 %collective-permute-start.21 = (bf16[640,256]{1,0:T(8,128)(2,1)S(1)}, bf16[640,256]{1,0:T(8,128)(2,1)S(1)}, u32[]{:S(2)}, u32[]{:S(2)}) collective-permute-start(bf16[640,256]{1,0:T(8,128)(2,1)S(1)} %shard_map.84), channel_id=1, source_target_pairs={{0,8},{4,20},{8,0},{12,28},{16,24},{20,4},{24,16},{28,12},{1,9},{5... | collective-permute-start | bytes 983048 | tf_op jit(solution)/shard_map/ppermute | solution.py:29
  61.9 16.2 %collective-permute-start.24 = (bf16[704,256]{1,0:T(8,128)(2,1)S(1)}, bf16[704,256]{1,0:T(8,128)(2,1)S(1)}, u32[]{:S(2)}, u32[]{:S(2)}) collective-permute-start(bf16[704,256]{1,0:T(8,128)(2,1)S(1)} %collective-permute-done.20.refs_0_.refs_30_), channel_id=1, source_target_pairs={{0,4},{4,0},{1,5},{5,1},{2,6},{6,2},{3,7},{7,3},{8,12},{12,8},{9,1... | collective-permute-start | bytes 1081352 | tf_op jit(solution)/shard_map/ppermute | solution.py:23
  62.1 9.0 %collective-permute-start.9 = (bf16[640,256]{1,0:T(8,128)(2,1)S(1)}, bf16[640,256]{1,0:T(8,128)(2,1)S(1)}, u32[]{:S(2)}, u32[]{:S(2)}) collective-permute-start(bf16[640,256]{1,0:T(8,128)(2,1)S(1)} %collective-permute-done.5.refs_15_), channel_id=1, source_target_pairs={{0,4},{4,0},{1,5},{5,1},{2,6},{6,2},{3,7},{7,3},{8,12},{12,8},{9,1... | collective-permute-start | bytes 983048 | tf_op jit(solution)/shard_map/ppermute | solution.py:23
  67.5 7.1 %collective-permute-start.7 = (bf16[640,256]{1,0:T(8,128)(2,1)S(1)}, bf16[640,256]{1,0:T(8,128)(2,1)S(1)}, u32[]{:S(2)}, u32[]{:S(2)}) collective-permute-start(bf16[640,256]{1,0:T(8,128)(2,1)S(1)} %collective-permute-done.5.refs_15_), channel_id=1, source_target_pairs={{0,16},{4,12},{8,24},{12,4},{16,0},{20,28},{24,8},{28,20},{1,17},{... | collective-permute-start | bytes 983048 | tf_op jit(solution)/shard_map/ppermute | solution.py:29
  69.0 9.1 %collective-permute-start.22 = (bf16[640,256]{1,0:T(8,128)(2,1)S(1)}, bf16[640,256]{1,0:T(8,128)(2,1)S(1)}, u32[]{:S(2)}, u32[]{:S(2)}) collective-permute-start(bf16[640,256]{1,0:T(8,128)(2,1)S(1)} %shard_map.84), channel_id=1, source_target_pairs={{0,16},{4,12},{8,24},{12,4},{16,0},{20,28},{24,8},{28,20},{1,17},{... | collective-permute-start | bytes 983048 | tf_op jit(solution)/shard_map/ppermute | solution.py:29
  69.6 12.1 %collective-permute-start.23 = (bf16[640,256]{1,0:T(8,128)(2,1)S(1)}, bf16[640,256]{1,0:T(8,128)(2,1)S(1)}, u32[]{:S(2)}, u32[]{:S(2)}) collective-permute-start(bf16[640,256]{1,0:T(8,128)(2,1)S(1)} %collective-permute-done.21.refs_31_), channel_id=1, source_target_pairs={{0,16},{4,12},{8,24},{12,4},{16,0},{20,28},{24,8},{28,20},{1,17},{... | collective-permute-start | bytes 983048 | tf_op jit(solution)/shard_map/ppermute | solution.py:29
  71.1 11.0 %collective-permute-start.19 = (bf16[640,256]{1,0:T(8,128)(2,1)S(1)}, bf16[640,256]{1,0:T(8,128)(2,1)S(1)}, u32[]{:S(2)}, u32[]{:S(2)}) collective-permute-start(bf16[640,256]{1,0:T(8,128)(2,1)S(1)} %collective-permute-done.15.refs_25_), channel_id=1, source_target_pairs={{0,4},{4,0},{1,5},{5,1},{2,6},{6,2},{3,7},{7,3},{8,12},{12,8},{9,1... | collective-permute-start | bytes 983048 | tf_op jit(solution)/shard_map/ppermute | solution.py:23
  74.6 7.4 %collective-permute-start.11 = (bf16[640,256]{1,0:T(8,128)(2,1)S(1)}, bf16[640,256]{1,0:T(8,128)(2,1)S(1)}, u32[]{:S(2)}, u32[]{:S(2)}) collective-permute-start(bf16[640,256]{1,0:T(8,128)(2,1)S(1)} %collective-permute-done.7.refs_17_), channel_id=1, source_target_pairs={{0,4},{4,0},{1,5},{5,1},{2,6},{6,2},{3,7},{7,3},{8,12},{12,8},{9,1... | collective-permute-start | bytes 983048 | tf_op jit(solution)/shard_map/ppermute | solution.py:23
  78.1 4.0 %collective-permute-start.25 = (bf16[640,256]{1,0:T(8,128)(2,1)S(1)}, bf16[640,256]{1,0:T(8,128)(2,1)S(1)}, u32[]{:S(2)}, u32[]{:S(2)}) collective-permute-start(bf16[640,256]{1,0:T(8,128)(2,1)S(1)} %collective-permute-done.21.refs_31_), channel_id=1, source_target_pairs={{0,4},{4,0},{1,5},{5,1},{2,6},{6,2},{3,7},{7,3},{8,12},{12,8},{9,1... | collective-permute-start | bytes 983048 | tf_op jit(solution)/shard_map/ppermute | solution.py:23
  78.1 3.9 %collective-permute-start.26 = (bf16[640,256]{1,0:T(8,128)(2,1)S(1)}, bf16[640,256]{1,0:T(8,128)(2,1)S(1)}, u32[]{:S(2)}, u32[]{:S(2)}) collective-permute-start(bf16[640,256]{1,0:T(8,128)(2,1)S(1)} %collective-permute-done.22.refs_32_), channel_id=1, source_target_pairs={{0,4},{4,0},{1,5},{5,1},{2,6},{6,2},{3,7},{7,3},{8,12},{12,8},{9,1... | collective-permute-start | bytes 983048 | tf_op jit(solution)/shard_map/ppermute | solution.py:23
  81.6 1.6 %collective-permute-start.27 = (bf16[640,256]{1,0:T(8,128)(2,1)S(1)}, bf16[640,256]{1,0:T(8,128)(2,1)S(1)}, u32[]{:S(2)}, u32[]{:S(2)}) collective-permute-start(bf16[640,256]{1,0:T(8,128)(2,1)S(1)} %collective-permute-done.23.refs_33_), channel_id=1, source_target_pairs={{0,4},{4,0},{1,5},{5,1},{2,6},{6,2},{3,7},{7,3},{8,12},{12,8},{9,1... | collective-permute-start | bytes 983048 | tf_op jit(solution)/shard_map/ppermute | solution.py:23
  81.6 1.6 %copy-start.6 = (f32[2048]{0:T(1024)S(1)}, f32[2048]{0:T(1024)}, u32[]{:S(2)}) copy-start(f32[2048]{0:T(1024)} %param.10) | copy-start | bytes 24580
  83.2 0.7 copy-start.7
where the time goes:
time: 92.8 us; the launch traced here: 91.7 us
  waiting for transfers between devices  52.4 us (56%)
  starting transfers between devices  28.3 us (30%)
  Pallas kernels  9.74 us (10%)
    ppermute x6, waiting for transfers between devices, shift(): lax.ppermute(v, 'tensor', [(i, (i + k) % n) for i in range(n)])  29 us
    ppermute x9, waiting for transfers between devices, plane_xor(): return lambda v: lax.ppermute(v, PLANE, pairs)  22.2 us
    ppermute x6, starting transfers between devices, shift(): lax.ppermute(v, 'tensor', [(i, (i + k) % n) for i in range(n)])  13.8 us
    ppermute x9, starting transfers between devices, plane_xor(): return lambda v: lax.ppermute(v, PLANE, pairs)  12.7 us
    pallas_call x1, Pallas kernels, body(): pl.pallas_call(functools.partial(kernel, dims, nearest(n), plan), name='m...  7.84 us
  transfers between devices with their start and end apart: 28, of which 11 were waited for; matrix products, arithmetic and copies ran while one was open for 0% of the time, Pallas kernels for 0%

commit v1 on v0

--- a/solution.py
+++ b/solution.py
@@ -11,6 +11,7 @@
 epsilon = 1e-06
 theta_base = 10000.0
 PLANE = ("query", "cand")
+UNROLL = 4
 
 
 def shift(k):
@@ -140,19 +141,49 @@
     return jnp.cos(angles), jnp.sin(angles)
 
 
-def kernel(dims, rounds, plan, *refs):
+def rows_of(start, size):
+    return pl.ds(pl.multiple_of(start, size), size)
+
+
+def places(rounds, plan, q_at, me, parity):
+    sources = []
+    for by_place in rounds:
+        value = by_place[0]
+        for t in range(1, len(by_place)):
+            value = jnp.where(me == t, by_place[t], value)
+        sources.append(value)
+    parts = []
+    for masks, crossed in plan:
+        mask = jnp.where(parity == 0, masks[0], masks[1])
+        parts.append(lax.bitwise_xor(q_at, mask) * 2 + (parity if not crossed else 1 - parity))
+    return sources, parts
+
+
+def add_up(terms):
+    chains = [functools.reduce(jnp.add, terms[i::2]) for i in range(2)]
+    return chains[0] + chains[1]
+
+
+def rotated(lower, upper, cos, sin):
+    return lower * cos - upper * sin, upper * cos + lower * sin
+
+
+TRANS = (((1,), (1,)), ((), ()))
+
+
+def first_kernel(dims, rounds, plan, *refs):
     n, rows, cand_len, prefix_rows, prefix_len, depth, head, _ = dims
     n_pieces = len(plan)
-    n_in = 11 + (n - 1) + (n - 1) * n_pieces
-    cand_ref, gain_ref, cos_ref, sin_ref, len_ref = refs[:5]
-    prefix_refs = refs[5:7]
-    own_q, own_out, own_k, own_v = refs[7:11]
+    count = n - 2
+    cand_ref, gain_ref, cos_ref, sin_ref = refs[:4]
+    prefix_refs = refs[4:8]
+    own_q, own_k, own_v = refs[8:11]
     x_refs = refs[11 : 11 + n - 1]
+    n_in = 11 + n - 1 + count * n_pieces
     piece_refs = refs[11 + n - 1 : n_in]
-    o_ref = refs[n_in]
-    x_own, w_query, w_out, w_kv, p_raw, normed, kv_scr, q_scr, heads, sems = refs[n_in + 1 :]
+    normed, q_ref, kv_ref = refs[n_in : n_in + 3]
+    x_own, w_query, w_kv, p_raw, sems = refs[n_in + 3 :]
     me = lax.axis_index("tensor")
-    q_at = lax.axis_index("query")
     parity = lax.rem(lax.axis_index("cand"), 2)
     width = depth // n
     half = head // 2
@@ -160,120 +191,175 @@
     size = w_query.shape[1]
     chunks = width // size
 
-    def rows_of(start, size):
-        return pl.ds(pl.multiple_of(start, size), size)
-
-    def table(places):
-        value = places[0]
-        for t in range(1, n):
-            value = jnp.where(me == t, places[t], value)
-        return value
-
     moves = [
         (cand_ref.at[rows_of(me * rows, rows), :], x_own),
         (own_k, w_kv.at[pl.ds(0, share), :]),
         (own_v, w_kv.at[pl.ds(share, share), :]),
         (own_q, w_query),
-        (own_out, w_out),
     ]
     copies = [pltpu.make_async_copy(src, dst, sems.at[i]) for i, (src, dst) in enumerate(moves)]
     for c in copies:
         c.start()
-
-    sources = [me] + [table(places) for places in rounds]
-    pieces = [piece_refs[r * n_pieces : (r + 1) * n_pieces] for r in range(n - 1)]
-    parts = []
-    for masks, crossed in plan:
-        mask = jnp.where(parity == 0, masks[0], masks[1])
-        parts.append(lax.bitwise_xor(q_at, mask) * 2 + (parity if not crossed else 1 - parity))
+    sources, parts = places(rounds, plan, lax.axis_index("query"), me, parity)
+    sources = [me] + sources
+    pieces = [piece_refs[r * n_pieces : (r + 1) * n_pieces] for r in range(count)]
 
     fixed = size + head + 2 * share
-    prefix_in = [prefix_refs] + [(p[0], p[n_pieces // 2]) for p in pieces]
+    prefix_in = [prefix_refs[:2]] + [(p[0], p[n_pieces // 2]) for p in pieces] + [prefix_refs[2:]]
     for source, both in zip(sources, prefix_in):
         for ref, side in zip(both, (parity, 1 - parity)):
-            for at, count, start, lane in prefix_blocks(
+            for at, height, start, lane in prefix_blocks(
                 fixed, side, prefix_rows, prefix_len, width, size
             ):
-                to = rows_of(start, count) if 2 * prefix_rows == prefix_len else pl.ds(start, count)
-                p_raw[source * chunks + lane // size, to, :] = ref[pl.ds(at, count), :]
+                whole = 2 * prefix_rows != prefix_len
+                to = pl.ds(start, height) if whole else rows_of(start, height)
+                p_raw[source * chunks + lane // size, to, :] = ref[pl.ds(at, height), :]
 
     block = 32
 
     def normalise(parts_in, to_rows):
-        values = [v.astype(jnp.float32) for _, v in parts_in]
-        square = sum(jnp.sum(v * v, axis=-1, keepdims=True) for v in values) / depth
+        values = [ref[at].astype(jnp.float32) for _, ref, at in parts_in]
+        square = sum(v * v for v in values)
+        square = jnp.sum(square, axis=-1, keepdims=True) / depth
         scale = lax.rsqrt(square + epsilon)
-        for (chunk, _), v in zip(parts_in, values):
+        for (chunk, ref, at), v in zip(parts_in, values):
             normed[chunk, to_rows, :] = (v * scale * gain_ref[chunk]).astype(jnp.bfloat16)
 
-    @pl.loop(0, prefix_len // block)
-    def _(i):
+    def prefix_block(i, carry):
         at = rows_of(i * block, block)
         to = pl.ds(pl.multiple_of(rows + i * block, block), block)
-        normalise([(c, p_raw[c, at, :]) for c in range(n * chunks)], to)
-
+        normalise([(c, p_raw, (c, at, slice(None))) for c in range(n * chunks)], to)
+        return carry
+
+    lax.fori_loop(0, prefix_len // block, prefix_block, 0, unroll=UNROLL)
     copies[0].wait()
-    x_all = [x_own] + list(x_refs)
     x_from = [me] + [lax.rem(me - k + n, n) for k in range(1, n)]
 
-    @pl.loop(0, rows // block)
-    def _(i):
+    def cand_block(i, carry):
         at = rows_of(i * block, block)
         normalise(
             [
-                (source * chunks + h, ref[at, pl.ds(h * size, size)])
-                for source, ref in zip(x_from, x_all)
+                (source * chunks + h, ref, (at, pl.ds(h * size, size)))
+                for source, ref in zip(x_from, [x_own] + list(x_refs))
                 for h in range(chunks)
             ],
             at,
         )
-
-    cos, sin = cos_ref[...], sin_ref[...]
-    cand_cos = jnp.concatenate([cos[prefix_len:]] * (rows // cand_len), axis=0)
-    cand_sin = jnp.concatenate([sin[prefix_len:]] * (rows // cand_len), axis=0)
-    all_cos = jnp.concatenate([cand_cos, cos[:prefix_len]], axis=0)
-    all_sin = jnp.concatenate([cand_sin, sin[:prefix_len]], axis=0)
-    trans = (((1,), (1,)), ((), ()))
-
-    copies[1].wait()
-    copies[2].wait()
-    made = None
+        return carry
+
+    lax.fori_loop(0, rows // block, cand_block, 0, unroll=UNROLL)
+
+    for c in copies[1:3]:
+        c.wait()
+    made = []
     for i, part in enumerate(parts):
         weights = jnp.concatenate(
             [w_kv[:, rows_of(part * size, size)]]
             + [p[i][pl.ds(size + head, 2 * share), :] for p in pieces],
             axis=0,
         )
-        term = lax.dot_general(normed[part], weights, trans, preferred_element_type=jnp.float32)
-        made = term if made is None else made + term
-    for k, source in enumerate(sources):
-        kv_scr[source] = made[:, k * 2 * share : (k + 1) * 2 * share].astype(jnp.bfloat16)
+        made.append(
+            lax.dot_general(normed[part], weights, TRANS, preferred_element_type=jnp.float32)
+        )
+    made = functools.reduce(jnp.add, made).astype(jnp.bfloat16)
+    for k in range(n - 1):
+        kv_ref[k] = made[:, k * 2 * share : (k + 1) * 2 * share]
+
+    cand_cos = jnp.concatenate([cos_ref[prefix_len:, :]] * (rows // cand_len), axis=0)
+    cand_sin = jnp.concatenate([sin_ref[prefix_len:, :]] * (rows // cand_len), axis=0)
+    copies[3].wait()
+    weights_of = [
+        [w_query[rows_of(part * size, size), :] for part in parts]
+    ] + [[v[pl.ds(0, size), :] for v in p] for p in pieces]
+
+    def project(ks, first, count):
+        made = None
+        for i, part in enumerate(parts):
+            weights = [weights_of[k][i] for k in ks]
+            weights = weights[0] if len(ks) == 1 else jnp.concatenate(weights, axis=1)
+            term = jnp.dot(
+                normed[part, pl.ds(first, count), :], weights, preferred_element_type=jnp.float32
+            )
+            made = term if made is None else made + term
+        return made
+
+    def store(k, made, first, count):
+        lower, upper = rotated(
+            made[:, :half],
+            made[:, half:],
+            cand_cos[first : first + count],
+            cand_sin[first : first + count],
+        )
+        q_ref[k, pl.ds(first, count), :half] = (lower * head ** (-0.5)).astype(jnp.bfloat16)
+        q_ref[k, pl.ds(first, count), half:] = (upper * head ** (-0.5)).astype(jnp.bfloat16)
+
+    for k in range(0, n - 1, 2):
+        if k + 1 < n - 1:
+            made = project((k, k + 1), 0, rows)
+            store(k, made[:, :head], 0, rows)
+            store(k + 1, made[:, head:], 0, rows)
+        else:
+            parts_made = [project((k,), at, rows // 2) for at in (0, rows // 2)]
+            for at, made in zip((0, rows // 2), parts_made):
+                store(k, made, at, rows // 2)
+
+
+def last_kernel(dims, rounds, plan, *refs):
+    n, rows, cand_len, _, prefix_len, _, head, _ = dims
+    n_pieces = len(plan)
+    normed, q_in, kv_in, cos_ref, sin_ref, len_ref, own_out = refs[:7]
+    n_in = 7 + (n - 1) * n_pieces
+    piece_refs = refs[7:n_in]
+    o_ref = refs[n_in]
+    w_out, kv_scr, heads, sem = refs[n_in + 1 :]
+    me = lax.axis_index("tensor")
+    parity = lax.rem(lax.axis_index("cand"), 2)
+    half = head // 2
+    share = kv_in.shape[2] // 2
+    size = normed.shape[2]
+    c = pltpu.make_async_copy(own_out, w_out, sem)
+    c.start()
+    sources, parts = places(rounds, plan, lax.axis_index("query"), me, parity)
+    pieces = [piece_refs[r * n_pieces : (r + 1) * n_pieces] for r in range(n - 1)]
+    cos, sin = cos_ref[...], sin_ref[...]
+    cand_cos = jnp.concatenate([cos[prefix_len:]] * (rows // cand_len), axis=0)
+    cand_sin = jnp.concatenate([sin[prefix_len:]] * (rows // cand_len), axis=0)
+    all_cos = jnp.concatenate([cand_cos, cos[:prefix_len]], axis=0)
+    all_sin = jnp.concatenate([cand_sin, sin[:prefix_len]], axis=0)
+
+    last = pieces[-1]
+    made = add_up(
+        [
+            lax.dot_general(
+                normed[part],
+                last[i][pl.ds(size + head, 2 * share), :],
+                TRANS,
+                preferred_element_type=jnp.float32,
+            )
+            for i, part in enumerate(parts)
+        ]
+    )
+    for k, source in enumerate([me] + sources):
+        kv_scr[source] = kv_in[k] if k < n - 1 else made.astype(jnp.bfloat16)
+    made = add_up(
+        [
+            jnp.dot(
+                normed[part, pl.ds(0, rows), :],
+                last[i][pl.ds(0, size), :],
+                preferred_element_type=jnp.float32,
+            )
+            for i, part in enumerate(parts)
+        ]
+    )
+    lower, upper = rotated(made[:, :half], made[:, half:], cand_cos, cand_sin)
+    last_q = jnp.concatenate([lower, upper], axis=1) * head ** (-0.5)
+    last_q = last_q.astype(jnp.bfloat16)
+
     shares = [kv_scr[s] for s in range(n)]
     low = jnp.concatenate([p[:, :share] for p in shares[: n // 2]], axis=1).astype(jnp.float32)
     up = jnp.concatenate([p[:, :share] for p in shares[n // 2 :]], axis=1).astype(jnp.float32)
-    keys = jnp.concatenate(
-        [low * all_cos - up * all_sin, up * all_cos + low * all_sin], axis=1
-    ).astype(jnp.bfloat16)
+    keys = jnp.concatenate(rotated(low, up, all_cos, all_sin), axis=1).astype(jnp.bfloat16)
     values = jnp.concatenate([p[:, share:] for p in shares], axis=1)
-    prefix_keys, prefix_values = keys[rows:], values[rows:]
-
-    scale = head ** (-0.5)
-    for k in range(n - 1, -1, -1):
-        if k == 0:
-            copies[3].wait()
-        made = None
-        for i, part in enumerate(parts):
-            if k == 0:
-                weights = w_query[rows_of(part * size, size), :]
-            else:
-                weights = pieces[k - 1][i][pl.ds(0, size), :]
-            term = jnp.dot(
-                normed[part, pl.ds(0, rows), :], weights, preferred_element_type=jnp.float32
-            )
-            made = term if made is None else made + term
-        lower, upper = made[:, :half], made[:, half:]
-        q_scr[k, :, :half] = ((lower * cand_cos - upper * cand_sin) * scale).astype(jnp.bfloat16)
-        q_scr[k, :, half:] = ((upper * cand_cos + lower * cand_sin) * scale).astype(jnp.bfloat16)
 
     tall = (n, cand_len, cand_len + prefix_len)
     slot = lax.broadcasted_iota(jnp.int32, tall, 1).reshape(n * cand_len, tall[2])
@@ -282,28 +368,33 @@
     for j in range(rows // cand_len):
         own = slice(j * cand_len, (j + 1) * cand_len)
         live = slot[:, :1] < len_ref[me * (rows // cand_len) + j]
-        keys_j = jnp.concatenate([keys[own], prefix_keys], axis=0)
-        values_j = jnp.concatenate([values[own], prefix_values], axis=0)
-        queries = jnp.concatenate([q_scr[k, own, :] for k in range(n)], axis=0)
-        scores = lax.dot_general(queries, keys_j, trans, preferred_element_type=jnp.float32)
+        keys_j = jnp.concatenate([keys[own], keys[rows:]], axis=0)
+        values_j = jnp.concatenate([values[own], values[rows:]], axis=0)
+        queries = jnp.concatenate([q_in[k, own, :] for k in range(n - 1)] + [last_q[own]], axis=0)
+        scores = lax.dot_general(queries, keys_j, TRANS, preferred_element_type=jnp.float32)
         scores = jnp.where(seen, scores, -jnp.inf)
         weights = jnp.exp(scores - scores.max(-1, keepdims=True))
         divisor = weights.sum(-1, keepdims=True)
         mix = jnp.dot(weights.astype(jnp.bfloat16), values_j, preferred_element_type=jnp.float32)
-        mix = jnp.where(live, mix / divisor, 0.0).astype(jnp.bfloat16)
+        mix = (mix * jnp.where(live, 1.0 / divisor, 0.0)).astype(jnp.bfloat16)
         for k in range(n):
             heads[k, own, :] = mix[k * cand_len : (k + 1) * cand_len]
 
-    copies[4].wait()
-    for i, part in enumerate(parts):
-        spot = rows_of(part * size, size)
+    c.wait()
+    for i in range(0, n_pieces, 2):
+        spots = [rows_of(part * size, size) for part in parts[i : i + 2]]
         total = None
         for k in range(n):
-            weights = w_out[:, spot] if k == 0 else pieces[k - 1][i][pl.ds(size, head), :]
-            term = jnp.dot(heads[k], weights, preferred_element_type=jnp.float32)
-            term = term.astype(jnp.bfloat16).astype(jnp.float32)
+            if k == 0:
+                weights = [w_out[:, spot] for spot in spots]
+            else:
+                weights = [p[pl.ds(size, head), :] for p in pieces[k - 1][i : i + 2]]
+            term = jnp.dot(
+                heads[k], jnp.concatenate(weights, axis=1), preferred_element_type=jnp.float32
+            )
             total = term if total is None else total + term
-        o_ref[:, spot] = total.astype(jnp.bfloat16)
+        for at, spot in enumerate(spots):
+            o_ref[:, spot] = total[:, at * size : (at + 1) * size].astype(jnp.bfloat16)
 
 
 def body(cand_states, prefix_states, norm_gain, w_query, w_key, w_value, w_out, cand_lengths):
@@ -351,32 +442,50 @@
     cos, sin = rotary_tables(prefix_len + cand_len, half, head)
 
     dims = (n, rows, cand_len, prefix_rows, prefix_len, depth, head, out_cols)
-    return pl.pallas_call(
-        functools.partial(kernel, dims, nearest(n), plan),
-        name="main",
-        out_shape=jax.ShapeDtypeStruct((rows, out_cols), jnp.bfloat16),
-        in_specs=[hbm, vmem, vmem, vmem, smem]
-        + [vmem] * 2
-        + [hbm] * 4
-        + [vmem] * (len(xs) + len(pieces)),
-        out_specs=vmem,
+    count = len(spreads[0])
+    every = rows + prefix_len
+    early = pieces[: (n - 2) * count]
+    last = pieces[(n - 2) * count :]
+    normed, queries, pairs = pl.pallas_call(
+        functools.partial(first_kernel, dims, nearest(n), plan),
+        name="first",
+        out_shape=[
+            jax.ShapeDtypeStruct((depth // size, every, size), jnp.bfloat16),
+            jax.ShapeDtypeStruct((n - 1, rows, head), jnp.bfloat16),
+            jax.ShapeDtypeStruct((n - 1, every, 2 * share), jnp.bfloat16),
+        ],
+        in_specs=[hbm, vmem, vmem, vmem]
+        + [vmem] * 4
+        + [hbm] * 3
+        + [vmem] * (len(xs) + len(early)),
+        out_specs=[vmem] * 3,
         scratch_shapes=[
             pltpu.VMEM((rows, depth // n), jnp.bfloat16),
             pltpu.VMEM((depth, head), jnp.bfloat16),
-            pltpu.VMEM((head, out_cols), jnp.bfloat16),
             pltpu.VMEM((2 * share, depth), jnp.bfloat16),
             pltpu.VMEM((depth // size, prefix_len, size), jnp.bfloat16),
-            pltpu.VMEM((depth // size, rows + prefix_len, size), jnp.bfloat16),
-            pltpu.VMEM((n, rows + prefix_len, 2 * share), jnp.bfloat16),
+            pltpu.SemaphoreType.DMA((4,)),
+        ],
+        compiler_params=pltpu.CompilerParams(vmem_limit_bytes=24 * 2**20),
+    )(
+        cand_states, norm_gain.reshape(depth // size, 1, size), cos, sin,
+        piece, across, last[0], last[count // 2],
+        w_query, key_t, value_t, *xs, *early,
+    )
+    return pl.pallas_call(
+        functools.partial(last_kernel, dims, nearest(n), plan),
+        name="main",
+        out_shape=jax.ShapeDtypeStruct((rows, out_cols), jnp.bfloat16),
+        in_specs=[vmem] * 5 + [smem, hbm] + [vmem] * len(pieces),
+        out_specs=vmem,
+        scratch_shapes=[
+            pltpu.VMEM((head, out_cols), jnp.bfloat16),
+            pltpu.VMEM((n, every, 2 * share), jnp.bfloat16),
             pltpu.VMEM((n, rows, head), jnp.bfloat16),
-            pltpu.VMEM((n, rows, head), jnp.bfloat16),
-            pltpu.SemaphoreType.DMA((5,)),
+            pltpu.SemaphoreType.DMA,
         ],
-        compiler_params=pltpu.CompilerParams(vmem_limit_bytes=32 * 2**20),
-    )(
-        cand_states, norm_gain.reshape(depth // size, 1, size), cos, sin, cand_lengths,
-        piece, across, w_query, w_out, key_t, value_t, *xs, *pieces,
-    )
+        compiler_params=pltpu.CompilerParams(vmem_limit_bytes=24 * 2**20),
+    )(normed, queries, pairs, cos, sin, cand_lengths, w_out, *pieces)
 
 
 def solution(mesh):

time: 92.8 us -> 86.1 us (0.928)
  waiting for transfers between devices: 52.4 us -> 43.9 us
  starting transfers between devices: 28.3 us -> 30.6 us
    ppermute x6, waiting for transfers between devices: 29 us -> 24.8 us  [shift(): lax.ppermute(v, 'tensor', [(i, (i + k) % n) for i in range(n)])]
    ppermute x9, waiting for transfers between devices: 22.2 us -> 19.1 us  [plane_xor(): return lambda v: lax.ppermute(v, PLANE, pairs)]
    ppermute x13, waiting for transfers between devices: 1.21 us -> 0.03 us  [other_core(): return lax.ppermute(v, 'cand', [(i, i ^ 1) for i in range(n)])]
    pallas_call x1 -> x2, Pallas kernels: 7.84 us -> 7.69 us  [the longest x1 4.8 us: body(): pl.pallas_call(functools.partial(last_kernel, dims, nearest(n), plan), na...]
  transfers between devices with their start and end apart: 28 -> 28, of which waited for: 11 -> 9; matrix products, arithmetic and copies ran while one was open for 0% -> 1% of each run, Pallas kernels for 0% -> 3%
where the time goes in v1:
time: 86.1 us; the launch traced here: 84.9 us
  waiting for transfers between devices  43.9 us (51%)
  starting transfers between devices  30.6 us (36%)
  Pallas kernels  9.59 us (11%)
    ppermute x6, waiting for transfers between devices, shift(): lax.ppermute(v, 'tensor', [(i, (i + k) % n) for i in range(n)])  24.8 us
    ppermute x9, waiting for transfers between devices, plane_xor(): return lambda v: lax.ppermute(v, PLANE, pairs)  19.1 us
    ppermute x6, starting transfers between devices, shift(): lax.ppermute(v, 'tensor', [(i, (i + k) % n) for i in range(n)])  14.7 us
    ppermute x9, starting transfers between devices, plane_xor(): return lambda v: lax.ppermute(v, PLANE, pairs)  13.6 us
    pallas_call x1, Pallas kernels, body(): pl.pallas_call(functools.partial(last_kernel, dims, nearest(n), plan), na...  4.8 us
    pallas_call x1, Pallas kernels, body(): pl.pallas_call(functools.partial(first_kernel, dims, nearest(n), plan), n...  2.89 us
    ppermute x13, starting transfers between devices, other_core(): return lax.ppermute(v, 'cand', [(i, i ^ 1) for i in range(n)])  2.24 us
    pallas_call x1, Pallas kernels, body(): pl.pallas_call(functools.partial(cut_kernel, (prefix_rows, prefix_len, ca...  1.83 us
  transfers between devices with their start and end apart: 28, of which 9 were waited for; matrix products, arithmetic and copies ran while one was open for 1% of the time, Pallas kernels for 3%

profile of v1, /device:TPU:0, one launch (start us, length us, event | category | flops | bytes accessed | tf_op | source)
XLA Modules:
  0.0 84.9 jit_solution(14052871046278885172)
XLA Ops:
  0.0 1.8 %cut.1.refs_4_ = bf16[704,256]{1,0:T(8,128)(2,1)} custom-call(bf16[2048,256]{1,0:T(8,128)(2,1)} %refs_8_.1, bf16[256,2048]{1,0:T(8,128)(2,1)} %refs_6_.1, bf16[64,2048]{1,0:T(8,128)(2,1)} %bitcast.3, bf16[64,2048]{1,0:T(8,128)(2,1)} %bitcast.5, bf16[32,512]{1,0:T(8,128)(2,1)} %p_ref.1), custom_call_target="tpu_custom_call" | custom-call | tf_op jit(solution)/shard_map/cut/pallas_call | solution.py:424
  1.8 0.0 copy-start.3
  1.9 3.1 %collective-permute-start.1 = (bf16[704,256]{1,0:T(8,128)(2,1)}, bf16[704,256]{1,0:T(8,128)(2,1)S(1)}, u32[]{:S(2)}, u32[]{:S(2)}) collective-permute-start(bf16[704,256]{1,0:T(8,128)(2,1)} %cut.1.refs_4_), channel_id=1, source_target_pairs={{0,1},{1,2},{2,3},{3,0},{4,5},{5,6},{6,7},{7,4},{8,9},{9,10},{10,1... | collective-permute-start | bytes 1081352 | tf_op jit(solution)/shard_map/ppermute | solution.py:19
  5.0 2.1 %collective-permute-start.14 = (bf16[704,256]{1,0:T(8,128)(2,1)}, bf16[704,256]{1,0:T(8,128)(2,1)S(1)}, u32[]{:S(2)}, u32[]{:S(2)}) collective-permute-start(bf16[704,256]{1,0:T(8,128)(2,1)} %cut.1.refs_4_), channel_id=1, source_target_pairs={{0,3},{1,0},{2,1},{3,2},{4,7},{5,4},{6,5},{7,6},{8,11},{9,8},{10,9... | collective-permute-start | bytes 1081352 | tf_op jit(solution)/shard_map/ppermute | solution.py:19
  7.1 0.1 constant_dynamic-slice_fusion
  7.1 0.0 copy-start
  7.1 0.0 copy-start.4
  7.1 0.0 copy-start.5
  7.2 0.0 copy-start.6
  7.2 0.1 collective-permute-start.4
  7.2 0.1 collective-permute-start
  7.3 9.2 %collective-permute-done.1.refs_0_.refs_14_.refs_7_ = bf16[704,256]{1,0:T(8,128)(2,1)S(1)} collective-permute-done((bf16[704,256]{1,0:T(8,128)(2,1)}, bf16[704,256]{1,0:T(8,128)(2,1)S(1)}, u32[]{:S(2)}, u32[]{:S(2)}) %collective-permute-start.1) | collective-permute-done | bytes 360480 | tf_op jit(solution)/shard_map/ppermute | solution.py:19
  16.5 1.8 %collective-permute-start.7 = (bf16[640,256]{1,0:T(8,128)(2,1)S(1)}, bf16[640,256]{1,0:T(8,128)(2,1)S(1)}, u32[]{:S(2)}, u32[]{:S(2)}) collective-permute-start(bf16[640,256]{1,0:T(8,128)(2,1)S(1)} %shard_map.82), channel_id=1, source_target_pairs={{0,8},{4,20},{8,0},{12,28},{16,24},{20,4},{24,16},{28,12},{1,9},{5... | collective-permute-start | bytes 983048 | tf_op jit(solution)/shard_map/ppermute | solution.py:30
  18.3 4.7 %collective-permute-done.14.refs_0_.refs_22_.refs_15_ = bf16[704,256]{1,0:T(8,128)(2,1)S(1)} collective-permute-done((bf16[704,256]{1,0:T(8,128)(2,1)}, bf16[704,256]{1,0:T(8,128)(2,1)S(1)}, u32[]{:S(2)}, u32[]{:S(2)}) %collective-permute-start.14) | collective-permute-done | bytes 360480 | tf_op jit(solution)/shard_map/ppermute | solution.py:19
  23.0 1.8 %collective-permute-start.15 = (bf16[640,256]{1,0:T(8,128)(2,1)S(1)}, bf16[640,256]{1,0:T(8,128)(2,1)S(1)}, u32[]{:S(2)}, u32[]{:S(2)}) collective-permute-start(bf16[640,256]{1,0:T(8,128)(2,1)S(1)} %shard_map.83), channel_id=1, source_target_pairs={{0,8},{4,20},{8,0},{12,28},{16,24},{20,4},{24,16},{28,12},{1,9},{5... | collective-permute-start | bytes 983048 | tf_op jit(solution)/shard_map/ppermute | solution.py:30
  24.8 2.6 %collective-permute-start.5 = (bf16[256,512]{1,0:T(8,128)(2,1)S(1)}, bf16[256,512]{1,0:T(8,128)(2,1)S(1)}, u32[]{:S(2)}, u32[]{:S(2)}) collective-permute-start(bf16[256,512]{1,0:T(8,128)(2,1)S(1)} %get-tuple-element.12), channel_id=1, source_target_pairs={{0,2},{1,3},{2,0},{3,1},{4,6},{5,7},{6,4},{7,5},{8,10},{9,11},{10,... | collective-permute-start | bytes 786440 | tf_op jit(solution)/shard_map/ppermute | solution.py:19
  27.4 1.7 %collective-permute-done.4.refs_11_ = bf16[256,512]{1,0:T(8,128)(2,1)S(1)} collective-permute-done((bf16[256,512]{1,0:T(8,128)(2,1)S(1)}, bf16[256,512]{1,0:T(8,128)(2,1)S(1)}, u32[]{:S(2)}, u32[]{:S(2)}) %collective-permute-start.4) | collective-permute-done | bytes 262176 | tf_op jit(solution)/shard_map/ppermute | solution.py:19
  29.1 2.0 %collective-permute-start.6 = (bf16[256,512]{1,0:T(8,128)(2,1)S(1)}, bf16[256,512]{1,0:T(8,128)(2,1)S(1)}, u32[]{:S(2)}, u32[]{:S(2)}) collective-permute-start(bf16[256,512]{1,0:T(8,128)(2,1)S(1)} %get-tuple-element.11), channel_id=1, source_target_pairs={{0,3},{1,0},{2,1},{3,2},{4,7},{5,4},{6,5},{7,6},{8,11},{9,8},{10,9... | collective-permute-start | bytes 786440 | tf_op jit(solution)/shard_map/ppermute | solution.py:19
  31.1 9.2 %collective-permute-done.5.refs_12_ = bf16[256,512]{1,0:T(8,128)(2,1)S(1)} collective-permute-done((bf16[256,512]{1,0:T(8,128)(2,1)S(1)}, bf16[256,512]{1,0:T(8,128)(2,1)S(1)}, u32[]{:S(2)}, u32[]{:S(2)}) %collective-permute-start.5) | collective-permute-done | bytes 262176 | tf_op jit(solution)/shard_map/ppermute | solution.py:19
  40.3 4.9 %collective-permute-start.2 = (bf16[704,256]{1,0:T(8,128)(2,1)S(1)}, bf16[704,256]{1,0:T(8,128)(2,1)S(1)}, u32[]{:S(2)}, u32[]{:S(2)}) collective-permute-start(bf16[704,256]{1,0:T(8,128)(2,1)S(1)} %collective-permute-done.1.refs_0_.refs_14_.refs_7_), channel_id=1, source_target_pairs={{0,1},{1,2},{2,3},{3,0},{4,5},{5,6},{6,7},{7,4},{8,9},{9,10},{10,1... | collective-permute-start | bytes 1081352 | tf_op jit(solution)/shard_map/ppermute | solution.py:19
  45.2 0.0 collective-permute-done.refs_5_
  45.2 1.6 %collective-permute-start.8 = (bf16[640,256]{1,0:T(8,128)(2,1)S(1)}, bf16[640,256]{1,0:T(8,128)(2,1)S(1)}, u32[]{:S(2)}, u32[]{:S(2)}) collective-permute-start(bf16[640,256]{1,0:T(8,128)(2,1)S(1)} %shard_map.82), channel_id=1, source_target_pairs={{0,16},{4,12},{8,24},{12,4},{16,0},{20,28},{24,8},{28,20},{1,17},{... | collective-permute-start | bytes 983048 | tf_op jit(solution)/shard_map/ppermute | solution.py:30
  46.8 0.0 collective-permute-done.7.refs_15_.refs_8_
  46.8 0.1 collective-permute-start.18
  47.0 1.5 %collective-permute-start.16 = (bf16[640,256]{1,0:T(8,128)(2,1)S(1)}, bf16[640,256]{1,0:T(8,128)(2,1)S(1)}, u32[]{:S(2)}, u32[]{:S(2)}) collective-permute-start(bf16[640,256]{1,0:T(8,128)(2,1)S(1)} %shard_map.83), channel_id=1, source_target_pairs={{0,16},{4,12},{8,24},{12,4},{16,0},{20,28},{24,8},{28,20},{1,17},{... | collective-permute-start | bytes 983048 | tf_op jit(solution)/shard_map/ppermute | solution.py:30
  48.5 3.9 %collective-permute-done.8.refs_16_.refs_9_ = bf16[640,256]{1,0:T(8,128)(2,1)S(1)} collective-permute-done((bf16[640,256]{1,0:T(8,128)(2,1)S(1)}, bf16[640,256]{1,0:T(8,128)(2,1)S(1)}, u32[]{:S(2)}, u32[]{:S(2)}) %collective-permute-start.8) | collective-permute-done | bytes 327712 | tf_op jit(solution)/shard_map/ppermute | solution.py:30
  52.4 1.5 %collective-permute-start.9 = (bf16[640,256]{1,0:T(8,128)(2,1)S(1)}, bf16[640,256]{1,0:T(8,128)(2,1)S(1)}, u32[]{:S(2)}, u32[]{:S(2)}) collective-permute-start(bf16[640,256]{1,0:T(8,128)(2,1)S(1)} %collective-permute-done.7.refs_15_.refs_8_), channel_id=1, source_target_pairs={{0,16},{4,12},{8,24},{12,4},{16,0},{20,28},{24,8},{28,20},{1,17},{... | collective-permute-start | bytes 983048 | tf_op jit(solution)/shard_map/ppermute | solution.py:30
  53.9 2.0 %collective-permute-done.16.refs_24_.refs_17_ = bf16[640,256]{1,0:T(8,128)(2,1)S(1)} collective-permute-done((bf16[640,256]{1,0:T(8,128)(2,1)S(1)}, bf16[640,256]{1,0:T(8,128)(2,1)S(1)}, u32[]{:S(2)}, u32[]{:S(2)}) %collective-permute-start.16) | collective-permute-done | bytes 327712 | tf_op jit(solution)/shard_map/ppermute | solution.py:30
  55.9 1.5 %collective-permute-start.17 = (bf16[640,256]{1,0:T(8,128)(2,1)S(1)}, bf16[640,256]{1,0:T(8,128)(2,1)S(1)}, u32[]{:S(2)}, u32[]{:S(2)}) collective-permute-start(bf16[640,256]{1,0:T(8,128)(2,1)S(1)} %collective-permute-done.15.refs_23_.refs_16_), channel_id=1, source_target_pairs={{0,16},{4,12},{8,24},{12,4},{16,0},{20,28},{24,8},{28,20},{1,17},{... | collective-permute-start | bytes 983048 | tf_op jit(solution)/shard_map/ppermute | solution.py:30
  57.4 0.5 collective-permute-start.12
  58.0 0.0 collective-permute-done.18.refs_26_.refs_19_
  58.0 1.6 %collective-permute-start.22 = (bf16[640,256]{1,0:T(8,128)(2,1)S(1)}, bf16[640,256]{1,0:T(8,128)(2,1)S(1)}, u32[]{:S(2)}, u32[]{:S(2)}) collective-permute-start(bf16[640,256]{1,0:T(8,128)(2,1)S(1)} %shard_map.84), channel_id=1, source_target_pairs={{0,8},{4,20},{8,0},{12,28},{16,24},{20,4},{24,16},{28,12},{1,9},{5... | collective-permute-start | bytes 983048 | tf_op jit(solution)/shard_map/ppermute | solution.py:30
  59.5 5.7 %collective-permute-done.17.refs_25_.refs_18_ = bf16[640,256]{1,0:T(8,128)(2,1)S(1)} collective-permute-done((bf16[640,256]{1,0:T(8,128)(2,1)S(1)}, bf16[640,256]{1,0:T(8,128)(2,1)S(1)}, u32[]{:S(2)}, u32[]{:S(2)}) %collective-permute-start.17) | collective-permute-done | bytes 327712 | tf_op jit(solution)/shard_map/ppermute | solution.py:30
  65.3 0.5 collective-permute-start.20
  65.8 2.3 %collective-permute-start.23 = (bf16[640,256]{1,0:T(8,128)(2,1)S(1)}, bf16[640,256]{1,0:T(8,128)(2,1)S(1)}, u32[]{:S(2)}, u32[]{:S(2)}) collective-permute-start(bf16[640,256]{1,0:T(8,128)(2,1)S(1)} %shard_map.84), channel_id=1, source_target_pairs={{0,16},{4,12},{8,24},{12,4},{16,0},{20,28},{24,8},{28,20},{1,17},{... | collective-permute-start | bytes 983048 | tf_op jit(solution)/shard_map/ppermute | solution.py:30
  68.1 0.1 collective-permute-start.24
  68.1 0.0 collective-permute-done.19.refs_27_.refs_20_
  68.1 0.0 collective-permute-start.13
  68.2 0.0 collective-permute-done.20.refs_28_.refs_21_
  68.2 0.5 collective-permute-start.21
  68.7 4.5 %collective-permute-done.23.refs_25_ = bf16[640,256]{1,0:T(8,128)(2,1)S(1)} collective-permute-done((bf16[640,256]{1,0:T(8,128)(2,1)S(1)}, bf16[640,256]{1,0:T(8,128)(2,1)S(1)}, u32[]{:S(2)}, u32[]{:S(2)}) %collective-permute-start.23) | collective-permute-done | bytes 327712 | tf_op jit(solution)/shard_map/ppermute | solution.py:30
  73.1 0.5 collective-permute-start.26
  73.6 3.0 %collective-permute-done.24.refs_26_ = bf16[640,256]{1,0:T(8,128)(2,1)S(1)} collective-permute-done((bf16[640,256]{1,0:T(8,128)(2,1)S(1)}, bf16[640,256]{1,0:T(8,128)(2,1)S(1)}, u32[]{:S(2)}, u32[]{:S(2)}) %collective-permute-start.24) | collective-permute-done | bytes 327712 | tf_op jit(solution)/shard_map/ppermute | solution.py:30
  76.6 0.4 fusion
  77.1 0.0 copy-start.1
  77.1 0.0 copy-start.7
  77.1 2.9 %first.1 = (bf16[8,320,256]{2,1,0:T(8,128)(2,1)S(1)}, bf16[3,256,256]{2,1,0:T(8,128)(2,1)S(1)}, bf16[3,320,128]{2,1,0:T(8,128)(2,1)S(1)}) custom-call(bf16[1024,512]{1,0:T(8,128)(2,1)S(1)} %copy-done.2, f32[8,1,256]{2,1,0:T(1,128)S(1)} %bitcast.7, f32[192,128]{1,0:T(8,128)S(1)} %get-tuple-element.15.refs_2_.refs_3_, ...), custom_call_target="tpu_custom_call" | custom-call | tf_op jit(solution)/shard_map/first/pallas_call | solution.py:449
  80.1 4.8 %main.1 = bf16[256,2048]{1,0:T(8,128)(2,1)} custom-call(bf16[8,320,256]{2,1,0:T(8,128)(2,1)S(1)} %get-tuple-element.8.refs_0_, bf16[3,256,256]{2,1,0:T(8,128)(2,1)S(1)} %get-tuple-element.9.refs_1_, bf16[3,320,128]{2,1,0:T(8,128)(2,1)S(1)} %get-tuple-element.10.refs_2_, f32[192,128]{1,0:T(8,128)S(1)} %get-tuple-element.15.refs_2_.refs_3_, ...), custom_call_target="tpu_custom_call" | custom-call | tf_op jit(solution)/shard_map/main/pallas_call | solution.py:475
  (33 shorter events, 0.1 us)
Async XLA Ops:
  0.0 7.1 %copy-start.2 = (bf16[1024,512]{1,0:T(8,128)(2,1)S(1)}, bf16[1024,512]{1,0:T(8,128)(2,1)}, u32[]{:S(2)}) copy-start(bf16[1024,512]{1,0:T(8,128)(2,1)} %refs_0_.1) | copy-start | bytes 3145732
  1.8 5.4 %copy-start.3 = (bf16[704,256]{1,0:T(8,128)(2,1)S(1)}, bf16[704,256]{1,0:T(8,128)(2,1)}, u32[]{:S(2)}) copy-start(bf16[704,256]{1,0:T(8,128)(2,1)} %cut.1.refs_4_) | copy-start | bytes 1081348
  1.9 14.7 %collective-permute-start.1 = (bf16[704,256]{1,0:T(8,128)(2,1)}, bf16[704,256]{1,0:T(8,128)(2,1)S(1)}, u32[]{:S(2)}, u32[]{:S(2)}) collective-permute-start(bf16[704,256]{1,0:T(8,128)(2,1)} %cut.1.refs_4_), channel_id=1, source_target_pairs={{0,1},{1,2},{2,3},{3,0},{4,5},{5,6},{6,7},{7,4},{8,9},{9,10},{10,1... | collective-permute-start | bytes 1081352 | tf_op jit(solution)/shard_map/ppermute | solution.py:19
  5.0 18.0 %collective-permute-start.14 = (bf16[704,256]{1,0:T(8,128)(2,1)}, bf16[704,256]{1,0:T(8,128)(2,1)S(1)}, u32[]{:S(2)}, u32[]{:S(2)}) collective-permute-start(bf16[704,256]{1,0:T(8,128)(2,1)} %cut.1.refs_4_), channel_id=1, source_target_pairs={{0,3},{1,0},{2,1},{3,2},{4,7},{5,4},{6,5},{7,6},{8,11},{9,8},{10,9... | collective-permute-start | bytes 1081352 | tf_op jit(solution)/shard_map/ppermute | solution.py:19
  7.1 69.9 %copy-start = (bf16[2048,256]{1,0:T(8,128)(2,1)S(1)}, bf16[2048,256]{1,0:T(8,128)(2,1)}, u32[]{:S(2)}) copy-start(bf16[2048,256]{1,0:T(8,128)(2,1)} %refs_8_.1) | copy-start | bytes 3145732
  7.1 69.9 %copy-start.4 = (bf16[2048,64]{0,1:T(8,128)(2,1)S(1)}, bf16[2048,64]{0,1:T(8,128)(2,1)}, u32[]{:S(2)}) copy-start(bf16[2048,64]{0,1:T(8,128)(2,1)} %param.12) | copy-start | bytes 786436
  7.1 69.9 %copy-start.5 = (bf16[2048,64]{0,1:T(8,128)(2,1)S(1)}, bf16[2048,64]{0,1:T(8,128)(2,1)}, u32[]{:S(2)}) copy-start(bf16[2048,64]{0,1:T(8,128)(2,1)} %param.13) | copy-start | bytes 786436
  7.2 69.9 %copy-start.6 = (f32[2048]{0:T(1024)S(1)}, f32[2048]{0:T(1024)}, u32[]{:S(2)}) copy-start(f32[2048]{0:T(1024)} %param.10) | copy-start | bytes 24580
  7.2 21.9 %collective-permute-start.4 = (bf16[256,512]{1,0:T(8,128)(2,1)S(1)}, bf16[256,512]{1,0:T(8,128)(2,1)S(1)}, u32[]{:S(2)}, u32[]{:S(2)}) collective-permute-start(bf16[256,512]{1,0:T(8,128)(2,1)S(1)} %get-tuple-element.13), channel_id=1, source_target_pairs={{0,1},{1,2},{2,3},{3,0},{4,5},{5,6},{6,7},{7,4},{8,9},{9,10},{10,1... | collective-permute-start | bytes 786440 | tf_op jit(solution)/shard_map/ppermute | solution.py:19
  7.2 38.0 %collective-permute-start = (bf16[704,256]{1,0:T(8,128)(2,1)S(1)}, bf16[704,256]{1,0:T(8,128)(2,1)S(1)}, u32[]{:S(2)}, u32[]{:S(2)}) collective-permute-start(bf16[704,256]{1,0:T(8,128)(2,1)S(1)} %copy-done.3), channel_id=1, source_target_pairs={{0,4},{4,0},{1,5},{5,1},{2,6},{6,2},{3,7},{7,3},{8,12},{12,8},{9,1... | collective-permute-start | bytes 1081352 | tf_op jit(solution)/shard_map/ppermute | solution.py:24
  16.5 30.3 %collective-permute-start.7 = (bf16[640,256]{1,0:T(8,128)(2,1)S(1)}, bf16[640,256]{1,0:T(8,128)(2,1)S(1)}, u32[]{:S(2)}, u32[]{:S(2)}) collective-permute-start(bf16[640,256]{1,0:T(8,128)(2,1)S(1)} %shard_map.82), channel_id=1, source_target_pairs={{0,8},{4,20},{8,0},{12,28},{16,24},{20,4},{24,16},{28,12},{1,9},{5... | collective-permute-start | bytes 983048 | tf_op jit(solution)/shard_map/ppermute | solution.py:30
  23.0 23.9 %collective-permute-start.15 = (bf16[640,256]{1,0:T(8,128)(2,1)S(1)}, bf16[640,256]{1,0:T(8,128)(2,1)S(1)}, u32[]{:S(2)}, u32[]{:S(2)}) collective-permute-start(bf16[640,256]{1,0:T(8,128)(2,1)S(1)} %shard_map.83), channel_id=1, source_target_pairs={{0,8},{4,20},{8,0},{12,28},{16,24},{20,4},{24,16},{28,12},{1,9},{5... | collective-permute-start | bytes 983048 | tf_op jit(solution)/shard_map/ppermute | solution.py:30
  24.8 15.5 %collective-permute-start.5 = (bf16[256,512]{1,0:T(8,128)(2,1)S(1)}, bf16[256,512]{1,0:T(8,128)(2,1)S(1)}, u32[]{:S(2)}, u32[]{:S(2)}) collective-permute-start(bf16[256,512]{1,0:T(8,128)(2,1)S(1)} %get-tuple-element.12), channel_id=1, source_target_pairs={{0,2},{1,3},{2,0},{3,1},{4,6},{5,7},{6,4},{7,5},{8,10},{9,11},{10,... | collective-permute-start | bytes 786440 | tf_op jit(solution)/shard_map/ppermute | solution.py:19
  29.1 16.1 %collective-permute-start.6 = (bf16[256,512]{1,0:T(8,128)(2,1)S(1)}, bf16[256,512]{1,0:T(8,128)(2,1)S(1)}, u32[]{:S(2)}, u32[]{:S(2)}) collective-permute-start(bf16[256,512]{1,0:T(8,128)(2,1)S(1)} %get-tuple-element.11), channel_id=1, source_target_pairs={{0,3},{1,0},{2,1},{3,2},{4,7},{5,4},{6,5},{7,6},{8,11},{9,8},{10,9... | collective-permute-start | bytes 786440 | tf_op jit(solution)/shard_map/ppermute | solution.py:19
  40.3 17.1 %collective-permute-start.2 = (bf16[704,256]{1,0:T(8,128)(2,1)S(1)}, bf16[704,256]{1,0:T(8,128)(2,1)S(1)}, u32[]{:S(2)}, u32[]{:S(2)}) collective-permute-start(bf16[704,256]{1,0:T(8,128)(2,1)S(1)} %collective-permute-done.1.refs_0_.refs_14_.refs_7_), channel_id=1, source_target_pairs={{0,1},{1,2},{2,3},{3,0},{4,5},{5,6},{6,7},{7,4},{8,9},{9,10},{10,1... | collective-permute-start | bytes 1081352 | tf_op jit(solution)/shard_map/ppermute | solution.py:19
  45.2 12.2 %collective-permute-start.10 = (bf16[704,256]{1,0:T(8,128)(2,1)S(1)}, bf16[704,256]{1,0:T(8,128)(2,1)S(1)}, u32[]{:S(2)}, u32[]{:S(2)}) collective-permute-start(bf16[704,256]{1,0:T(8,128)(2,1)S(1)} %collective-permute-done.1.refs_0_.refs_14_.refs_7_), channel_id=1, source_target_pairs={{0,4},{4,0},{1,5},{5,1},{2,6},{6,2},{3,7},{7,3},{8,12},{12,8},{9,1... | collective-permute-start | bytes 1081352 | tf_op jit(solution)/shard_map/ppermute | solution.py:24
  45.2 7.1 %collective-permute-start.8 = (bf16[640,256]{1,0:T(8,128)(2,1)S(1)}, bf16[640,256]{1,0:T(8,128)(2,1)S(1)}, u32[]{:S(2)}, u32[]{:S(2)}) collective-permute-start(bf16[640,256]{1,0:T(8,128)(2,1)S(1)} %shard_map.82), channel_id=1, source_target_pairs={{0,16},{4,12},{8,24},{12,4},{16,0},{20,28},{24,8},{28,20},{1,17},{... | collective-permute-start | bytes 983048 | tf_op jit(solution)/shard_map/ppermute | solution.py:30
  46.8 11.1 %collective-permute-start.18 = (bf16[704,256]{1,0:T(8,128)(2,1)S(1)}, bf16[704,256]{1,0:T(8,128)(2,1)S(1)}, u32[]{:S(2)}, u32[]{:S(2)}) collective-permute-start(bf16[704,256]{1,0:T(8,128)(2,1)S(1)} %collective-permute-done.14.refs_0_.refs_22_.refs_15_), channel_id=1, source_target_pairs={{0,4},{4,0},{1,5},{5,1},{2,6},{6,2},{3,7},{7,3},{8,12},{12,8},{9,1... | collective-permute-start | bytes 1081352 | tf_op jit(solution)/shard_map/ppermute | solution.py:24
  47.0 8.9 %collective-permute-start.16 = (bf16[640,256]{1,0:T(8,128)(2,1)S(1)}, bf16[640,256]{1,0:T(8,128)(2,1)S(1)}, u32[]{:S(2)}, u32[]{:S(2)}) collective-permute-start(bf16[640,256]{1,0:T(8,128)(2,1)S(1)} %shard_map.83), channel_id=1, source_target_pairs={{0,16},{4,12},{8,24},{12,4},{16,0},{20,28},{24,8},{28,20},{1,17},{... | collective-permute-start | bytes 983048 | tf_op jit(solution)/shard_map/ppermute | solution.py:30
  52.4 7.1 %collective-permute-start.9 = (bf16[640,256]{1,0:T(8,128)(2,1)S(1)}, bf16[640,256]{1,0:T(8,128)(2,1)S(1)}, u32[]{:S(2)}, u32[]{:S(2)}) collective-permute-start(bf16[640,256]{1,0:T(8,128)(2,1)S(1)} %collective-permute-done.7.refs_15_.refs_8_), channel_id=1, source_target_pairs={{0,16},{4,12},{8,24},{12,4},{16,0},{20,28},{24,8},{28,20},{1,17},{... | collective-permute-start | bytes 983048 | tf_op jit(solution)/shard_map/ppermute | solution.py:30
  55.9 9.3 %collective-permute-start.17 = (bf16[640,256]{1,0:T(8,128)(2,1)S(1)}, bf16[640,256]{1,0:T(8,128)(2,1)S(1)}, u32[]{:S(2)}, u32[]{:S(2)}) collective-permute-start(bf16[640,256]{1,0:T(8,128)(2,1)S(1)} %collective-permute-done.15.refs_23_.refs_16_), channel_id=1, source_target_pairs={{0,16},{4,12},{8,24},{12,4},{16,0},{20,28},{24,8},{28,20},{1,17},{... | collective-permute-start | bytes 983048 | tf_op jit(solution)/shard_map/ppermute | solution.py:30
  57.4 7.8 %collective-permute-start.11 = (bf16[640,256]{1,0:T(8,128)(2,1)S(1)}, bf16[640,256]{1,0:T(8,128)(2,1)S(1)}, u32[]{:S(2)}, u32[]{:S(2)}) collective-permute-start(bf16[640,256]{1,0:T(8,128)(2,1)S(1)} %collective-permute-done.7.refs_15_.refs_8_), channel_id=1, source_target_pairs={{0,4},{4,0},{1,5},{5,1},{2,6},{6,2},{3,7},{7,3},{8,12},{12,8},{9,1... | collective-permute-start | bytes 983048 | tf_op jit(solution)/shard_map/ppermute | solution.py:24
  57.4 8.3 %collective-permute-start.12 = (bf16[640,256]{1,0:T(8,128)(2,1)S(1)}, bf16[640,256]{1,0:T(8,128)(2,1)S(1)}, u32[]{:S(2)}, u32[]{:S(2)}) collective-permute-start(bf16[640,256]{1,0:T(8,128)(2,1)S(1)} %collective-permute-done.8.refs_16_.refs_9_), channel_id=1, source_target_pairs={{0,4},{4,0},{1,5},{5,1},{2,6},{6,2},{3,7},{7,3},{8,12},{12,8},{9,1... | collective-permute-start | bytes 983048 | tf_op jit(solution)/shard_map/ppermute | solution.py:24
  58.0 10.1 %collective-permute-start.22 = (bf16[640,256]{1,0:T(8,128)(2,1)S(1)}, bf16[640,256]{1,0:T(8,128)(2,1)S(1)}, u32[]{:S(2)}, u32[]{:S(2)}) collective-permute-start(bf16[640,256]{1,0:T(8,128)(2,1)S(1)} %shard_map.84), channel_id=1, source_target_pairs={{0,8},{4,20},{8,0},{12,28},{16,24},{20,4},{24,16},{28,12},{1,9},{5... | collective-permute-start | bytes 983048 | tf_op jit(solution)/shard_map/ppermute | solution.py:30
  59.5 13.6 %collective-permute-start.3 = (bf16[704,256]{1,0:T(8,128)(2,1)S(1)}, bf16[704,256]{1,0:T(8,128)(2,1)S(1)}, u32[]{:S(2)}, u32[]{:S(2)}) collective-permute-start(bf16[704,256]{1,0:T(8,128)(2,1)S(1)} %collective-permute-done.2.refs_6_.refs_0_.refs_23_), channel_id=1, source_target_pairs={{0,4},{4,0},{1,5},{5,1},{2,6},{6,2},{3,7},{7,3},{8,12},{12,8},{9,1... | collective-permute-start | bytes 1081352 | tf_op jit(solution)/shard_map/ppermute | solution.py:24
  65.2 2.9 %collective-permute-start.19 = (bf16[640,256]{1,0:T(8,128)(2,1)S(1)}, bf16[640,256]{1,0:T(8,128)(2,1)S(1)}, u32[]{:S(2)}, u32[]{:S(2)}) collective-permute-start(bf16[640,256]{1,0:T(8,128)(2,1)S(1)} %collective-permute-done.15.refs_23_.refs_16_), channel_id=1, source_target_pairs={{0,4},{4,0},{1,5},{5,1},{2,6},{6,2},{3,7},{7,3},{8,12},{12,8},{9,1... | collective-permute-start | bytes 983048 | tf_op jit(solution)/shard_map/ppermute | solution.py:24
  65.3 2.9 %collective-permute-start.20 = (bf16[640,256]{1,0:T(8,128)(2,1)S(1)}, bf16[640,256]{1,0:T(8,128)(2,1)S(1)}, u32[]{:S(2)}, u32[]{:S(2)}) collective-permute-start(bf16[640,256]{1,0:T(8,128)(2,1)S(1)} %collective-permute-done.16.refs_24_.refs_17_), channel_id=1, source_target_pairs={{0,4},{4,0},{1,5},{5,1},{2,6},{6,2},{3,7},{7,3},{8,12},{12,8},{9,1... | collective-permute-start | bytes 983048 | tf_op jit(solution)/shard_map/ppermute | solution.py:24
  65.8 7.4 %collective-permute-start.23 = (bf16[640,256]{1,0:T(8,128)(2,1)S(1)}, bf16[640,256]{1,0:T(8,128)(2,1)S(1)}, u32[]{:S(2)}, u32[]{:S(2)}) collective-permute-start(bf16[640,256]{1,0:T(8,128)(2,1)S(1)} %shard_map.84), channel_id=1, source_target_pairs={{0,16},{4,12},{8,24},{12,4},{16,0},{20,28},{24,8},{28,20},{1,17},{... | collective-permute-start | bytes 983048 | tf_op jit(solution)/shard_map/ppermute | solution.py:30
  68.1 8.6 %collective-permute-start.24 = (bf16[640,256]{1,0:T(8,128)(2,1)S(1)}, bf16[640,256]{1,0:T(8,128)(2,1)S(1)}, u32[]{:S(2)}, u32[]{:S(2)}) collective-permute-start(bf16[640,256]{1,0:T(8,128)(2,1)S(1)} %collective-permute-done.22.refs_24_), channel_id=1, source_target_pairs={{0,16},{4,12},{8,24},{12,4},{16,0},{20,28},{24,8},{28,20},{1,17},{... | collective-permute-start | bytes 983048 | tf_op jit(solution)/shard_map/ppermute | solution.py:30
  68.1 8.9 %collective-permute-start.13 = (bf16[640,256]{1,0:T(8,128)(2,1)S(1)}, bf16[640,256]{1,0:T(8,128)(2,1)S(1)}, u32[]{:S(2)}, u32[]{:S(2)}) collective-permute-start(bf16[640,256]{1,0:T(8,128)(2,1)S(1)} %collective-permute-done.9.refs_17_.refs_10_), channel_id=1, source_target_pairs={{0,4},{4,0},{1,5},{5,1},{2,6},{6,2},{3,7},{7,3},{8,12},{12,8},{9,1... | collective-permute-start | bytes 983048 | tf_op jit(solution)/shard_map/ppermute | solution.py:24
  68.2 8.9 %collective-permute-start.21 = (bf16[640,256]{1,0:T(8,128)(2,1)S(1)}, bf16[640,256]{1,0:T(8,128)(2,1)S(1)}, u32[]{:S(2)}, u32[]{:S(2)}) collective-permute-start(bf16[640,256]{1,0:T(8,128)(2,1)S(1)} %collective-permute-done.17.refs_25_.refs_18_), channel_id=1, source_target_pairs={{0,4},{4,0},{1,5},{5,1},{2,6},{6,2},{3,7},{7,3},{8,12},{12,8},{9,1... | collective-permute-start | bytes 983048 | tf_op jit(solution)/shard_map/ppermute | solution.py:24
  73.1 6.9 %collective-permute-start.25 = (bf16[640,256]{1,0:T(8,128)(2,1)S(1)}, bf16[640,256]{1,0:T(8,128)(2,1)S(1)}, u32[]{:S(2)}, u32[]{:S(2)}) collective-permute-start(bf16[640,256]{1,0:T(8,128)(2,1)S(1)} %collective-permute-done.22.refs_24_), channel_id=1, source_target_pairs={{0,4},{4,0},{1,5},{5,1},{2,6},{6,2},{3,7},{7,3},{8,12},{12,8},{9,1... | collective-permute-start | bytes 983048 | tf_op jit(solution)/shard_map/ppermute | solution.py:24
  73.1 6.9 %collective-permute-start.26 = (bf16[640,256]{1,0:T(8,128)(2,1)S(1)}, bf16[640,256]{1,0:T(8,128)(2,1)S(1)}, u32[]{:S(2)}, u32[]{:S(2)}) collective-permute-start(bf16[640,256]{1,0:T(8,128)(2,1)S(1)} %collective-permute-done.23.refs_25_), channel_id=1, source_target_pairs={{0,4},{4,0},{1,5},{5,1},{2,6},{6,2},{3,7},{7,3},{8,12},{12,8},{9,1... | collective-permute-start | bytes 983048 | tf_op jit(solution)/shard_map/ppermute | solution.py:24
  76.6 3.4 %collective-permute-start.27 = (bf16[640,256]{1,0:T(8,128)(2,1)S(1)}, bf16[640,256]{1,0:T(8,128)(2,1)S(1)}, u32[]{:S(2)}, u32[]{:S(2)}) collective-permute-start(bf16[640,256]{1,0:T(8,128)(2,1)S(1)} %collective-permute-done.24.refs_26_), channel_id=1, source_target_pairs={{0,4},{4,0},{1,5},{5,1},{2,6},{6,2},{3,7},{7,3},{8,12},{12,8},{9,1... | collective-permute-start | bytes 983048 | tf_op jit(solution)/shard_map/ppermute | solution.py:24
  77.1 3.0 %copy-start.1 = (bf16[256,2048]{1,0:T(8,128)(2,1)S(1)}, bf16[256,2048]{1,0:T(8,128)(2,1)}, u32[]{:S(2)}) copy-start(bf16[256,2048]{1,0:T(8,128)(2,1)} %refs_6_.1) | copy-start | bytes 3145732
  77.1 3.0 %copy-start.7 = (s32[8]{0:T(128)S(1)}, s32[8]{0:T(128)}, u32[]{:S(2)}) copy-start(s32[8]{0:T(128)} %refs_5_.1) | copy-start | bytes 100

commit v2 on v1

--- a/solution.py
+++ b/solution.py
@@ -103,19 +103,20 @@
     return [(row, prefix_len, 0, parity * size)]
 
 
-def cut_kernel(dims, q_ref, out_ref, k_ref, v_ref, p_ref, o_ref, sems):
+def cut_kernel(dims, q_ref, out_ref, k_ref, v_ref, p_ref, o_ref, held, sems, out_sems):
     prefix_rows, prefix_len, width = dims
     size, head = o_ref.shape[1], out_ref.shape[0]
     share = k_ref.shape[0]
     parity = lax.rem(lax.axis_index("cand"), 2)
     part = (lax.axis_index("query") * 2 + parity) * size
     at = pl.ds(pl.multiple_of(part, size), size)
-    copies = []
+    copies, outs = [], []
 
     def copy(src, row, count):
-        copies.append(
-            pltpu.make_async_copy(src, o_ref.at[pl.ds(row, count), :], sems.at[len(copies)])
-        )
+        i = len(copies)
+        spot = pl.ds(row, count)
+        copies.append(pltpu.make_async_copy(src, held.at[spot, :], sems.at[i]))
+        outs.append(pltpu.make_async_copy(held.at[spot, :], o_ref.at[spot, :], out_sems.at[i]))
 
     half, half_head = size // 2, head // 2
     for i in range(2):
@@ -131,8 +132,11 @@
         copy(p_ref.at[pl.ds(start, count), lanes], row, count)
     for c in copies:
         c.start()
-    for c in copies:
+    for c, out in zip(copies, outs):
         c.wait()
+        out.start()
+    for out in outs:
+        out.wait()
 
 
 def rotary_tables(count, half, head_size):
@@ -304,12 +308,48 @@
                 store(k, made, at, rows // 2)
 
 
+def late(count):
+    return (count // 2 - 1, count - 1)
+
+
+def second_kernel(dims, rounds, plan, *refs):
+    n, rows, _, _, _, _, head, _ = dims
+    share2 = 2 * (head // n)
+    normed, piece_refs, q_ref, kv_ref = refs[0], refs[1:-2], refs[-2], refs[-1]
+    me = lax.axis_index("tensor")
+    parity = lax.rem(lax.axis_index("cand"), 2)
+    size = normed.shape[2]
+    _, parts = places(rounds, plan, lax.axis_index("query"), me, parity)
+    parts = [part for i, part in enumerate(parts) if i not in late(len(plan))]
+    kv_ref[...] = add_up(
+        [
+            lax.dot_general(
+                normed[part],
+                ref[pl.ds(size + head, share2), :],
+                TRANS,
+                preferred_element_type=jnp.float32,
+            )
+            for part, ref in zip(parts, piece_refs)
+        ]
+    )
+    q_ref[...] = add_up(
+        [
+            jnp.dot(
+                normed[part, pl.ds(0, rows), :],
+                ref[pl.ds(0, size), :],
+                preferred_element_type=jnp.float32,
+            )
+            for part, ref in zip(parts, piece_refs)
+        ]
+    )
+
+
 def last_kernel(dims, rounds, plan, *refs):
     n, rows, cand_len, _, prefix_len, _, head, _ = dims
     n_pieces = len(plan)
-    normed, q_in, kv_in, cos_ref, sin_ref, len_ref, own_out = refs[:7]
-    n_in = 7 + (n - 1) * n_pieces
-    piece_refs = refs[7:n_in]
+    normed, q_in, kv_in, cos_ref, sin_ref, len_ref, own_out, q_part, kv_part = refs[:9]
+    n_in = 9 + (n - 1) * n_pieces
+    piece_refs = refs[9:n_in]
     o_ref = refs[n_in]
     w_out, kv_scr, heads, sem = refs[n_in + 1 :]
     me = lax.axis_index("tensor")
@@ -327,28 +367,28 @@
     all_cos = jnp.concatenate([cand_cos, cos[:prefix_len]], axis=0)
     all_sin = jnp.concatenate([cand_sin, sin[:prefix_len]], axis=0)
 
-    last = pieces[-1]
-    made = add_up(
+    last = [(parts[i], pieces[-1][i]) for i in late(n_pieces)]
+    made = kv_part[...] + add_up(
         [
             lax.dot_general(
                 normed[part],
-                last[i][pl.ds(size + head, 2 * share), :],
+                ref[pl.ds(size + head, 2 * share), :],
                 TRANS,
                 preferred_element_type=jnp.float32,
             )
-            for i, part in enumerate(parts)
+            for part, ref in last
         ]
     )
     for k, source in enumerate([me] + sources):
         kv_scr[source] = kv_in[k] if k < n - 1 else made.astype(jnp.bfloat16)
-    made = add_up(
+    made = q_part[...] + add_up(
         [
             jnp.dot(
                 normed[part, pl.ds(0, rows), :],
-                last[i][pl.ds(0, size), :],
+                ref[pl.ds(0, size), :],
                 preferred_element_type=jnp.float32,
             )
-            for i, part in enumerate(parts)
+            for part, ref in last
         ]
     )
     lower, upper = rotated(made[:, :half], made[:, half:], cand_cos, cand_sin)
@@ -361,24 +401,30 @@
     keys = jnp.concatenate(rotated(low, up, all_cos, all_sin), axis=1).astype(jnp.bfloat16)
     values = jnp.concatenate([p[:, share:] for p in shares], axis=1)
 
-    tall = (n, cand_len, cand_len + prefix_len)
-    slot = lax.broadcasted_iota(jnp.int32, tall, 1).reshape(n * cand_len, tall[2])
-    other = lax.broadcasted_iota(jnp.int32, tall, 2).reshape(n * cand_len, tall[2])
+    group = min(2, n)
+    tall = (group, cand_len, cand_len + prefix_len)
+    slot = lax.broadcasted_iota(jnp.int32, tall, 1).reshape(group * cand_len, tall[2])
+    other = lax.broadcasted_iota(jnp.int32, tall, 2).reshape(group * cand_len, tall[2])
     seen = (slot >= other) | (other >= cand_len)
     for j in range(rows // cand_len):
         own = slice(j * cand_len, (j + 1) * cand_len)
         live = slot[:, :1] < len_ref[me * (rows // cand_len) + j]
         keys_j = jnp.concatenate([keys[own], keys[rows:]], axis=0)
         values_j = jnp.concatenate([values[own], values[rows:]], axis=0)
-        queries = jnp.concatenate([q_in[k, own, :] for k in range(n - 1)] + [last_q[own]], axis=0)
-        scores = lax.dot_general(queries, keys_j, TRANS, preferred_element_type=jnp.float32)
-        scores = jnp.where(seen, scores, -jnp.inf)
-        weights = jnp.exp(scores - scores.max(-1, keepdims=True))
-        divisor = weights.sum(-1, keepdims=True)
-        mix = jnp.dot(weights.astype(jnp.bfloat16), values_j, preferred_element_type=jnp.float32)
-        mix = (mix * jnp.where(live, 1.0 / divisor, 0.0)).astype(jnp.bfloat16)
-        for k in range(n):
-            heads[k, own, :] = mix[k * cand_len : (k + 1) * cand_len]
+        for g in range(0, n, group):
+            heads_g = range(g, g + group)
+            queries = [q_in[k, own, :] if k < n - 1 else last_q[own] for k in heads_g]
+            queries = jnp.concatenate(queries, axis=0) if group > 1 else queries[0]
+            scores = lax.dot_general(queries, keys_j, TRANS, preferred_element_type=jnp.float32)
+            scores = jnp.where(seen, scores, -jnp.inf)
+            weights = jnp.exp(scores - scores.max(-1, keepdims=True))
+            divisor = weights.sum(-1, keepdims=True)
+            mix = jnp.dot(
+                weights.astype(jnp.bfloat16), values_j, preferred_element_type=jnp.float32
+            )
+            mix = (mix * jnp.where(live, 1.0 / divisor, 0.0)).astype(jnp.bfloat16)
+            for at, k in enumerate(heads_g):
+                heads[k, own, :] = mix[at * cand_len : (at + 1) * cand_len]
 
     c.wait()
     for i in range(0, n_pieces, 2):
@@ -426,8 +472,12 @@
         name="cut",
         out_shape=jax.ShapeDtypeStruct((height + tail, size), jnp.bfloat16),
         in_specs=[any_spec] * 5,
-        out_specs=vmem,
-        scratch_shapes=[pltpu.SemaphoreType.DMA((8,))],
+        out_specs=any_spec,
+        scratch_shapes=[
+            pltpu.VMEM((height + tail, size), jnp.bfloat16),
+            pltpu.SemaphoreType.DMA((8,)),
+            pltpu.SemaphoreType.DMA((8,)),
+        ],
         compiler_params=pltpu.CompilerParams(vmem_limit_bytes=60 * 2**20),
     )(w_query, w_out, key_t, value_t, near)
     moved = along_line(piece, height)
@@ -472,11 +522,22 @@
         piece, across, last[0], last[count // 2],
         w_query, key_t, value_t, *xs, *early,
     )
+    q_part, kv_part = pl.pallas_call(
+        functools.partial(second_kernel, dims, nearest(n), plan),
+        name="second",
+        out_shape=[
+            jax.ShapeDtypeStruct((rows, head), jnp.float32),
+            jax.ShapeDtypeStruct((every, 2 * share), jnp.float32),
+        ],
+        in_specs=[vmem] * (1 + count - 2),
+        out_specs=[vmem] * 2,
+        compiler_params=pltpu.CompilerParams(vmem_limit_bytes=16 * 2**20),
+    )(normed, *[v for i, v in enumerate(last) if i not in late(count)])
     return pl.pallas_call(
         functools.partial(last_kernel, dims, nearest(n), plan),
         name="main",
         out_shape=jax.ShapeDtypeStruct((rows, out_cols), jnp.bfloat16),
-        in_specs=[vmem] * 5 + [smem, hbm] + [vmem] * len(pieces),
+        in_specs=[vmem] * 5 + [smem, hbm] + [vmem] * (2 + len(pieces)),
         out_specs=vmem,
         scratch_shapes=[
             pltpu.VMEM((head, out_cols), jnp.bfloat16),
@@ -485,7 +546,7 @@
             pltpu.SemaphoreType.DMA,
         ],
         compiler_params=pltpu.CompilerParams(vmem_limit_bytes=24 * 2**20),
-    )(normed, queries, pairs, cos, sin, cand_lengths, w_out, *pieces)
+    )(normed, queries, pairs, cos, sin, cand_lengths, w_out, q_part, kv_part, *pieces)
 
 
 def solution(mesh):

time: 86.1 us -> 86.4 us (level)
  transfers between devices with their start and end apart: 28 -> 28, of which waited for: 9 -> 9; matrix products, arithmetic and copies ran while one was open for 1% -> 1% of each run, Pallas kernels for 3% -> 4%
where the time goes in v2:
time: 86.4 us; the launch traced here: 85.2 us
  waiting for transfers between devices  43.9 us (51%)
  starting transfers between devices  30.6 us (35%)
  Pallas kernels  9.39 us (11%)
    ppermute x6, waiting for transfers between devices, shift(): lax.ppermute(v, 'tensor', [(i, (i + k) % n) for i in range(n)])  24.8 us
    ppermute x9, waiting for transfers between devices, plane_xor(): return lambda v: lax.ppermute(v, PLANE, pairs)  19.1 us
    ppermute x6, starting transfers between devices, shift(): lax.ppermute(v, 'tensor', [(i, (i + k) % n) for i in range(n)])  14.7 us
    ppermute x9, starting transfers between devices, plane_xor(): return lambda v: lax.ppermute(v, PLANE, pairs)  13.6 us
    pallas_call x1, Pallas kernels, body(): pl.pallas_call(functools.partial(last_kernel, dims, nearest(n), plan), na...  3.99 us
    pallas_call x1, Pallas kernels, body(): pl.pallas_call(functools.partial(first_kernel, dims, nearest(n), plan), n...  2.9 us
    ppermute x13, starting transfers between devices, other_core(): return lax.ppermute(v, 'cand', [(i, i ^ 1) for i in range(n)])  2.24 us
    pallas_call x1, Pallas kernels, body(): pl.pallas_call(functools.partial(cut_kernel, (prefix_rows, prefix_len, ca...  1.81 us
  transfers between devices with their start and end apart: 28, of which 9 were waited for; matrix products, arithmetic and copies ran while one was open for 1% of the time, Pallas kernels for 4%

profile of v2, /device:TPU:0, one launch (start us, length us, event | category | flops | bytes accessed | tf_op | source)
XLA Modules:
  0.0 85.2 jit_solution(1672490739956546495)
XLA Ops:
  0.0 1.8 %cut.1.refs_4_ = bf16[704,256]{1,0:T(8,128)(2,1)} custom-call(bf16[2048,256]{1,0:T(8,128)(2,1)} %refs_8_.1, bf16[256,2048]{1,0:T(8,128)(2,1)} %refs_6_.1, bf16[64,2048]{1,0:T(8,128)(2,1)} %bitcast.3, bf16[64,2048]{1,0:T(8,128)(2,1)} %bitcast.5, bf16[32,512]{1,0:T(8,128)(2,1)} %p_ref.1), custom_call_target="tpu_custom_call" | custom-call | tf_op jit(solution)/shard_map/cut/pallas_call | solution.py:470
  1.8 0.0 copy-start.3
  1.8 3.1 %collective-permute-start.1 = (bf16[704,256]{1,0:T(8,128)(2,1)}, bf16[704,256]{1,0:T(8,128)(2,1)S(1)}, u32[]{:S(2)}, u32[]{:S(2)}) collective-permute-start(bf16[704,256]{1,0:T(8,128)(2,1)} %cut.1.refs_4_), channel_id=1, source_target_pairs={{0,1},{1,2},{2,3},{3,0},{4,5},{5,6},{6,7},{7,4},{8,9},{9,10},{10,1... | collective-permute-start | bytes 1081352 | tf_op jit(solution)/shard_map/ppermute | solution.py:19
  4.9 2.1 %collective-permute-start.14 = (bf16[704,256]{1,0:T(8,128)(2,1)}, bf16[704,256]{1,0:T(8,128)(2,1)S(1)}, u32[]{:S(2)}, u32[]{:S(2)}) collective-permute-start(bf16[704,256]{1,0:T(8,128)(2,1)} %cut.1.refs_4_), channel_id=1, source_target_pairs={{0,3},{1,0},{2,1},{3,2},{4,7},{5,4},{6,5},{7,6},{8,11},{9,8},{10,9... | collective-permute-start | bytes 1081352 | tf_op jit(solution)/shard_map/ppermute | solution.py:19
  7.0 0.1 constant_dynamic-slice_fusion
  7.1 0.0 copy-start
  7.1 0.0 copy-start.4
  7.1 0.0 copy-start.5
  7.1 0.0 copy-start.6
  7.2 0.1 collective-permute-start.4
  7.2 0.1 collective-permute-start
  7.3 9.2 %collective-permute-done.1.refs_0_.refs_14_.refs_9_ = bf16[704,256]{1,0:T(8,128)(2,1)S(1)} collective-permute-done((bf16[704,256]{1,0:T(8,128)(2,1)}, bf16[704,256]{1,0:T(8,128)(2,1)S(1)}, u32[]{:S(2)}, u32[]{:S(2)}) %collective-permute-start.1) | collective-permute-done | bytes 360480 | tf_op jit(solution)/shard_map/ppermute | solution.py:19
  16.5 1.8 %collective-permute-start.7 = (bf16[640,256]{1,0:T(8,128)(2,1)S(1)}, bf16[640,256]{1,0:T(8,128)(2,1)S(1)}, u32[]{:S(2)}, u32[]{:S(2)}) collective-permute-start(bf16[640,256]{1,0:T(8,128)(2,1)S(1)} %shard_map.82), channel_id=1, source_target_pairs={{0,8},{4,20},{8,0},{12,28},{16,24},{20,4},{24,16},{28,12},{1,9},{5... | collective-permute-start | bytes 983048 | tf_op jit(solution)/shard_map/ppermute | solution.py:30
  18.3 4.7 %collective-permute-done.14.refs_0_.refs_22_.refs_17_ = bf16[704,256]{1,0:T(8,128)(2,1)S(1)} collective-permute-done((bf16[704,256]{1,0:T(8,128)(2,1)}, bf16[704,256]{1,0:T(8,128)(2,1)S(1)}, u32[]{:S(2)}, u32[]{:S(2)}) %collective-permute-start.14) | collective-permute-done | bytes 360480 | tf_op jit(solution)/shard_map/ppermute | solution.py:19
  23.0 1.8 %collective-permute-start.15 = (bf16[640,256]{1,0:T(8,128)(2,1)S(1)}, bf16[640,256]{1,0:T(8,128)(2,1)S(1)}, u32[]{:S(2)}, u32[]{:S(2)}) collective-permute-start(bf16[640,256]{1,0:T(8,128)(2,1)S(1)} %shard_map.83), channel_id=1, source_target_pairs={{0,8},{4,20},{8,0},{12,28},{16,24},{20,4},{24,16},{28,12},{1,9},{5... | collective-permute-start | bytes 983048 | tf_op jit(solution)/shard_map/ppermute | solution.py:30
  24.8 2.6 %collective-permute-start.5 = (bf16[256,512]{1,0:T(8,128)(2,1)S(1)}, bf16[256,512]{1,0:T(8,128)(2,1)S(1)}, u32[]{:S(2)}, u32[]{:S(2)}) collective-permute-start(bf16[256,512]{1,0:T(8,128)(2,1)S(1)} %get-tuple-element.16), channel_id=1, source_target_pairs={{0,2},{1,3},{2,0},{3,1},{4,6},{5,7},{6,4},{7,5},{8,10},{9,11},{10,... | collective-permute-start | bytes 786440 | tf_op jit(solution)/shard_map/ppermute | solution.py:19
  27.4 1.7 %collective-permute-done.4.refs_11_ = bf16[256,512]{1,0:T(8,128)(2,1)S(1)} collective-permute-done((bf16[256,512]{1,0:T(8,128)(2,1)S(1)}, bf16[256,512]{1,0:T(8,128)(2,1)S(1)}, u32[]{:S(2)}, u32[]{:S(2)}) %collective-permute-start.4) | collective-permute-done | bytes 262176 | tf_op jit(solution)/shard_map/ppermute | solution.py:19
  29.1 2.0 %collective-permute-start.6 = (bf16[256,512]{1,0:T(8,128)(2,1)S(1)}, bf16[256,512]{1,0:T(8,128)(2,1)S(1)}, u32[]{:S(2)}, u32[]{:S(2)}) collective-permute-start(bf16[256,512]{1,0:T(8,128)(2,1)S(1)} %get-tuple-element.15), channel_id=1, source_target_pairs={{0,3},{1,0},{2,1},{3,2},{4,7},{5,4},{6,5},{7,6},{8,11},{9,8},{10,9... | collective-permute-start | bytes 786440 | tf_op jit(solution)/shard_map/ppermute | solution.py:19
  31.1 9.2 %collective-permute-done.5.refs_12_ = bf16[256,512]{1,0:T(8,128)(2,1)S(1)} collective-permute-done((bf16[256,512]{1,0:T(8,128)(2,1)S(1)}, bf16[256,512]{1,0:T(8,128)(2,1)S(1)}, u32[]{:S(2)}, u32[]{:S(2)}) %collective-permute-start.5) | collective-permute-done | bytes 262176 | tf_op jit(solution)/shard_map/ppermute | solution.py:19
  40.3 4.9 %collective-permute-start.2 = (bf16[704,256]{1,0:T(8,128)(2,1)S(1)}, bf16[704,256]{1,0:T(8,128)(2,1)S(1)}, u32[]{:S(2)}, u32[]{:S(2)}) collective-permute-start(bf16[704,256]{1,0:T(8,128)(2,1)S(1)} %collective-permute-done.1.refs_0_.refs_14_.refs_9_), channel_id=1, source_target_pairs={{0,1},{1,2},{2,3},{3,0},{4,5},{5,6},{6,7},{7,4},{8,9},{9,10},{10,1... | collective-permute-start | bytes 1081352 | tf_op jit(solution)/shard_map/ppermute | solution.py:19
  45.2 0.0 collective-permute-done.6.refs_13_
  45.2 1.6 %collective-permute-start.8 = (bf16[640,256]{1,0:T(8,128)(2,1)S(1)}, bf16[640,256]{1,0:T(8,128)(2,1)S(1)}, u32[]{:S(2)}, u32[]{:S(2)}) collective-permute-start(bf16[640,256]{1,0:T(8,128)(2,1)S(1)} %shard_map.82), channel_id=1, source_target_pairs={{0,16},{4,12},{8,24},{12,4},{16,0},{20,28},{24,8},{28,20},{1,17},{... | collective-permute-start | bytes 983048 | tf_op jit(solution)/shard_map/ppermute | solution.py:30
  46.8 0.0 collective-permute-done.7.refs_15_.refs_10_
  46.8 0.1 collective-permute-start.18
  47.0 0.0 collective-permute-done.15.refs_23_.refs_18_
  47.0 1.5 %collective-permute-start.16 = (bf16[640,256]{1,0:T(8,128)(2,1)S(1)}, bf16[640,256]{1,0:T(8,128)(2,1)S(1)}, u32[]{:S(2)}, u32[]{:S(2)}) collective-permute-start(bf16[640,256]{1,0:T(8,128)(2,1)S(1)} %shard_map.83), channel_id=1, source_target_pairs={{0,16},{4,12},{8,24},{12,4},{16,0},{20,28},{24,8},{28,20},{1,17},{... | collective-permute-start | bytes 983048 | tf_op jit(solution)/shard_map/ppermute | solution.py:30
  48.5 3.9 %collective-permute-done.8.refs_16_.refs_11_ = bf16[640,256]{1,0:T(8,128)(2,1)S(1)} collective-permute-done((bf16[640,256]{1,0:T(8,128)(2,1)S(1)}, bf16[640,256]{1,0:T(8,128)(2,1)S(1)}, u32[]{:S(2)}, u32[]{:S(2)}) %collective-permute-start.8) | collective-permute-done | bytes 327712 | tf_op jit(solution)/shard_map/ppermute | solution.py:30
  52.4 1.5 %collective-permute-start.9 = (bf16[640,256]{1,0:T(8,128)(2,1)S(1)}, bf16[640,256]{1,0:T(8,128)(2,1)S(1)}, u32[]{:S(2)}, u32[]{:S(2)}) collective-permute-start(bf16[640,256]{1,0:T(8,128)(2,1)S(1)} %collective-permute-done.7.refs_15_.refs_10_), channel_id=1, source_target_pairs={{0,16},{4,12},{8,24},{12,4},{16,0},{20,28},{24,8},{28,20},{1,17},{... | collective-permute-start | bytes 983048 | tf_op jit(solution)/shard_map/ppermute | solution.py:30
  53.9 2.0 %collective-permute-done.16.refs_24_.refs_19_ = bf16[640,256]{1,0:T(8,128)(2,1)S(1)} collective-permute-done((bf16[640,256]{1,0:T(8,128)(2,1)S(1)}, bf16[640,256]{1,0:T(8,128)(2,1)S(1)}, u32[]{:S(2)}, u32[]{:S(2)}) %collective-permute-start.16) | collective-permute-done | bytes 327712 | tf_op jit(solution)/shard_map/ppermute | solution.py:30
  55.9 1.5 %collective-permute-start.17 = (bf16[640,256]{1,0:T(8,128)(2,1)S(1)}, bf16[640,256]{1,0:T(8,128)(2,1)S(1)}, u32[]{:S(2)}, u32[]{:S(2)}) collective-permute-start(bf16[640,256]{1,0:T(8,128)(2,1)S(1)} %collective-permute-done.15.refs_23_.refs_18_), channel_id=1, source_target_pairs={{0,16},{4,12},{8,24},{12,4},{16,0},{20,28},{24,8},{28,20},{1,17},{... | collective-permute-start | bytes 983048 | tf_op jit(solution)/shard_map/ppermute | solution.py:30
  57.4 0.5 collective-permute-start.12
  58.0 1.6 %collective-permute-start.22 = (bf16[640,256]{1,0:T(8,128)(2,1)S(1)}, bf16[640,256]{1,0:T(8,128)(2,1)S(1)}, u32[]{:S(2)}, u32[]{:S(2)}) collective-permute-start(bf16[640,256]{1,0:T(8,128)(2,1)S(1)} %shard_map.84), channel_id=1, source_target_pairs={{0,8},{4,20},{8,0},{12,28},{16,24},{20,4},{24,16},{28,12},{1,9},{5... | collective-permute-start | bytes 983048 | tf_op jit(solution)/shard_map/ppermute | solution.py:30
  59.5 5.7 %collective-permute-done.17.refs_25_.refs_20_ = bf16[640,256]{1,0:T(8,128)(2,1)S(1)} collective-permute-done((bf16[640,256]{1,0:T(8,128)(2,1)S(1)}, bf16[640,256]{1,0:T(8,128)(2,1)S(1)}, u32[]{:S(2)}, u32[]{:S(2)}) %collective-permute-start.17) | collective-permute-done | bytes 327712 | tf_op jit(solution)/shard_map/ppermute | solution.py:30
  65.2 0.5 collective-permute-start.20
  65.7 2.3 %collective-permute-start.23 = (bf16[640,256]{1,0:T(8,128)(2,1)S(1)}, bf16[640,256]{1,0:T(8,128)(2,1)S(1)}, u32[]{:S(2)}, u32[]{:S(2)}) collective-permute-start(bf16[640,256]{1,0:T(8,128)(2,1)S(1)} %shard_map.84), channel_id=1, source_target_pairs={{0,16},{4,12},{8,24},{12,4},{16,0},{20,28},{24,8},{28,20},{1,17},{... | collective-permute-start | bytes 983048 | tf_op jit(solution)/shard_map/ppermute | solution.py:30
  68.1 0.1 collective-permute-start.26
  68.1 0.0 collective-permute-start.13
  68.2 0.5 collective-permute-start.21
  68.6 4.5 %collective-permute-done.23.refs_3_.refs_27_ = bf16[640,256]{1,0:T(8,128)(2,1)S(1)} collective-permute-done((bf16[640,256]{1,0:T(8,128)(2,1)S(1)}, bf16[640,256]{1,0:T(8,128)(2,1)S(1)}, u32[]{:S(2)}, u32[]{:S(2)}) %collective-permute-start.23) | collective-permute-done | bytes 327712 | tf_op jit(solution)/shard_map/ppermute | solution.py:30
  73.1 0.5 collective-permute-start.25
  73.6 3.0 %collective-permute-done.26.refs_28_ = bf16[640,256]{1,0:T(8,128)(2,1)S(1)} collective-permute-done((bf16[640,256]{1,0:T(8,128)(2,1)S(1)}, bf16[640,256]{1,0:T(8,128)(2,1)S(1)}, u32[]{:S(2)}, u32[]{:S(2)}) %collective-permute-start.26) | collective-permute-done | bytes 327712 | tf_op jit(solution)/shard_map/ppermute | solution.py:30
  76.6 0.4 fusion
  77.1 2.9 %first.1 = (bf16[8,320,256]{2,1,0:T(8,128)(2,1)S(1)}, bf16[3,256,256]{2,1,0:T(8,128)(2,1)S(1)}, bf16[3,320,128]{2,1,0:T(8,128)(2,1)S(1)}) custom-call(bf16[1024,512]{1,0:T(8,128)(2,1)S(1)} %copy-done.2, f32[8,1,256]{2,1,0:T(1,128)S(1)} %bitcast.7, f32[192,128]{1,0:T(8,128)S(1)} %get-tuple-element.19.refs_2_.refs_3_, ...), custom_call_target="tpu_custom_call" | custom-call | tf_op jit(solution)/shard_map/first/pallas_call | solution.py:499
  80.0 0.0 copy-start.1
  80.0 0.0 copy-start.7
  80.0 0.6 second.1
  80.7 0.6 copy-done.1
  81.2 4.0 %main.1 = bf16[256,2048]{1,0:T(8,128)(2,1)} custom-call(bf16[8,320,256]{2,1,0:T(8,128)(2,1)S(1)} %get-tuple-element.10.refs_0_, bf16[3,256,256]{2,1,0:T(8,128)(2,1)S(1)} %get-tuple-element.11.refs_1_, bf16[3,320,128]{2,1,0:T(8,128)(2,1)S(1)} %get-tuple-element.12.refs_2_, f32[192,128]{1,0:T(8,128)S(1)} %get-tuple-element.19.refs_2_.refs_3_, ...), custom_call_target="tpu_custom_call" | custom-call | tf_op jit(solution)/shard_map/main/pallas_call | solution.py:536
  (34 shorter events, 0.2 us)
Async XLA Ops:
  0.0 7.0 %copy-start.2 = (bf16[1024,512]{1,0:T(8,128)(2,1)S(1)}, bf16[1024,512]{1,0:T(8,128)(2,1)}, u32[]{:S(2)}) copy-start(bf16[1024,512]{1,0:T(8,128)(2,1)} %refs_0_.1) | copy-start | bytes 3145732
  1.8 5.4 %copy-start.3 = (bf16[704,256]{1,0:T(8,128)(2,1)S(1)}, bf16[704,256]{1,0:T(8,128)(2,1)}, u32[]{:S(2)}) copy-start(bf16[704,256]{1,0:T(8,128)(2,1)} %cut.1.refs_4_) | copy-start | bytes 1081348
  1.8 14.7 %collective-permute-start.1 = (bf16[704,256]{1,0:T(8,128)(2,1)}, bf16[704,256]{1,0:T(8,128)(2,1)S(1)}, u32[]{:S(2)}, u32[]{:S(2)}) collective-permute-start(bf16[704,256]{1,0:T(8,128)(2,1)} %cut.1.refs_4_), channel_id=1, source_target_pairs={{0,1},{1,2},{2,3},{3,0},{4,5},{5,6},{6,7},{7,4},{8,9},{9,10},{10,1... | collective-permute-start | bytes 1081352 | tf_op jit(solution)/shard_map/ppermute | solution.py:19
  4.9 18.0 %collective-permute-start.14 = (bf16[704,256]{1,0:T(8,128)(2,1)}, bf16[704,256]{1,0:T(8,128)(2,1)S(1)}, u32[]{:S(2)}, u32[]{:S(2)}) collective-permute-start(bf16[704,256]{1,0:T(8,128)(2,1)} %cut.1.refs_4_), channel_id=1, source_target_pairs={{0,3},{1,0},{2,1},{3,2},{4,7},{5,4},{6,5},{7,6},{8,11},{9,8},{10,9... | collective-permute-start | bytes 1081352 | tf_op jit(solution)/shard_map/ppermute | solution.py:19
  7.1 69.9 %copy-start = (bf16[2048,256]{1,0:T(8,128)(2,1)S(1)}, bf16[2048,256]{1,0:T(8,128)(2,1)}, u32[]{:S(2)}) copy-start(bf16[2048,256]{1,0:T(8,128)(2,1)} %refs_8_.1) | copy-start | bytes 3145732
  7.1 69.9 %copy-start.4 = (bf16[2048,64]{0,1:T(8,128)(2,1)S(1)}, bf16[2048,64]{0,1:T(8,128)(2,1)}, u32[]{:S(2)}) copy-start(bf16[2048,64]{0,1:T(8,128)(2,1)} %param.12) | copy-start | bytes 786436
  7.1 69.9 %copy-start.5 = (bf16[2048,64]{0,1:T(8,128)(2,1)S(1)}, bf16[2048,64]{0,1:T(8,128)(2,1)}, u32[]{:S(2)}) copy-start(bf16[2048,64]{0,1:T(8,128)(2,1)} %param.13) | copy-start | bytes 786436
  7.1 69.9 %copy-start.6 = (f32[2048]{0:T(1024)S(1)}, f32[2048]{0:T(1024)}, u32[]{:S(2)}) copy-start(f32[2048]{0:T(1024)} %param.10) | copy-start | bytes 24580
  7.2 21.9 %collective-permute-start.4 = (bf16[256,512]{1,0:T(8,128)(2,1)S(1)}, bf16[256,512]{1,0:T(8,128)(2,1)S(1)}, u32[]{:S(2)}, u32[]{:S(2)}) collective-permute-start(bf16[256,512]{1,0:T(8,128)(2,1)S(1)} %get-tuple-element.17), channel_id=1, source_target_pairs={{0,1},{1,2},{2,3},{3,0},{4,5},{5,6},{6,7},{7,4},{8,9},{9,10},{10,1... | collective-permute-start | bytes 786440 | tf_op jit(solution)/shard_map/ppermute | solution.py:19
  7.2 38.0 %collective-permute-start = (bf16[704,256]{1,0:T(8,128)(2,1)S(1)}, bf16[704,256]{1,0:T(8,128)(2,1)S(1)}, u32[]{:S(2)}, u32[]{:S(2)}) collective-permute-start(bf16[704,256]{1,0:T(8,128)(2,1)S(1)} %copy-done.3), channel_id=1, source_target_pairs={{0,4},{4,0},{1,5},{5,1},{2,6},{6,2},{3,7},{7,3},{8,12},{12,8},{9,1... | collective-permute-start | bytes 1081352 | tf_op jit(solution)/shard_map/ppermute | solution.py:24
  16.5 30.3 %collective-permute-start.7 = (bf16[640,256]{1,0:T(8,128)(2,1)S(1)}, bf16[640,256]{1,0:T(8,128)(2,1)S(1)}, u32[]{:S(2)}, u32[]{:S(2)}) collective-permute-start(bf16[640,256]{1,0:T(8,128)(2,1)S(1)} %shard_map.82), channel_id=1, source_target_pairs={{0,8},{4,20},{8,0},{12,28},{16,24},{20,4},{24,16},{28,12},{1,9},{5... | collective-permute-start | bytes 983048 | tf_op jit(solution)/shard_map/ppermute | solution.py:30
  23.0 23.9 %collective-permute-start.15 = (bf16[640,256]{1,0:T(8,128)(2,1)S(1)}, bf16[640,256]{1,0:T(8,128)(2,1)S(1)}, u32[]{:S(2)}, u32[]{:S(2)}) collective-permute-start(bf16[640,256]{1,0:T(8,128)(2,1)S(1)} %shard_map.83), channel_id=1, source_target_pairs={{0,8},{4,20},{8,0},{12,28},{16,24},{20,4},{24,16},{28,12},{1,9},{5... | collective-permute-start | bytes 983048 | tf_op jit(solution)/shard_map/ppermute | solution.py:30
  24.8 15.5 %collective-permute-start.5 = (bf16[256,512]{1,0:T(8,128)(2,1)S(1)}, bf16[256,512]{1,0:T(8,128)(2,1)S(1)}, u32[]{:S(2)}, u32[]{:S(2)}) collective-permute-start(bf16[256,512]{1,0:T(8,128)(2,1)S(1)} %get-tuple-element.16), channel_id=1, source_target_pairs={{0,2},{1,3},{2,0},{3,1},{4,6},{5,7},{6,4},{7,5},{8,10},{9,11},{10,... | collective-permute-start | bytes 786440 | tf_op jit(solution)/shard_map/ppermute | solution.py:19
  29.1 16.1 %collective-permute-start.6 = (bf16[256,512]{1,0:T(8,128)(2,1)S(1)}, bf16[256,512]{1,0:T(8,128)(2,1)S(1)}, u32[]{:S(2)}, u32[]{:S(2)}) collective-permute-start(bf16[256,512]{1,0:T(8,128)(2,1)S(1)} %get-tuple-element.15), channel_id=1, source_target_pairs={{0,3},{1,0},{2,1},{3,2},{4,7},{5,4},{6,5},{7,6},{8,11},{9,8},{10,9... | collective-permute-start | bytes 786440 | tf_op jit(solution)/shard_map/ppermute | solution.py:19
  40.3 17.1 %collective-permute-start.2 = (bf16[704,256]{1,0:T(8,128)(2,1)S(1)}, bf16[704,256]{1,0:T(8,128)(2,1)S(1)}, u32[]{:S(2)}, u32[]{:S(2)}) collective-permute-start(bf16[704,256]{1,0:T(8,128)(2,1)S(1)} %collective-permute-done.1.refs_0_.refs_14_.refs_9_), channel_id=1, source_target_pairs={{0,1},{1,2},{2,3},{3,0},{4,5},{5,6},{6,7},{7,4},{8,9},{9,10},{10,1... | collective-permute-start | bytes 1081352 | tf_op jit(solution)/shard_map/ppermute | solution.py:19
  45.2 12.2 %collective-permute-start.10 = (bf16[704,256]{1,0:T(8,128)(2,1)S(1)}, bf16[704,256]{1,0:T(8,128)(2,1)S(1)}, u32[]{:S(2)}, u32[]{:S(2)}) collective-permute-start(bf16[704,256]{1,0:T(8,128)(2,1)S(1)} %collective-permute-done.1.refs_0_.refs_14_.refs_9_), channel_id=1, source_target_pairs={{0,4},{4,0},{1,5},{5,1},{2,6},{6,2},{3,7},{7,3},{8,12},{12,8},{9,1... | collective-permute-start | bytes 1081352 | tf_op jit(solution)/shard_map/ppermute | solution.py:24
  45.2 7.1 %collective-permute-start.8 = (bf16[640,256]{1,0:T(8,128)(2,1)S(1)}, bf16[640,256]{1,0:T(8,128)(2,1)S(1)}, u32[]{:S(2)}, u32[]{:S(2)}) collective-permute-start(bf16[640,256]{1,0:T(8,128)(2,1)S(1)} %shard_map.82), channel_id=1, source_target_pairs={{0,16},{4,12},{8,24},{12,4},{16,0},{20,28},{24,8},{28,20},{1,17},{... | collective-permute-start | bytes 983048 | tf_op jit(solution)/shard_map/ppermute | solution.py:30
  46.8 11.1 %collective-permute-start.18 = (bf16[704,256]{1,0:T(8,128)(2,1)S(1)}, bf16[704,256]{1,0:T(8,128)(2,1)S(1)}, u32[]{:S(2)}, u32[]{:S(2)}) collective-permute-start(bf16[704,256]{1,0:T(8,128)(2,1)S(1)} %collective-permute-done.14.refs_0_.refs_22_.refs_17_), channel_id=1, source_target_pairs={{0,4},{4,0},{1,5},{5,1},{2,6},{6,2},{3,7},{7,3},{8,12},{12,8},{9,1... | collective-permute-start | bytes 1081352 | tf_op jit(solution)/shard_map/ppermute | solution.py:24
  47.0 8.9 %collective-permute-start.16 = (bf16[640,256]{1,0:T(8,128)(2,1)S(1)}, bf16[640,256]{1,0:T(8,128)(2,1)S(1)}, u32[]{:S(2)}, u32[]{:S(2)}) collective-permute-start(bf16[640,256]{1,0:T(8,128)(2,1)S(1)} %shard_map.83), channel_id=1, source_target_pairs={{0,16},{4,12},{8,24},{12,4},{16,0},{20,28},{24,8},{28,20},{1,17},{... | collective-permute-start | bytes 983048 | tf_op jit(solution)/shard_map/ppermute | solution.py:30
  52.4 7.1 %collective-permute-start.9 = (bf16[640,256]{1,0:T(8,128)(2,1)S(1)}, bf16[640,256]{1,0:T(8,128)(2,1)S(1)}, u32[]{:S(2)}, u32[]{:S(2)}) collective-permute-start(bf16[640,256]{1,0:T(8,128)(2,1)S(1)} %collective-permute-done.7.refs_15_.refs_10_), channel_id=1, source_target_pairs={{0,16},{4,12},{8,24},{12,4},{16,0},{20,28},{24,8},{28,20},{1,17},{... | collective-permute-start | bytes 983048 | tf_op jit(solution)/shard_map/ppermute | solution.py:30
  55.9 9.3 %collective-permute-start.17 = (bf16[640,256]{1,0:T(8,128)(2,1)S(1)}, bf16[640,256]{1,0:T(8,128)(2,1)S(1)}, u32[]{:S(2)}, u32[]{:S(2)}) collective-permute-start(bf16[640,256]{1,0:T(8,128)(2,1)S(1)} %collective-permute-done.15.refs_23_.refs_18_), channel_id=1, source_target_pairs={{0,16},{4,12},{8,24},{12,4},{16,0},{20,28},{24,8},{28,20},{1,17},{... | collective-permute-start | bytes 983048 | tf_op jit(solution)/shard_map/ppermute | solution.py:30
  57.4 7.8 %collective-permute-start.11 = (bf16[640,256]{1,0:T(8,128)(2,1)S(1)}, bf16[640,256]{1,0:T(8,128)(2,1)S(1)}, u32[]{:S(2)}, u32[]{:S(2)}) collective-permute-start(bf16[640,256]{1,0:T(8,128)(2,1)S(1)} %collective-permute-done.7.refs_15_.refs_10_), channel_id=1, source_target_pairs={{0,4},{4,0},{1,5},{5,1},{2,6},{6,2},{3,7},{7,3},{8,12},{12,8},{9,1... | collective-permute-start | bytes 983048 | tf_op jit(solution)/shard_map/ppermute | solution.py:24
  57.4 8.3 %collective-permute-start.12 = (bf16[640,256]{1,0:T(8,128)(2,1)S(1)}, bf16[640,256]{1,0:T(8,128)(2,1)S(1)}, u32[]{:S(2)}, u32[]{:S(2)}) collective-permute-start(bf16[640,256]{1,0:T(8,128)(2,1)S(1)} %collective-permute-done.8.refs_16_.refs_11_), channel_id=1, source_target_pairs={{0,4},{4,0},{1,5},{5,1},{2,6},{6,2},{3,7},{7,3},{8,12},{12,8},{9,1... | collective-permute-start | bytes 983048 | tf_op jit(solution)/shard_map/ppermute | solution.py:24
  58.0 10.1 %collective-permute-start.22 = (bf16[640,256]{1,0:T(8,128)(2,1)S(1)}, bf16[640,256]{1,0:T(8,128)(2,1)S(1)}, u32[]{:S(2)}, u32[]{:S(2)}) collective-permute-start(bf16[640,256]{1,0:T(8,128)(2,1)S(1)} %shard_map.84), channel_id=1, source_target_pairs={{0,8},{4,20},{8,0},{12,28},{16,24},{20,4},{24,16},{28,12},{1,9},{5... | collective-permute-start | bytes 983048 | tf_op jit(solution)/shard_map/ppermute | solution.py:30
  59.5 13.6 %collective-permute-start.3 = (bf16[704,256]{1,0:T(8,128)(2,1)S(1)}, bf16[704,256]{1,0:T(8,128)(2,1)S(1)}, u32[]{:S(2)}, u32[]{:S(2)}) collective-permute-start(bf16[704,256]{1,0:T(8,128)(2,1)S(1)} %collective-permute-done.2.refs_6_.refs_0_.refs_1_.refs_25_), channel_id=1, source_target_pairs={{0,4},{4,0},{1,5},{5,1},{2,6},{6,2},{3,7},{7,3},{8,12},{12,8},{9,1... | collective-permute-start | bytes 1081352 | tf_op jit(solution)/shard_map/ppermute | solution.py:24
  65.2 2.9 %collective-permute-start.19 = (bf16[640,256]{1,0:T(8,128)(2,1)S(1)}, bf16[640,256]{1,0:T(8,128)(2,1)S(1)}, u32[]{:S(2)}, u32[]{:S(2)}) collective-permute-start(bf16[640,256]{1,0:T(8,128)(2,1)S(1)} %collective-permute-done.15.refs_23_.refs_18_), channel_id=1, source_target_pairs={{0,4},{4,0},{1,5},{5,1},{2,6},{6,2},{3,7},{7,3},{8,12},{12,8},{9,1... | collective-permute-start | bytes 983048 | tf_op jit(solution)/shard_map/ppermute | solution.py:24
  65.2 2.9 %collective-permute-start.20 = (bf16[640,256]{1,0:T(8,128)(2,1)S(1)}, bf16[640,256]{1,0:T(8,128)(2,1)S(1)}, u32[]{:S(2)}, u32[]{:S(2)}) collective-permute-start(bf16[640,256]{1,0:T(8,128)(2,1)S(1)} %collective-permute-done.16.refs_24_.refs_19_), channel_id=1, source_target_pairs={{0,4},{4,0},{1,5},{5,1},{2,6},{6,2},{3,7},{7,3},{8,12},{12,8},{9,1... | collective-permute-start | bytes 983048 | tf_op jit(solution)/shard_map/ppermute | solution.py:24
  65.7 7.4 %collective-permute-start.23 = (bf16[640,256]{1,0:T(8,128)(2,1)S(1)}, bf16[640,256]{1,0:T(8,128)(2,1)S(1)}, u32[]{:S(2)}, u32[]{:S(2)}) collective-permute-start(bf16[640,256]{1,0:T(8,128)(2,1)S(1)} %shard_map.84), channel_id=1, source_target_pairs={{0,16},{4,12},{8,24},{12,4},{16,0},{20,28},{24,8},{28,20},{1,17},{... | collective-permute-start | bytes 983048 | tf_op jit(solution)/shard_map/ppermute | solution.py:30
  68.1 8.6 %collective-permute-start.26 = (bf16[640,256]{1,0:T(8,128)(2,1)S(1)}, bf16[640,256]{1,0:T(8,128)(2,1)S(1)}, u32[]{:S(2)}, u32[]{:S(2)}) collective-permute-start(bf16[640,256]{1,0:T(8,128)(2,1)S(1)} %collective-permute-done.22.refs_2_.refs_26_), channel_id=1, source_target_pairs={{0,16},{4,12},{8,24},{12,4},{16,0},{20,28},{24,8},{28,20},{1,17},{... | collective-permute-start | bytes 983048 | tf_op jit(solution)/shard_map/ppermute | solution.py:30
  68.1 8.9 %collective-permute-start.13 = (bf16[640,256]{1,0:T(8,128)(2,1)S(1)}, bf16[640,256]{1,0:T(8,128)(2,1)S(1)}, u32[]{:S(2)}, u32[]{:S(2)}) collective-permute-start(bf16[640,256]{1,0:T(8,128)(2,1)S(1)} %collective-permute-done.9.refs_17_.refs_12_), channel_id=1, source_target_pairs={{0,4},{4,0},{1,5},{5,1},{2,6},{6,2},{3,7},{7,3},{8,12},{12,8},{9,1... | collective-permute-start | bytes 983048 | tf_op jit(solution)/shard_map/ppermute | solution.py:24
  68.2 8.9 %collective-permute-start.21 = (bf16[640,256]{1,0:T(8,128)(2,1)S(1)}, bf16[640,256]{1,0:T(8,128)(2,1)S(1)}, u32[]{:S(2)}, u32[]{:S(2)}) collective-permute-start(bf16[640,256]{1,0:T(8,128)(2,1)S(1)} %collective-permute-done.17.refs_25_.refs_20_), channel_id=1, source_target_pairs={{0,4},{4,0},{1,5},{5,1},{2,6},{6,2},{3,7},{7,3},{8,12},{12,8},{9,1... | collective-permute-start | bytes 983048 | tf_op jit(solution)/shard_map/ppermute | solution.py:24
  73.1 6.9 %collective-permute-start.24 = (bf16[640,256]{1,0:T(8,128)(2,1)S(1)}, bf16[640,256]{1,0:T(8,128)(2,1)S(1)}, u32[]{:S(2)}, u32[]{:S(2)}) collective-permute-start(bf16[640,256]{1,0:T(8,128)(2,1)S(1)} %collective-permute-done.22.refs_2_.refs_26_), channel_id=1, source_target_pairs={{0,4},{4,0},{1,5},{5,1},{2,6},{6,2},{3,7},{7,3},{8,12},{12,8},{9,1... | collective-permute-start | bytes 983048 | tf_op jit(solution)/shard_map/ppermute | solution.py:24
  73.1 6.9 %collective-permute-start.25 = (bf16[640,256]{1,0:T(8,128)(2,1)S(1)}, bf16[640,256]{1,0:T(8,128)(2,1)S(1)}, u32[]{:S(2)}, u32[]{:S(2)}) collective-permute-start(bf16[640,256]{1,0:T(8,128)(2,1)S(1)} %collective-permute-done.23.refs_3_.refs_27_), channel_id=1, source_target_pairs={{0,4},{4,0},{1,5},{5,1},{2,6},{6,2},{3,7},{7,3},{8,12},{12,8},{9,1... | collective-permute-start | bytes 983048 | tf_op jit(solution)/shard_map/ppermute | solution.py:24
  76.6 4.0 %collective-permute-start.27 = (bf16[640,256]{1,0:T(8,128)(2,1)S(1)}, bf16[640,256]{1,0:T(8,128)(2,1)S(1)}, u32[]{:S(2)}, u32[]{:S(2)}) collective-permute-start(bf16[640,256]{1,0:T(8,128)(2,1)S(1)} %collective-permute-done.26.refs_28_), channel_id=1, source_target_pairs={{0,4},{4,0},{1,5},{5,1},{2,6},{6,2},{3,7},{7,3},{8,12},{12,8},{9,1... | collective-permute-start | bytes 983048 | tf_op jit(solution)/shard_map/ppermute | solution.py:24
  80.0 1.2 %copy-start.1 = (bf16[256,2048]{1,0:T(8,128)(2,1)S(1)}, bf16[256,2048]{1,0:T(8,128)(2,1)}, u32[]{:S(2)}) copy-start(bf16[256,2048]{1,0:T(8,128)(2,1)} %refs_6_.1) | copy-start | bytes 3145732
  80.0 1.2 %copy-start.7 = (s32[8]{0:T(128)S(1)}, s32[8]{0:T(128)}, u32[]{:S(2)}) copy-start(s32[8]{0:T(128)} %refs_5_.1) | copy-start | bytes 100

commit v3 on v2

--- a/solution.py
+++ b/solution.py
@@ -11,7 +11,7 @@
 epsilon = 1e-06
 theta_base = 10000.0
 PLANE = ("query", "cand")
-UNROLL = 4
+UNROLL = 8
 
 
 def shift(k):
@@ -351,7 +351,7 @@
     n_in = 9 + (n - 1) * n_pieces
     piece_refs = refs[9:n_in]
     o_ref = refs[n_in]
-    w_out, kv_scr, heads, sem = refs[n_in + 1 :]
+    w_out, kv_scr, heads, made_out, sem, out_sems = refs[n_in + 1 :]
     me = lax.axis_index("tensor")
     parity = lax.rem(lax.axis_index("cand"), 2)
     half = head // 2
@@ -427,6 +427,7 @@
                 heads[k, own, :] = mix[at * cand_len : (at + 1) * cand_len]
 
     c.wait()
+    outs = []
     for i in range(0, n_pieces, 2):
         spots = [rows_of(part * size, size) for part in parts[i : i + 2]]
         total = None
@@ -440,7 +441,12 @@
             )
             total = term if total is None else total + term
         for at, spot in enumerate(spots):
-            o_ref[:, spot] = total[:, at * size : (at + 1) * size].astype(jnp.bfloat16)
+            made_out[i + at] = total[:, at * size : (at + 1) * size].astype(jnp.bfloat16)
+            out = pltpu.make_async_copy(made_out.at[i + at], o_ref.at[:, spot], out_sems.at[i + at])
+            out.start()
+            outs.append(out)
+    for out in outs:
+        out.wait()
 
 
 def body(cand_states, prefix_states, norm_gain, w_query, w_key, w_value, w_out, cand_lengths):
@@ -538,12 +544,14 @@
         name="main",
         out_shape=jax.ShapeDtypeStruct((rows, out_cols), jnp.bfloat16),
         in_specs=[vmem] * 5 + [smem, hbm] + [vmem] * (2 + len(pieces)),
-        out_specs=vmem,
+        out_specs=hbm,
         scratch_shapes=[
             pltpu.VMEM((head, out_cols), jnp.bfloat16),
             pltpu.VMEM((n, every, 2 * share), jnp.bfloat16),
             pltpu.VMEM((n, rows, head), jnp.bfloat16),
+            pltpu.VMEM((count, rows, size), jnp.bfloat16),
             pltpu.SemaphoreType.DMA,
+            pltpu.SemaphoreType.DMA((count,)),
         ],
         compiler_params=pltpu.CompilerParams(vmem_limit_bytes=24 * 2**20),
     )(normed, queries, pairs, cos, sin, cand_lengths, w_out, q_part, kv_part, *pieces)

time: 86.4 us -> 86 us (level)
  no operation moved by 1% of the time
where the time goes in v3:
time: 86 us; the launch traced here: 84.8 us
  waiting for transfers between devices  43.9 us (51%)
  starting transfers between devices  30.6 us (36%)
  Pallas kernels  9.01 us (10%)
    ppermute x6, waiting for transfers between devices, shift(): lax.ppermute(v, 'tensor', [(i, (i + k) % n) for i in range(n)])  24.8 us
    ppermute x9, waiting for transfers between devices, plane_xor(): return lambda v: lax.ppermute(v, PLANE, pairs)  19.1 us
    ppermute x6, starting transfers between devices, shift(): lax.ppermute(v, 'tensor', [(i, (i + k) % n) for i in range(n)])  14.7 us
    ppermute x9, starting transfers between devices, plane_xor(): return lambda v: lax.ppermute(v, PLANE, pairs)  13.6 us
    pallas_call x1, Pallas kernels, body(): pl.pallas_call(functools.partial(last_kernel, dims, nearest(n), plan), na...  3.72 us
    pallas_call x1, Pallas kernels, body(): pl.pallas_call(functools.partial(first_kernel, dims, nearest(n), plan), n...  2.78 us
    ppermute x13, starting transfers between devices, other_core(): return lax.ppermute(v, 'cand', [(i, i ^ 1) for i in range(n)])  2.24 us
    pallas_call x1, Pallas kernels, body(): pl.pallas_call(functools.partial(cut_kernel, (prefix_rows, prefix_len, ca...  1.81 us
  transfers between devices with their start and end apart: 28, of which 9 were waited for; matrix products, arithmetic and copies ran while one was open for 1% of the time, Pallas kernels for 4%

profile of v3, /device:TPU:0, one launch (start us, length us, event | category | flops | bytes accessed | tf_op | source)
XLA Modules:
  0.0 84.8 jit_solution(4639400040592593612)
XLA Ops:
  0.0 1.8 %cut.1.refs_4_ = bf16[704,256]{1,0:T(8,128)(2,1)} custom-call(bf16[2048,256]{1,0:T(8,128)(2,1)} %refs_8_.1, bf16[256,2048]{1,0:T(8,128)(2,1)} %refs_6_.1, bf16[64,2048]{1,0:T(8,128)(2,1)} %bitcast.3, bf16[64,2048]{1,0:T(8,128)(2,1)} %bitcast.5, bf16[32,512]{1,0:T(8,128)(2,1)} %p_ref.1), custom_call_target="tpu_custom_call" | custom-call | tf_op jit(solution)/shard_map/cut/pallas_call | solution.py:476
  1.8 0.0 copy-start.3
  1.8 3.1 %collective-permute-start.1 = (bf16[704,256]{1,0:T(8,128)(2,1)}, bf16[704,256]{1,0:T(8,128)(2,1)S(1)}, u32[]{:S(2)}, u32[]{:S(2)}) collective-permute-start(bf16[704,256]{1,0:T(8,128)(2,1)} %cut.1.refs_4_), channel_id=1, source_target_pairs={{0,1},{1,2},{2,3},{3,0},{4,5},{5,6},{6,7},{7,4},{8,9},{9,10},{10,1... | collective-permute-start | bytes 1081352 | tf_op jit(solution)/shard_map/ppermute | solution.py:19
  4.9 2.1 %collective-permute-start.14 = (bf16[704,256]{1,0:T(8,128)(2,1)}, bf16[704,256]{1,0:T(8,128)(2,1)S(1)}, u32[]{:S(2)}, u32[]{:S(2)}) collective-permute-start(bf16[704,256]{1,0:T(8,128)(2,1)} %cut.1.refs_4_), channel_id=1, source_target_pairs={{0,3},{1,0},{2,1},{3,2},{4,7},{5,4},{6,5},{7,6},{8,11},{9,8},{10,9... | collective-permute-start | bytes 1081352 | tf_op jit(solution)/shard_map/ppermute | solution.py:19
  7.0 0.1 constant_dynamic-slice_fusion
  7.1 0.0 copy-start
  7.1 0.0 copy-start.4
  7.1 0.0 copy-start.5
  7.1 0.0 copy-start.6
  7.2 0.1 collective-permute-start.4
  7.2 0.1 collective-permute-start
  7.3 9.2 %collective-permute-done.1.refs_0_.refs_14_.refs_9_ = bf16[704,256]{1,0:T(8,128)(2,1)S(1)} collective-permute-done((bf16[704,256]{1,0:T(8,128)(2,1)}, bf16[704,256]{1,0:T(8,128)(2,1)S(1)}, u32[]{:S(2)}, u32[]{:S(2)}) %collective-permute-start.1) | collective-permute-done | bytes 360480 | tf_op jit(solution)/shard_map/ppermute | solution.py:19
  16.5 1.8 %collective-permute-start.7 = (bf16[640,256]{1,0:T(8,128)(2,1)S(1)}, bf16[640,256]{1,0:T(8,128)(2,1)S(1)}, u32[]{:S(2)}, u32[]{:S(2)}) collective-permute-start(bf16[640,256]{1,0:T(8,128)(2,1)S(1)} %shard_map.82), channel_id=1, source_target_pairs={{0,8},{4,20},{8,0},{12,28},{16,24},{20,4},{24,16},{28,12},{1,9},{5... | collective-permute-start | bytes 983048 | tf_op jit(solution)/shard_map/ppermute | solution.py:30
  18.3 4.7 %collective-permute-done.14.refs_0_.refs_22_.refs_17_ = bf16[704,256]{1,0:T(8,128)(2,1)S(1)} collective-permute-done((bf16[704,256]{1,0:T(8,128)(2,1)}, bf16[704,256]{1,0:T(8,128)(2,1)S(1)}, u32[]{:S(2)}, u32[]{:S(2)}) %collective-permute-start.14) | collective-permute-done | bytes 360480 | tf_op jit(solution)/shard_map/ppermute | solution.py:19
  23.0 1.8 %collective-permute-start.15 = (bf16[640,256]{1,0:T(8,128)(2,1)S(1)}, bf16[640,256]{1,0:T(8,128)(2,1)S(1)}, u32[]{:S(2)}, u32[]{:S(2)}) collective-permute-start(bf16[640,256]{1,0:T(8,128)(2,1)S(1)} %shard_map.83), channel_id=1, source_target_pairs={{0,8},{4,20},{8,0},{12,28},{16,24},{20,4},{24,16},{28,12},{1,9},{5... | collective-permute-start | bytes 983048 | tf_op jit(solution)/shard_map/ppermute | solution.py:30
  24.8 2.6 %collective-permute-start.5 = (bf16[256,512]{1,0:T(8,128)(2,1)S(1)}, bf16[256,512]{1,0:T(8,128)(2,1)S(1)}, u32[]{:S(2)}, u32[]{:S(2)}) collective-permute-start(bf16[256,512]{1,0:T(8,128)(2,1)S(1)} %get-tuple-element.16), channel_id=1, source_target_pairs={{0,2},{1,3},{2,0},{3,1},{4,6},{5,7},{6,4},{7,5},{8,10},{9,11},{10,... | collective-permute-start | bytes 786440 | tf_op jit(solution)/shard_map/ppermute | solution.py:19
  27.4 1.7 %collective-permute-done.4.refs_11_ = bf16[256,512]{1,0:T(8,128)(2,1)S(1)} collective-permute-done((bf16[256,512]{1,0:T(8,128)(2,1)S(1)}, bf16[256,512]{1,0:T(8,128)(2,1)S(1)}, u32[]{:S(2)}, u32[]{:S(2)}) %collective-permute-start.4) | collective-permute-done | bytes 262176 | tf_op jit(solution)/shard_map/ppermute | solution.py:19
  29.1 2.0 %collective-permute-start.6 = (bf16[256,512]{1,0:T(8,128)(2,1)S(1)}, bf16[256,512]{1,0:T(8,128)(2,1)S(1)}, u32[]{:S(2)}, u32[]{:S(2)}) collective-permute-start(bf16[256,512]{1,0:T(8,128)(2,1)S(1)} %get-tuple-element.15), channel_id=1, source_target_pairs={{0,3},{1,0},{2,1},{3,2},{4,7},{5,4},{6,5},{7,6},{8,11},{9,8},{10,9... | collective-permute-start | bytes 786440 | tf_op jit(solution)/shard_map/ppermute | solution.py:19
  31.1 9.2 %collective-permute-done.5.refs_12_ = bf16[256,512]{1,0:T(8,128)(2,1)S(1)} collective-permute-done((bf16[256,512]{1,0:T(8,128)(2,1)S(1)}, bf16[256,512]{1,0:T(8,128)(2,1)S(1)}, u32[]{:S(2)}, u32[]{:S(2)}) %collective-permute-start.5) | collective-permute-done | bytes 262176 | tf_op jit(solution)/shard_map/ppermute | solution.py:19
  40.3 4.9 %collective-permute-start.2 = (bf16[704,256]{1,0:T(8,128)(2,1)S(1)}, bf16[704,256]{1,0:T(8,128)(2,1)S(1)}, u32[]{:S(2)}, u32[]{:S(2)}) collective-permute-start(bf16[704,256]{1,0:T(8,128)(2,1)S(1)} %collective-permute-done.1.refs_0_.refs_14_.refs_9_), channel_id=1, source_target_pairs={{0,1},{1,2},{2,3},{3,0},{4,5},{5,6},{6,7},{7,4},{8,9},{9,10},{10,1... | collective-permute-start | bytes 1081352 | tf_op jit(solution)/shard_map/ppermute | solution.py:19
  45.2 0.0 collective-permute-done.6.refs_13_
  45.2 1.6 %collective-permute-start.8 = (bf16[640,256]{1,0:T(8,128)(2,1)S(1)}, bf16[640,256]{1,0:T(8,128)(2,1)S(1)}, u32[]{:S(2)}, u32[]{:S(2)}) collective-permute-start(bf16[640,256]{1,0:T(8,128)(2,1)S(1)} %shard_map.82), channel_id=1, source_target_pairs={{0,16},{4,12},{8,24},{12,4},{16,0},{20,28},{24,8},{28,20},{1,17},{... | collective-permute-start | bytes 983048 | tf_op jit(solution)/shard_map/ppermute | solution.py:30
  46.8 0.0 collective-permute-done.7.refs_15_.refs_10_
  46.8 0.1 collective-permute-start.18
  47.0 0.0 collective-permute-done.15.refs_23_.refs_18_
  47.0 1.5 %collective-permute-start.16 = (bf16[640,256]{1,0:T(8,128)(2,1)S(1)}, bf16[640,256]{1,0:T(8,128)(2,1)S(1)}, u32[]{:S(2)}, u32[]{:S(2)}) collective-permute-start(bf16[640,256]{1,0:T(8,128)(2,1)S(1)} %shard_map.83), channel_id=1, source_target_pairs={{0,16},{4,12},{8,24},{12,4},{16,0},{20,28},{24,8},{28,20},{1,17},{... | collective-permute-start | bytes 983048 | tf_op jit(solution)/shard_map/ppermute | solution.py:30
  48.5 3.9 %collective-permute-done.8.refs_16_.refs_11_ = bf16[640,256]{1,0:T(8,128)(2,1)S(1)} collective-permute-done((bf16[640,256]{1,0:T(8,128)(2,1)S(1)}, bf16[640,256]{1,0:T(8,128)(2,1)S(1)}, u32[]{:S(2)}, u32[]{:S(2)}) %collective-permute-start.8) | collective-permute-done | bytes 327712 | tf_op jit(solution)/shard_map/ppermute | solution.py:30
  52.4 1.5 %collective-permute-start.9 = (bf16[640,256]{1,0:T(8,128)(2,1)S(1)}, bf16[640,256]{1,0:T(8,128)(2,1)S(1)}, u32[]{:S(2)}, u32[]{:S(2)}) collective-permute-start(bf16[640,256]{1,0:T(8,128)(2,1)S(1)} %collective-permute-done.7.refs_15_.refs_10_), channel_id=1, source_target_pairs={{0,16},{4,12},{8,24},{12,4},{16,0},{20,28},{24,8},{28,20},{1,17},{... | collective-permute-start | bytes 983048 | tf_op jit(solution)/shard_map/ppermute | solution.py:30
  53.9 2.0 %collective-permute-done.16.refs_24_.refs_19_ = bf16[640,256]{1,0:T(8,128)(2,1)S(1)} collective-permute-done((bf16[640,256]{1,0:T(8,128)(2,1)S(1)}, bf16[640,256]{1,0:T(8,128)(2,1)S(1)}, u32[]{:S(2)}, u32[]{:S(2)}) %collective-permute-start.16) | collective-permute-done | bytes 327712 | tf_op jit(solution)/shard_map/ppermute | solution.py:30
  55.9 1.5 %collective-permute-start.17 = (bf16[640,256]{1,0:T(8,128)(2,1)S(1)}, bf16[640,256]{1,0:T(8,128)(2,1)S(1)}, u32[]{:S(2)}, u32[]{:S(2)}) collective-permute-start(bf16[640,256]{1,0:T(8,128)(2,1)S(1)} %collective-permute-done.15.refs_23_.refs_18_), channel_id=1, source_target_pairs={{0,16},{4,12},{8,24},{12,4},{16,0},{20,28},{24,8},{28,20},{1,17},{... | collective-permute-start | bytes 983048 | tf_op jit(solution)/shard_map/ppermute | solution.py:30
  57.4 0.5 collective-permute-start.12
  58.0 1.6 %collective-permute-start.22 = (bf16[640,256]{1,0:T(8,128)(2,1)S(1)}, bf16[640,256]{1,0:T(8,128)(2,1)S(1)}, u32[]{:S(2)}, u32[]{:S(2)}) collective-permute-start(bf16[640,256]{1,0:T(8,128)(2,1)S(1)} %shard_map.84), channel_id=1, source_target_pairs={{0,8},{4,20},{8,0},{12,28},{16,24},{20,4},{24,16},{28,12},{1,9},{5... | collective-permute-start | bytes 983048 | tf_op jit(solution)/shard_map/ppermute | solution.py:30
  59.5 5.7 %collective-permute-done.17.refs_25_.refs_20_ = bf16[640,256]{1,0:T(8,128)(2,1)S(1)} collective-permute-done((bf16[640,256]{1,0:T(8,128)(2,1)S(1)}, bf16[640,256]{1,0:T(8,128)(2,1)S(1)}, u32[]{:S(2)}, u32[]{:S(2)}) %collective-permute-start.17) | collective-permute-done | bytes 327712 | tf_op jit(solution)/shard_map/ppermute | solution.py:30
  65.2 0.5 collective-permute-start.20
  65.7 2.3 %collective-permute-start.23 = (bf16[640,256]{1,0:T(8,128)(2,1)S(1)}, bf16[640,256]{1,0:T(8,128)(2,1)S(1)}, u32[]{:S(2)}, u32[]{:S(2)}) collective-permute-start(bf16[640,256]{1,0:T(8,128)(2,1)S(1)} %shard_map.84), channel_id=1, source_target_pairs={{0,16},{4,12},{8,24},{12,4},{16,0},{20,28},{24,8},{28,20},{1,17},{... | collective-permute-start | bytes 983048 | tf_op jit(solution)/shard_map/ppermute | solution.py:30
  68.1 0.1 collective-permute-start.26
  68.1 0.0 collective-permute-start.13
  68.2 0.5 collective-permute-start.21
  68.6 4.5 %collective-permute-done.23.refs_3_.refs_27_ = bf16[640,256]{1,0:T(8,128)(2,1)S(1)} collective-permute-done((bf16[640,256]{1,0:T(8,128)(2,1)S(1)}, bf16[640,256]{1,0:T(8,128)(2,1)S(1)}, u32[]{:S(2)}, u32[]{:S(2)}) %collective-permute-start.23) | collective-permute-done | bytes 327712 | tf_op jit(solution)/shard_map/ppermute | solution.py:30
  73.1 0.5 collective-permute-start.25
  73.6 3.0 %collective-permute-done.26.refs_28_ = bf16[640,256]{1,0:T(8,128)(2,1)S(1)} collective-permute-done((bf16[640,256]{1,0:T(8,128)(2,1)S(1)}, bf16[640,256]{1,0:T(8,128)(2,1)S(1)}, u32[]{:S(2)}, u32[]{:S(2)}) %collective-permute-start.26) | collective-permute-done | bytes 327712 | tf_op jit(solution)/shard_map/ppermute | solution.py:30
  76.6 0.4 fusion
  77.1 2.8 %first.1 = (bf16[8,320,256]{2,1,0:T(8,128)(2,1)S(1)}, bf16[3,256,256]{2,1,0:T(8,128)(2,1)S(1)}, bf16[3,320,128]{2,1,0:T(8,128)(2,1)S(1)}) custom-call(bf16[1024,512]{1,0:T(8,128)(2,1)S(1)} %copy-done.2, f32[8,1,256]{2,1,0:T(1,128)S(1)} %bitcast.7, f32[192,128]{1,0:T(8,128)S(1)} %get-tuple-element.19.refs_2_.refs_3_, ...), custom_call_target="tpu_custom_call" | custom-call | tf_op jit(solution)/shard_map/first/pallas_call | solution.py:505
  79.9 0.0 copy-start.1
  79.9 0.0 copy-start.7
  79.9 0.6 second.1
  80.6 0.6 copy-done.1
  81.1 3.7 %main.1 = bf16[256,2048]{1,0:T(8,128)(2,1)} custom-call(bf16[8,320,256]{2,1,0:T(8,128)(2,1)S(1)} %get-tuple-element.10.refs_0_, bf16[3,256,256]{2,1,0:T(8,128)(2,1)S(1)} %get-tuple-element.11.refs_1_, bf16[3,320,128]{2,1,0:T(8,128)(2,1)S(1)} %get-tuple-element.12.refs_2_, f32[192,128]{1,0:T(8,128)S(1)} %get-tuple-element.19.refs_2_.refs_3_, ...), custom_call_target="tpu_custom_call" | custom-call | tf_op jit(solution)/shard_map/main/pallas_call | solution.py:542
  (34 shorter events, 0.2 us)
Async XLA Ops:
  0.0 7.0 %copy-start.2 = (bf16[1024,512]{1,0:T(8,128)(2,1)S(1)}, bf16[1024,512]{1,0:T(8,128)(2,1)}, u32[]{:S(2)}) copy-start(bf16[1024,512]{1,0:T(8,128)(2,1)} %refs_0_.1) | copy-start | bytes 3145732
  1.8 5.4 %copy-start.3 = (bf16[704,256]{1,0:T(8,128)(2,1)S(1)}, bf16[704,256]{1,0:T(8,128)(2,1)}, u32[]{:S(2)}) copy-start(bf16[704,256]{1,0:T(8,128)(2,1)} %cut.1.refs_4_) | copy-start | bytes 1081348
  1.8 14.7 %collective-permute-start.1 = (bf16[704,256]{1,0:T(8,128)(2,1)}, bf16[704,256]{1,0:T(8,128)(2,1)S(1)}, u32[]{:S(2)}, u32[]{:S(2)}) collective-permute-start(bf16[704,256]{1,0:T(8,128)(2,1)} %cut.1.refs_4_), channel_id=1, source_target_pairs={{0,1},{1,2},{2,3},{3,0},{4,5},{5,6},{6,7},{7,4},{8,9},{9,10},{10,1... | collective-permute-start | bytes 1081352 | tf_op jit(solution)/shard_map/ppermute | solution.py:19
  4.9 18.0 %collective-permute-start.14 = (bf16[704,256]{1,0:T(8,128)(2,1)}, bf16[704,256]{1,0:T(8,128)(2,1)S(1)}, u32[]{:S(2)}, u32[]{:S(2)}) collective-permute-start(bf16[704,256]{1,0:T(8,128)(2,1)} %cut.1.refs_4_), channel_id=1, source_target_pairs={{0,3},{1,0},{2,1},{3,2},{4,7},{5,4},{6,5},{7,6},{8,11},{9,8},{10,9... | collective-permute-start | bytes 1081352 | tf_op jit(solution)/shard_map/ppermute | solution.py:19
  7.1 69.9 %copy-start = (bf16[2048,256]{1,0:T(8,128)(2,1)S(1)}, bf16[2048,256]{1,0:T(8,128)(2,1)}, u32[]{:S(2)}) copy-start(bf16[2048,256]{1,0:T(8,128)(2,1)} %refs_8_.1) | copy-start | bytes 3145732
  7.1 69.9 %copy-start.4 = (bf16[2048,64]{0,1:T(8,128)(2,1)S(1)}, bf16[2048,64]{0,1:T(8,128)(2,1)}, u32[]{:S(2)}) copy-start(bf16[2048,64]{0,1:T(8,128)(2,1)} %param.12) | copy-start | bytes 786436
  7.1 69.9 %copy-start.5 = (bf16[2048,64]{0,1:T(8,128)(2,1)S(1)}, bf16[2048,64]{0,1:T(8,128)(2,1)}, u32[]{:S(2)}) copy-start(bf16[2048,64]{0,1:T(8,128)(2,1)} %param.13) | copy-start | bytes 786436
  7.1 69.9 %copy-start.6 = (f32[2048]{0:T(1024)S(1)}, f32[2048]{0:T(1024)}, u32[]{:S(2)}) copy-start(f32[2048]{0:T(1024)} %param.10) | copy-start | bytes 24580
  7.2 21.9 %collective-permute-start.4 = (bf16[256,512]{1,0:T(8,128)(2,1)S(1)}, bf16[256,512]{1,0:T(8,128)(2,1)S(1)}, u32[]{:S(2)}, u32[]{:S(2)}) collective-permute-start(bf16[256,512]{1,0:T(8,128)(2,1)S(1)} %get-tuple-element.17), channel_id=1, source_target_pairs={{0,1},{1,2},{2,3},{3,0},{4,5},{5,6},{6,7},{7,4},{8,9},{9,10},{10,1... | collective-permute-start | bytes 786440 | tf_op jit(solution)/shard_map/ppermute | solution.py:19
  7.2 38.0 %collective-permute-start = (bf16[704,256]{1,0:T(8,128)(2,1)S(1)}, bf16[704,256]{1,0:T(8,128)(2,1)S(1)}, u32[]{:S(2)}, u32[]{:S(2)}) collective-permute-start(bf16[704,256]{1,0:T(8,128)(2,1)S(1)} %copy-done.3), channel_id=1, source_target_pairs={{0,4},{4,0},{1,5},{5,1},{2,6},{6,2},{3,7},{7,3},{8,12},{12,8},{9,1... | collective-permute-start | bytes 1081352 | tf_op jit(solution)/shard_map/ppermute | solution.py:24
  16.5 30.3 %collective-permute-start.7 = (bf16[640,256]{1,0:T(8,128)(2,1)S(1)}, bf16[640,256]{1,0:T(8,128)(2,1)S(1)}, u32[]{:S(2)}, u32[]{:S(2)}) collective-permute-start(bf16[640,256]{1,0:T(8,128)(2,1)S(1)} %shard_map.82), channel_id=1, source_target_pairs={{0,8},{4,20},{8,0},{12,28},{16,24},{20,4},{24,16},{28,12},{1,9},{5... | collective-permute-start | bytes 983048 | tf_op jit(solution)/shard_map/ppermute | solution.py:30
  23.0 23.9 %collective-permute-start.15 = (bf16[640,256]{1,0:T(8,128)(2,1)S(1)}, bf16[640,256]{1,0:T(8,128)(2,1)S(1)}, u32[]{:S(2)}, u32[]{:S(2)}) collective-permute-start(bf16[640,256]{1,0:T(8,128)(2,1)S(1)} %shard_map.83), channel_id=1, source_target_pairs={{0,8},{4,20},{8,0},{12,28},{16,24},{20,4},{24,16},{28,12},{1,9},{5... | collective-permute-start | bytes 983048 | tf_op jit(solution)/shard_map/ppermute | solution.py:30
  24.8 15.5 %collective-permute-start.5 = (bf16[256,512]{1,0:T(8,128)(2,1)S(1)}, bf16[256,512]{1,0:T(8,128)(2,1)S(1)}, u32[]{:S(2)}, u32[]{:S(2)}) collective-permute-start(bf16[256,512]{1,0:T(8,128)(2,1)S(1)} %get-tuple-element.16), channel_id=1, source_target_pairs={{0,2},{1,3},{2,0},{3,1},{4,6},{5,7},{6,4},{7,5},{8,10},{9,11},{10,... | collective-permute-start | bytes 786440 | tf_op jit(solution)/shard_map/ppermute | solution.py:19
  29.1 16.1 %collective-permute-start.6 = (bf16[256,512]{1,0:T(8,128)(2,1)S(1)}, bf16[256,512]{1,0:T(8,128)(2,1)S(1)}, u32[]{:S(2)}, u32[]{:S(2)}) collective-permute-start(bf16[256,512]{1,0:T(8,128)(2,1)S(1)} %get-tuple-element.15), channel_id=1, source_target_pairs={{0,3},{1,0},{2,1},{3,2},{4,7},{5,4},{6,5},{7,6},{8,11},{9,8},{10,9... | collective-permute-start | bytes 786440 | tf_op jit(solution)/shard_map/ppermute | solution.py:19
  40.3 17.1 %collective-permute-start.2 = (bf16[704,256]{1,0:T(8,128)(2,1)S(1)}, bf16[704,256]{1,0:T(8,128)(2,1)S(1)}, u32[]{:S(2)}, u32[]{:S(2)}) collective-permute-start(bf16[704,256]{1,0:T(8,128)(2,1)S(1)} %collective-permute-done.1.refs_0_.refs_14_.refs_9_), channel_id=1, source_target_pairs={{0,1},{1,2},{2,3},{3,0},{4,5},{5,6},{6,7},{7,4},{8,9},{9,10},{10,1... | collective-permute-start | bytes 1081352 | tf_op jit(solution)/shard_map/ppermute | solution.py:19
  45.2 12.2 %collective-permute-start.10 = (bf16[704,256]{1,0:T(8,128)(2,1)S(1)}, bf16[704,256]{1,0:T(8,128)(2,1)S(1)}, u32[]{:S(2)}, u32[]{:S(2)}) collective-permute-start(bf16[704,256]{1,0:T(8,128)(2,1)S(1)} %collective-permute-done.1.refs_0_.refs_14_.refs_9_), channel_id=1, source_target_pairs={{0,4},{4,0},{1,5},{5,1},{2,6},{6,2},{3,7},{7,3},{8,12},{12,8},{9,1... | collective-permute-start | bytes 1081352 | tf_op jit(solution)/shard_map/ppermute | solution.py:24
  45.2 7.1 %collective-permute-start.8 = (bf16[640,256]{1,0:T(8,128)(2,1)S(1)}, bf16[640,256]{1,0:T(8,128)(2,1)S(1)}, u32[]{:S(2)}, u32[]{:S(2)}) collective-permute-start(bf16[640,256]{1,0:T(8,128)(2,1)S(1)} %shard_map.82), channel_id=1, source_target_pairs={{0,16},{4,12},{8,24},{12,4},{16,0},{20,28},{24,8},{28,20},{1,17},{... | collective-permute-start | bytes 983048 | tf_op jit(solution)/shard_map/ppermute | solution.py:30
  46.8 11.1 %collective-permute-start.18 = (bf16[704,256]{1,0:T(8,128)(2,1)S(1)}, bf16[704,256]{1,0:T(8,128)(2,1)S(1)}, u32[]{:S(2)}, u32[]{:S(2)}) collective-permute-start(bf16[704,256]{1,0:T(8,128)(2,1)S(1)} %collective-permute-done.14.refs_0_.refs_22_.refs_17_), channel_id=1, source_target_pairs={{0,4},{4,0},{1,5},{5,1},{2,6},{6,2},{3,7},{7,3},{8,12},{12,8},{9,1... | collective-permute-start | bytes 1081352 | tf_op jit(solution)/shard_map/ppermute | solution.py:24
  47.0 8.9 %collective-permute-start.16 = (bf16[640,256]{1,0:T(8,128)(2,1)S(1)}, bf16[640,256]{1,0:T(8,128)(2,1)S(1)}, u32[]{:S(2)}, u32[]{:S(2)}) collective-permute-start(bf16[640,256]{1,0:T(8,128)(2,1)S(1)} %shard_map.83), channel_id=1, source_target_pairs={{0,16},{4,12},{8,24},{12,4},{16,0},{20,28},{24,8},{28,20},{1,17},{... | collective-permute-start | bytes 983048 | tf_op jit(solution)/shard_map/ppermute | solution.py:30
  52.4 7.1 %collective-permute-start.9 = (bf16[640,256]{1,0:T(8,128)(2,1)S(1)}, bf16[640,256]{1,0:T(8,128)(2,1)S(1)}, u32[]{:S(2)}, u32[]{:S(2)}) collective-permute-start(bf16[640,256]{1,0:T(8,128)(2,1)S(1)} %collective-permute-done.7.refs_15_.refs_10_), channel_id=1, source_target_pairs={{0,16},{4,12},{8,24},{12,4},{16,0},{20,28},{24,8},{28,20},{1,17},{... | collective-permute-start | bytes 983048 | tf_op jit(solution)/shard_map/ppermute | solution.py:30
  55.9 9.3 %collective-permute-start.17 = (bf16[640,256]{1,0:T(8,128)(2,1)S(1)}, bf16[640,256]{1,0:T(8,128)(2,1)S(1)}, u32[]{:S(2)}, u32[]{:S(2)}) collective-permute-start(bf16[640,256]{1,0:T(8,128)(2,1)S(1)} %collective-permute-done.15.refs_23_.refs_18_), channel_id=1, source_target_pairs={{0,16},{4,12},{8,24},{12,4},{16,0},{20,28},{24,8},{28,20},{1,17},{... | collective-permute-start | bytes 983048 | tf_op jit(solution)/shard_map/ppermute | solution.py:30
  57.4 7.8 %collective-permute-start.11 = (bf16[640,256]{1,0:T(8,128)(2,1)S(1)}, bf16[640,256]{1,0:T(8,128)(2,1)S(1)}, u32[]{:S(2)}, u32[]{:S(2)}) collective-permute-start(bf16[640,256]{1,0:T(8,128)(2,1)S(1)} %collective-permute-done.7.refs_15_.refs_10_), channel_id=1, source_target_pairs={{0,4},{4,0},{1,5},{5,1},{2,6},{6,2},{3,7},{7,3},{8,12},{12,8},{9,1... | collective-permute-start | bytes 983048 | tf_op jit(solution)/shard_map/ppermute | solution.py:24
  57.4 8.3 %collective-permute-start.12 = (bf16[640,256]{1,0:T(8,128)(2,1)S(1)}, bf16[640,256]{1,0:T(8,128)(2,1)S(1)}, u32[]{:S(2)}, u32[]{:S(2)}) collective-permute-start(bf16[640,256]{1,0:T(8,128)(2,1)S(1)} %collective-permute-done.8.refs_16_.refs_11_), channel_id=1, source_target_pairs={{0,4},{4,0},{1,5},{5,1},{2,6},{6,2},{3,7},{7,3},{8,12},{12,8},{9,1... | collective-permute-start | bytes 983048 | tf_op jit(solution)/shard_map/ppermute | solution.py:24
  58.0 10.1 %collective-permute-start.22 = (bf16[640,256]{1,0:T(8,128)(2,1)S(1)}, bf16[640,256]{1,0:T(8,128)(2,1)S(1)}, u32[]{:S(2)}, u32[]{:S(2)}) collective-permute-start(bf16[640,256]{1,0:T(8,128)(2,1)S(1)} %shard_map.84), channel_id=1, source_target_pairs={{0,8},{4,20},{8,0},{12,28},{16,24},{20,4},{24,16},{28,12},{1,9},{5... | collective-permute-start | bytes 983048 | tf_op jit(solution)/shard_map/ppermute | solution.py:30
  59.5 13.6 %collective-permute-start.3 = (bf16[704,256]{1,0:T(8,128)(2,1)S(1)}, bf16[704,256]{1,0:T(8,128)(2,1)S(1)}, u32[]{:S(2)}, u32[]{:S(2)}) collective-permute-start(bf16[704,256]{1,0:T(8,128)(2,1)S(1)} %collective-permute-done.2.refs_6_.refs_0_.refs_1_.refs_25_), channel_id=1, source_target_pairs={{0,4},{4,0},{1,5},{5,1},{2,6},{6,2},{3,7},{7,3},{8,12},{12,8},{9,1... | collective-permute-start | bytes 1081352 | tf_op jit(solution)/shard_map/ppermute | solution.py:24
  65.2 2.9 %collective-permute-start.19 = (bf16[640,256]{1,0:T(8,128)(2,1)S(1)}, bf16[640,256]{1,0:T(8,128)(2,1)S(1)}, u32[]{:S(2)}, u32[]{:S(2)}) collective-permute-start(bf16[640,256]{1,0:T(8,128)(2,1)S(1)} %collective-permute-done.15.refs_23_.refs_18_), channel_id=1, source_target_pairs={{0,4},{4,0},{1,5},{5,1},{2,6},{6,2},{3,7},{7,3},{8,12},{12,8},{9,1... | collective-permute-start | bytes 983048 | tf_op jit(solution)/shard_map/ppermute | solution.py:24
  65.2 2.9 %collective-permute-start.20 = (bf16[640,256]{1,0:T(8,128)(2,1)S(1)}, bf16[640,256]{1,0:T(8,128)(2,1)S(1)}, u32[]{:S(2)}, u32[]{:S(2)}) collective-permute-start(bf16[640,256]{1,0:T(8,128)(2,1)S(1)} %collective-permute-done.16.refs_24_.refs_19_), channel_id=1, source_target_pairs={{0,4},{4,0},{1,5},{5,1},{2,6},{6,2},{3,7},{7,3},{8,12},{12,8},{9,1... | collective-permute-start | bytes 983048 | tf_op jit(solution)/shard_map/ppermute | solution.py:24
  65.7 7.4 %collective-permute-start.23 = (bf16[640,256]{1,0:T(8,128)(2,1)S(1)}, bf16[640,256]{1,0:T(8,128)(2,1)S(1)}, u32[]{:S(2)}, u32[]{:S(2)}) collective-permute-start(bf16[640,256]{1,0:T(8,128)(2,1)S(1)} %shard_map.84), channel_id=1, source_target_pairs={{0,16},{4,12},{8,24},{12,4},{16,0},{20,28},{24,8},{28,20},{1,17},{... | collective-permute-start | bytes 983048 | tf_op jit(solution)/shard_map/ppermute | solution.py:30
  68.1 8.6 %collective-permute-start.26 = (bf16[640,256]{1,0:T(8,128)(2,1)S(1)}, bf16[640,256]{1,0:T(8,128)(2,1)S(1)}, u32[]{:S(2)}, u32[]{:S(2)}) collective-permute-start(bf16[640,256]{1,0:T(8,128)(2,1)S(1)} %collective-permute-done.22.refs_2_.refs_26_), channel_id=1, source_target_pairs={{0,16},{4,12},{8,24},{12,4},{16,0},{20,28},{24,8},{28,20},{1,17},{... | collective-permute-start | bytes 983048 | tf_op jit(solution)/shard_map/ppermute | solution.py:30
  68.1 8.9 %collective-permute-start.13 = (bf16[640,256]{1,0:T(8,128)(2,1)S(1)}, bf16[640,256]{1,0:T(8,128)(2,1)S(1)}, u32[]{:S(2)}, u32[]{:S(2)}) collective-permute-start(bf16[640,256]{1,0:T(8,128)(2,1)S(1)} %collective-permute-done.9.refs_17_.refs_12_), channel_id=1, source_target_pairs={{0,4},{4,0},{1,5},{5,1},{2,6},{6,2},{3,7},{7,3},{8,12},{12,8},{9,1... | collective-permute-start | bytes 983048 | tf_op jit(solution)/shard_map/ppermute | solution.py:24
  68.2 8.9 %collective-permute-start.21 = (bf16[640,256]{1,0:T(8,128)(2,1)S(1)}, bf16[640,256]{1,0:T(8,128)(2,1)S(1)}, u32[]{:S(2)}, u32[]{:S(2)}) collective-permute-start(bf16[640,256]{1,0:T(8,128)(2,1)S(1)} %collective-permute-done.17.refs_25_.refs_20_), channel_id=1, source_target_pairs={{0,4},{4,0},{1,5},{5,1},{2,6},{6,2},{3,7},{7,3},{8,12},{12,8},{9,1... | collective-permute-start | bytes 983048 | tf_op jit(solution)/shard_map/ppermute | solution.py:24
  73.1 6.8 %collective-permute-start.24 = (bf16[640,256]{1,0:T(8,128)(2,1)S(1)}, bf16[640,256]{1,0:T(8,128)(2,1)S(1)}, u32[]{:S(2)}, u32[]{:S(2)}) collective-permute-start(bf16[640,256]{1,0:T(8,128)(2,1)S(1)} %collective-permute-done.22.refs_2_.refs_26_), channel_id=1, source_target_pairs={{0,4},{4,0},{1,5},{5,1},{2,6},{6,2},{3,7},{7,3},{8,12},{12,8},{9,1... | collective-permute-start | bytes 983048 | tf_op jit(solution)/shard_map/ppermute | solution.py:24
  73.1 6.8 %collective-permute-start.25 = (bf16[640,256]{1,0:T(8,128)(2,1)S(1)}, bf16[640,256]{1,0:T(8,128)(2,1)S(1)}, u32[]{:S(2)}, u32[]{:S(2)}) collective-permute-start(bf16[640,256]{1,0:T(8,128)(2,1)S(1)} %collective-permute-done.23.refs_3_.refs_27_), channel_id=1, source_target_pairs={{0,4},{4,0},{1,5},{5,1},{2,6},{6,2},{3,7},{7,3},{8,12},{12,8},{9,1... | collective-permute-start | bytes 983048 | tf_op jit(solution)/shard_map/ppermute | solution.py:24
  76.6 3.9 %collective-permute-start.27 = (bf16[640,256]{1,0:T(8,128)(2,1)S(1)}, bf16[640,256]{1,0:T(8,128)(2,1)S(1)}, u32[]{:S(2)}, u32[]{:S(2)}) collective-permute-start(bf16[640,256]{1,0:T(8,128)(2,1)S(1)} %collective-permute-done.26.refs_28_), channel_id=1, source_target_pairs={{0,4},{4,0},{1,5},{5,1},{2,6},{6,2},{3,7},{7,3},{8,12},{12,8},{9,1... | collective-permute-start | bytes 983048 | tf_op jit(solution)/shard_map/ppermute | solution.py:24
  79.9 1.2 %copy-start.1 = (bf16[256,2048]{1,0:T(8,128)(2,1)S(1)}, bf16[256,2048]{1,0:T(8,128)(2,1)}, u32[]{:S(2)}) copy-start(bf16[256,2048]{1,0:T(8,128)(2,1)} %refs_6_.1) | copy-start | bytes 3145732
  79.9 1.2 %copy-start.7 = (s32[8]{0:T(128)S(1)}, s32[8]{0:T(128)}, u32[]{:S(2)}) copy-start(s32[8]{0:T(128)} %refs_5_.1) | copy-start | bytes 100
